TPU v7x, 32 devices: a whole 2x2x4 slice. The times are simulated.
32 devices in a mesh: seq: 8 (over z, y), head: 4 (over x, core).
Axes of the slice: x: 2, y: 2, z: 4, core: 2. Of those that a mesh axis runs over, the one named last changes fastest.
Arguments:
- source: bfloat16 [2, 8192, 768], P(None, ('seq', 'head')), may hold values from -6 to 6
- target: bfloat16 [2, 4096, 768], P(None, ('seq', 'head')), may hold values from -6 to 6
- cotangent: bfloat16 [2, 4096, 768], P(None, ('seq', 'head')), may hold values from -6 to 6
- src_lengths: int32 [2, 16], replicated, may hold values from 1 to 2048, 8192 in all within a row
- tgt_lengths: int32 [2, 8], replicated, may hold values from 1 to 1024, 4096 in all within a row
- retrieved: int32 [2, 1024], replicated, may hold values from 0 to 8191
- encoder_qkv: bfloat16 [768, 2304], P(('seq', 'head')), may hold values from -0.21875 to 0.21875
- encoder_out: bfloat16 [768, 768], P(('seq', 'head')), may hold values from -2.5 to 2.5
- encoder_up: bfloat16 [768, 3072], P(('seq', 'head')), may hold values from -0.21875 to 0.21875
- encoder_down: bfloat16 [3072, 768], P(('seq', 'head')), may hold values from -0.109375 to 0.109375
- encoder_gains: bfloat16 [2, 768], P(None, ('seq', 'head')), may hold values from 0.5 to 1.5
- encoder_biases: bfloat16 [10, 768], P(None, ('seq', 'head')), may hold values from -1.796875 to 1.796875
- decoder_qkv: bfloat16 [768, 2304], P(('seq', 'head')), may hold values from -0.21875 to 0.21875
- decoder_out: bfloat16 [768, 768], P(('seq', 'head')), may hold values from -2.5 to 2.5
- cross_query: bfloat16 [768, 768], P(('seq', 'head')), may hold values from -0.21875 to 0.21875
- cross_keyvalue: bfloat16 [768, 1536], P(('seq', 'head')), may hold values from -0.21875 to 0.21875
- cross_out: bfloat16 [768, 768], P(('seq', 'head')), may hold values from -3.5 to 3.5
- decoder_up: bfloat16 [768, 3072], P(('seq', 'head')), may hold values from -0.21875 to 0.21875
- decoder_down: bfloat16 [3072, 768], P(('seq', 'head')), may hold values from -0.109375 to 0.109375
- decoder_gains: bfloat16 [3, 768], P(None, ('seq', 'head')), may hold values from 0.5 to 1.5
- decoder_biases: bfloat16 [14, 768], P(None, ('seq', 'head')), may hold values from -1.796875 to 1.796875
Outputs:
- decoded: float32 [2, 4096, 768], P(None, ('seq', 'head'))
- grad_source: float32 [2, 8192, 768], P(None, ('seq', 'head'))
- grad_target: float32 [2, 4096, 768], P(None, ('seq', 'head'))
- grad_encoder_qkv: float32 [768, 2304], P(('seq', 'head'))
- grad_encoder_out: float32 [768, 768], P(('seq', 'head'))
- grad_encoder_up: float32 [768, 3072], P(('seq', 'head'))
- grad_encoder_down: float32 [3072, 768], P(('seq', 'head'))
- grad_encoder_gains: float32 [2, 768], P(None, ('seq', 'head'))
- grad_encoder_biases: float32 [10, 768], P(None, ('seq', 'head'))
- grad_decoder_qkv: float32 [768, 2304], P(('seq', 'head'))
- grad_decoder_out: float32 [768, 768], P(('seq', 'head'))
- grad_cross_query: float32 [768, 768], P(('seq', 'head'))
- grad_cross_keyvalue: float32 [768, 1536], P(('seq', 'head'))
- grad_cross_out: float32 [768, 768], P(('seq', 'head'))
- grad_decoder_up: float32 [768, 3072], P(('seq', 'head'))
- grad_decoder_down: float32 [3072, 768], P(('seq', 'head'))
- grad_decoder_gains: float32 [3, 768], P(None, ('seq', 'head'))
- grad_decoder_biases: float32 [14, 768], P(None, ('seq', 'head'))
Inputs may be any that keep to these rules, and one draw needn't show every extreme that they name: `src_lengths`: each row lists the lengths of one micro-batch's source documents in order; a row sums to 8192 and its largest entry is exactly 2048. `tgt_lengths`: each row lists the lengths of one micro-batch's target documents in order; a row sums to 4096 and its largest entry is exactly 1024. `retrieved`: positions in the source stream of the same micro-batch; a position may repeat.
All inputs are finite; a program needn't handle non-finite values.
Results may differ from a plain program's by a relative error of at most 0.025.
Values may be sent and summed in bfloat16 or wider, within the bound.
A program may use at most 320 MiB of HBM per device.

v0:
```python
import jax
import jax.numpy as jnp
from jax import lax
from jax.sharding import PartitionSpec as P

D = 768
HEADS = 12
HEAD_DIM = 64
FF = 3072
MICRO = 2
STRETCH = 1024
REACH = 2


EPSILON = 1e-05
NEGATIVE = -1e30


def passed_along(value, axis, by):
    devices = lax.axis_size(axis)
    pairs = [(i, i + by) for i in range(devices) if 0 <= i + by < devices]
    return lax.ppermute(value, axis, pairs)


def layer_norm(resid, gain, shift):
    center = resid - jnp.mean(resid, axis=-1, keepdims=True)
    spread = jnp.mean(center * center, axis=-1, keepdims=True)
    return center * lax.rsqrt(spread + EPSILON) * gain + shift


def gelu_exact(value):
    return jax.nn.gelu(value, approximate=False)


def doc_ids(lengths, positions):
    starts = jnp.cumsum(lengths) - lengths
    inside = (starts[None, :] <= positions[:, None]).astype(jnp.int32)
    return jnp.sum(inside, axis=1) - 1


def doc_start(lengths, document):
    starts = jnp.cumsum(lengths) - lengths
    return jnp.sum(jnp.where(jnp.arange(starts.shape[0], dtype=jnp.int32) == document, starts, 0))


def joined_bias(biases):
    query_part = biases[0].reshape(HEADS, HEAD_DIM)
    value_part = biases[1].reshape(HEADS, HEAD_DIM)
    return jnp.stack([query_part, jnp.zeros_like(query_part), value_part], axis=1).reshape(3 * D)


def row_sum(grad):
    return jnp.sum(grad.astype(jnp.float32), axis=0)


def contract_rows(left, right):
    return jnp.einsum("ti,tj->ij", left, right, preferred_element_type=jnp.float32)


def times_transpose(left, right):
    return jnp.einsum("ti,ji->tj", left, right, preferred_element_type=jnp.float32)


def split_parts(value):
    upper = value.astype(jnp.bfloat16)
    lower = (value - upper.astype(jnp.float32)).astype(jnp.bfloat16)
    return (upper, lower)


def keep_state(state):
    return state


def to_heads(value):
    return lax.all_to_all(value, "head", split_axis=1, concat_axis=0, tiled=True)


def to_tokens(value):
    return lax.all_to_all(value, "head", split_axis=0, concat_axis=1, tiled=True)


def masked_scores(query, keys, allowed):
    scores = jnp.einsum("qhd,khd->hqk", query, keys, preferred_element_type=jnp.float32) * 0.125
    return jnp.where(allowed[None], scores, NEGATIVE)


def softmax_block(query, keys, values, allowed):
    scores = masked_scores(query, keys, allowed)
    peak = jnp.max(scores, axis=-1, keepdims=True)
    weights = jnp.exp(scores - peak)
    total = jnp.sum(weights, axis=-1, keepdims=True)
    probs = (weights / total).astype(jnp.bfloat16)
    output = jnp.einsum("hqk,khd->qhd", probs, values, preferred_element_type=jnp.float32)
    return (output, (peak + jnp.log(total))[:, :, 0])


def block_backward(query, keys, values, allowed, log_total, grad_out, delta):
    scores = masked_scores(query, keys, allowed)
    probs = jnp.where(allowed[None], jnp.exp(scores - log_total[:, :, None]), 0.0)
    grad_probs = jnp.einsum("qhd,khd->hqk", grad_out, values, preferred_element_type=jnp.float32)
    if delta is None:
        delta = jnp.sum(probs * grad_probs, axis=-1)
    grad_scores = (probs * (grad_probs - delta[:, :, None])).astype(jnp.bfloat16)
    grad_query = None
    grad_query = (
        jnp.einsum("hqk,khd->qhd", grad_scores, keys, preferred_element_type=jnp.float32) * 0.125
    )
    grad_keys = (
        jnp.einsum("hqk,qhd->khd", grad_scores, query, preferred_element_type=jnp.float32) * 0.125
    )
    grad_values = jnp.einsum(
        "hqk,qhd->khd", probs.astype(jnp.bfloat16), grad_out, preferred_element_type=jnp.float32
    )
    return (grad_query, jnp.stack([grad_keys, grad_values], axis=2))


def key_mask(context, first_key, width):
    query_pos, query_docs, first_doc, lengths = context
    key_pos = first_key + jnp.arange(width, dtype=jnp.int32)
    same = doc_ids(lengths, key_pos)[None, :] == query_docs[:, None]
    return (key_pos[None, :] <= query_pos[:, None]) & same


def key_live(context, first_key, width):
    query_pos, query_docs, first_doc, lengths = context
    return (first_key <= query_pos[-1]) & (first_key + width - 1 >= first_doc)


def self_forward(query, key_blocks, block_firsts, context):
    width = key_blocks.shape[1]
    count = key_blocks.shape[0]
    heads_here = query.shape[1]

    def stat_step(index, state):
        first_key = block_firsts[index]
        block = key_blocks[index]

        def stat_compute(state):
            peak, total = state
            allowed = key_mask(context, first_key, width)
            scores = masked_scores(query, block[:, :, 0], allowed)
            new_peak = jnp.maximum(peak, jnp.max(scores, axis=-1))
            weights = jnp.where(allowed[None], jnp.exp(scores - new_peak[:, :, None]), 0.0)
            return (new_peak, total * jnp.exp(peak - new_peak) + jnp.sum(weights, axis=-1))

        return lax.cond(key_live(context, first_key, width), stat_compute, keep_state, state)

    start_state = (
        jnp.full((heads_here, query.shape[0]), NEGATIVE, jnp.float32),
        jnp.zeros((heads_here, query.shape[0]), jnp.float32),
    )
    peak, total = lax.fori_loop(0, count, stat_step, start_state)
    log_total = peak + jnp.log(total)

    def out_step(index, running):
        first_key = block_firsts[index]
        block = key_blocks[index]

        def out_compute(running):
            allowed = key_mask(context, first_key, width)
            scores = masked_scores(query, block[:, :, 0], allowed)
            probs = jnp.where(allowed[None], jnp.exp(scores - log_total[:, :, None]), 0.0).astype(
                jnp.bfloat16
            )
            return running + jnp.einsum(
                "hqk,khd->qhd", probs, block[:, :, 1], preferred_element_type=jnp.float32
            )

        return lax.cond(key_live(context, first_key, width), out_compute, keep_state, running)

    output = lax.fori_loop(0, count, out_step, jnp.zeros(query.shape, jnp.float32))
    return (output, log_total)


def self_delta(query, key_blocks, block_firsts, context, log_total, grad_out):
    width = key_blocks.shape[1]

    def delta_step(index, delta):
        first_key = block_firsts[index]
        block = key_blocks[index]

        def delta_compute(delta):
            allowed = key_mask(context, first_key, width)
            scores = masked_scores(query, block[:, :, 0], allowed)
            probs = jnp.where(allowed[None], jnp.exp(scores - log_total[:, :, None]), 0.0)
            grad_probs = jnp.einsum(
                "qhd,khd->hqk", grad_out, block[:, :, 1], preferred_element_type=jnp.float32
            )
            return delta + jnp.sum(probs * grad_probs, axis=-1)

        return lax.cond(key_live(context, first_key, width), delta_compute, keep_state, delta)

    return lax.fori_loop(
        0, key_blocks.shape[0], delta_step, jnp.zeros(log_total.shape, jnp.float32)
    )


def block_grads(query, block, first_key, context, log_total, grad_out, delta):
    width = block.shape[0]

    def block_compute(unused):
        allowed = key_mask(context, first_key, width)
        return block_backward(
            query, block[:, :, 0], block[:, :, 1], allowed, log_total, grad_out, delta
        )

    def skip(unused):
        empty_query = jnp.zeros(query.shape, jnp.float32)
        empty_pairs = jnp.zeros(block.shape, jnp.float32)
        return (empty_query, empty_pairs)

    return lax.cond(key_live(context, first_key, width), block_compute, skip, 0)


def self_back_all(query, key_blocks, block_firsts, context, log_total, grad_out, delta):

    def grad_step(index, carry):
        grad_query, terms = carry
        found_query, found_pairs = block_grads(
            query, key_blocks[index], block_firsts[index], context, log_total, grad_out, delta
        )
        return (grad_query + found_query, terms.at[index].set(found_pairs))

    start_carry = (jnp.zeros(query.shape, jnp.float32), jnp.zeros(key_blocks.shape, jnp.float32))
    return lax.fori_loop(0, key_blocks.shape[0], grad_step, start_carry)


def encoder_forward(rows_in, weights, lengths):
    qkv_full, out_full, up_full, down_full, gains, biases = weights
    gains = gains.astype(jnp.float32)
    biases = biases.astype(jnp.float32)
    local = rows_in.shape[0]
    parts = lax.axis_size("head")
    heads_here = HEADS // parts
    group = local * parts
    count = group // STRETCH
    joined = (
        jnp.dot(rows_in, qkv_full, preferred_element_type=jnp.float32) + joined_bias(biases)
    ).astype(jnp.bfloat16)
    grouped = to_heads(joined.reshape(local, parts, 3 * D // parts))
    grouped = grouped.reshape(count, STRETCH, heads_here, 3, HEAD_DIM)
    positions = lax.axis_index("seq") * group + jnp.arange(group, dtype=jnp.int32)
    documents = doc_ids(lengths, positions).reshape(count, STRETCH)

    def one_stretch(items):
        block, docs_here = items
        allowed = docs_here[:, None] == docs_here[None, :]
        return softmax_block(block[:, :, 0], block[:, :, 1], block[:, :, 2], allowed)

    attended, log_total = lax.map(one_stretch, (grouped, documents))
    attended_low = attended.astype(jnp.bfloat16).reshape(group, 1, heads_here * HEAD_DIM)
    mixed = to_tokens(attended_low).reshape(local, D)
    branch = jnp.dot(mixed, out_full, preferred_element_type=jnp.float32) + biases[2]
    first, first_back = jax.vjp(
        layer_norm, rows_in.astype(jnp.float32) + branch, gains[0], biases[3]
    )
    first_low = first.astype(jnp.bfloat16)
    hidden = jnp.dot(first_low, up_full, preferred_element_type=jnp.float32) + biases[4:8].reshape(
        FF
    )
    active, active_back = jax.vjp(gelu_exact, hidden)
    active_low = active.astype(jnp.bfloat16)
    second = jnp.dot(active_low, down_full, preferred_element_type=jnp.float32) + biases[8]
    result, result_back = jax.vjp(layer_norm, first + second, gains[1], biases[9])

    def backward(grad_result):
        grad_sum, grad_gain_two, grad_shift_two = result_back(grad_result)
        grad_second = grad_sum.astype(jnp.bfloat16)
        grad_down = contract_rows(active_low, grad_second)
        grad_hidden = active_back(times_transpose(grad_second, down_full))[0].astype(jnp.bfloat16)
        grad_up = contract_rows(first_low, grad_hidden)
        grad_first = grad_sum + times_transpose(grad_hidden, up_full)
        grad_resid, grad_gain_one, grad_shift_one = first_back(grad_first)
        grad_branch = grad_resid.astype(jnp.bfloat16)
        grad_out = contract_rows(mixed, grad_branch)
        grad_mixed = times_transpose(grad_branch, out_full).astype(jnp.bfloat16)
        grad_attended = to_heads(grad_mixed.reshape(local, parts, heads_here * HEAD_DIM))
        grad_attended = grad_attended.reshape(count, STRETCH, heads_here, HEAD_DIM)

        def stretch_back(items):
            block, docs_here, lse_here, grad_here = items
            allowed = docs_here[:, None] == docs_here[None, :]
            grad_query, grad_pairs = block_backward(
                block[:, :, 0], block[:, :, 1], block[:, :, 2], allowed, lse_here, grad_here, None
            )
            return jnp.concatenate([grad_query[:, :, None], grad_pairs], axis=2).astype(
                jnp.bfloat16
            )

        grad_grouped = lax.map(stretch_back, (grouped, documents, log_total, grad_attended))
        grad_joined = to_tokens(grad_grouped.reshape(group, 1, 3 * D // parts)).reshape(
            local, 3 * D
        )
        grad_qkv = contract_rows(rows_in, grad_joined)
        grad_rows = grad_resid + times_transpose(grad_joined, qkv_full)
        joined_sums = row_sum(grad_joined).reshape(HEADS, 3, HEAD_DIM)
        grad_gains = jnp.stack([grad_gain_one, grad_gain_two])
        grad_biases = jnp.concatenate(
            [
                joined_sums[:, 0].reshape(1, D),
                joined_sums[:, 2].reshape(1, D),
                row_sum(grad_branch)[None],
                grad_shift_one[None],
                row_sum(grad_hidden).reshape(4, D),
                row_sum(grad_second)[None],
                grad_shift_two[None],
            ],
            axis=0,
        )
        return (grad_rows, (grad_qkv, grad_out, grad_up, grad_down, grad_gains, grad_biases))

    return (result, backward)


def decoder_forward(rows_in, fetched, weights, lengths):
    qkv_full, out_full, query_full, keyvalue_full, cross_full, up_full, down_full, gains, biases = (
        weights
    )
    gains = gains.astype(jnp.float32)
    biases = biases.astype(jnp.float32)
    local = rows_in.shape[0]
    parts = lax.axis_size("head")
    heads_here = HEADS // parts
    group = local * parts
    joined = (
        jnp.dot(rows_in, qkv_full, preferred_element_type=jnp.float32) + joined_bias(biases)
    ).astype(jnp.bfloat16)
    grouped = to_heads(joined.reshape(local, parts, 3 * D // parts)).reshape(
        group, heads_here, 3, HEAD_DIM
    )
    query = grouped[:, :, 0]
    own_pairs = grouped[:, :, 1:]
    query_first = lax.axis_index("seq") * group
    query_pos = query_first + jnp.arange(group, dtype=jnp.int32)
    query_docs = doc_ids(lengths, query_pos)
    context = (query_pos, query_docs, doc_start(lengths, query_docs[0]), lengths)
    nearby = [own_pairs]
    for step in range(REACH):
        nearby.append(passed_along(nearby[-1], "seq", 1))
    key_blocks = jnp.stack(nearby)
    block_firsts = query_first - jnp.arange(REACH + 1, dtype=jnp.int32) * group
    attended, log_total = self_forward(query, key_blocks, block_firsts, context)
    attended_low = attended.astype(jnp.bfloat16).reshape(group, 1, heads_here * HEAD_DIM)
    mixed = to_tokens(attended_low).reshape(local, D)
    branch = jnp.dot(mixed, out_full, preferred_element_type=jnp.float32) + biases[2]
    first, first_back = jax.vjp(
        layer_norm, rows_in.astype(jnp.float32) + branch, gains[0], biases[3]
    )
    first_low = first.astype(jnp.bfloat16)
    query_cross = jnp.dot(first_low, query_full, preferred_element_type=jnp.float32) + biases[4]
    query_cross = query_cross.astype(jnp.bfloat16).reshape(local, HEADS, HEAD_DIM)
    keyvalue = jnp.dot(fetched, keyvalue_full, preferred_element_type=jnp.float32)
    keyvalue = keyvalue + jnp.concatenate([jnp.zeros((D,), jnp.float32), biases[5]])
    retrieved_rows = fetched.shape[0]
    keys_cross = keyvalue[:, :D].astype(jnp.bfloat16).reshape(retrieved_rows, HEADS, HEAD_DIM)
    values_cross = keyvalue[:, D:].astype(jnp.bfloat16).reshape(retrieved_rows, HEADS, HEAD_DIM)
    every = jnp.ones((local, retrieved_rows), jnp.bool_)
    crossed, cross_total = softmax_block(query_cross, keys_cross, values_cross, every)
    crossed_low = crossed.reshape(local, D).astype(jnp.bfloat16)
    branch_cross = jnp.dot(crossed_low, cross_full, preferred_element_type=jnp.float32) + biases[6]
    second, second_back = jax.vjp(layer_norm, first + branch_cross, gains[1], biases[7])
    second_low = second.astype(jnp.bfloat16)
    hidden = jnp.dot(second_low, up_full, preferred_element_type=jnp.float32) + biases[
        8:12
    ].reshape(FF)
    active, active_back = jax.vjp(gelu_exact, hidden)
    active_low = active.astype(jnp.bfloat16)
    third = jnp.dot(active_low, down_full, preferred_element_type=jnp.float32) + biases[12]
    result, result_back = jax.vjp(layer_norm, second + third, gains[2], biases[13])

    def backward(grad_result):
        grad_sum_three, grad_gain_three, grad_shift_three = result_back(grad_result)
        grad_third = grad_sum_three.astype(jnp.bfloat16)
        grad_down = contract_rows(active_low, grad_third)
        grad_hidden = active_back(times_transpose(grad_third, down_full))[0].astype(jnp.bfloat16)
        grad_up = contract_rows(second_low, grad_hidden)
        grad_second = grad_sum_three + times_transpose(grad_hidden, up_full)
        grad_sum_two, grad_gain_two, grad_shift_two = second_back(grad_second)
        grad_branch_cross = grad_sum_two.astype(jnp.bfloat16)
        grad_cross = contract_rows(crossed_low, grad_branch_cross)
        grad_crossed = times_transpose(grad_branch_cross, cross_full).astype(jnp.bfloat16)
        grad_crossed = grad_crossed.reshape(local, HEADS, HEAD_DIM)
        grad_query_cross, grad_pairs_cross = block_backward(
            query_cross, keys_cross, values_cross, every, cross_total, grad_crossed, None
        )
        grad_query_cross = grad_query_cross.reshape(local, D).astype(jnp.bfloat16)
        grad_keyvalue = jnp.concatenate(
            [
                grad_pairs_cross[:, :, 0].reshape(retrieved_rows, D),
                grad_pairs_cross[:, :, 1].reshape(retrieved_rows, D),
            ],
            axis=1,
        )
        kv_upper, kv_lower = split_parts(grad_keyvalue)
        grad_keyvalue_weight = contract_rows(fetched, kv_upper) + contract_rows(fetched, kv_lower)
        grad_fetched_part = times_transpose(kv_upper, keyvalue_full) + times_transpose(
            kv_lower, keyvalue_full
        )
        grad_query_weight = contract_rows(first_low, grad_query_cross)
        grad_first = grad_sum_two + times_transpose(grad_query_cross, query_full)
        grad_resid, grad_gain_one, grad_shift_one = first_back(grad_first)
        grad_branch = grad_resid.astype(jnp.bfloat16)
        grad_out = contract_rows(mixed, grad_branch)
        grad_mixed = times_transpose(grad_branch, out_full).astype(jnp.bfloat16)
        grad_attended = to_heads(grad_mixed.reshape(local, parts, heads_here * HEAD_DIM))
        grad_attended = grad_attended.reshape(group, heads_here, HEAD_DIM)
        delta = self_delta(query, key_blocks, block_firsts, context, log_total, grad_attended)
        grad_query, terms = self_back_all(
            query, key_blocks, block_firsts, context, log_total, grad_attended, delta
        )
        carried = terms[REACH]
        for step in range(REACH - 1, -1, -1):
            carried = (
                passed_along(carried.astype(jnp.bfloat16), "seq", -1).astype(carried.dtype)
                + terms[step]
            )
        grad_grouped = jnp.concatenate([grad_query[:, :, None], carried], axis=2).astype(
            jnp.bfloat16
        )
        grad_joined = to_tokens(grad_grouped.reshape(group, 1, 3 * D // parts)).reshape(
            local, 3 * D
        )
        grad_qkv = contract_rows(rows_in, grad_joined)
        grad_rows = grad_resid + times_transpose(grad_joined, qkv_full)
        joined_sums = row_sum(grad_joined).reshape(HEADS, 3, HEAD_DIM)
        grad_gains = jnp.stack([grad_gain_one, grad_gain_two, grad_gain_three])
        grad_biases = jnp.concatenate(
            [
                joined_sums[:, 0].reshape(1, D),
                joined_sums[:, 2].reshape(1, D),
                row_sum(grad_branch)[None],
                grad_shift_one[None],
                row_sum(grad_query_cross)[None],
                jnp.sum(grad_pairs_cross[:, :, 1], axis=0).reshape(1, D),
                row_sum(grad_branch_cross)[None],
                grad_shift_two[None],
                row_sum(grad_hidden).reshape(4, D),
                row_sum(grad_third)[None],
                grad_shift_three[None],
            ],
            axis=0,
        )
        weight_grads = (
            grad_qkv,
            grad_out,
            grad_query_weight,
            grad_keyvalue_weight,
            grad_cross,
            grad_up,
            grad_down,
            grad_gains,
            grad_biases,
        )
        return (grad_rows, grad_fetched_part, weight_grads)

    return (result, backward)


def shards(
    source,
    target,
    cotangent,
    src_lengths,
    tgt_lengths,
    retrieved,
    encoder_qkv,
    encoder_out,
    encoder_up,
    encoder_down,
    encoder_gains,
    encoder_biases,
    decoder_qkv,
    decoder_out,
    cross_query,
    cross_keyvalue,
    cross_out,
    decoder_up,
    decoder_down,
    decoder_gains,
    decoder_biases,
):
    src_local = source.shape[1]
    my_index = lax.axis_index(("seq", "head"))
    shard_totals = None
    decoded_rows = []
    source_grads = []
    target_grads = []
    for micro in range(MICRO):
        full = (
            lax.all_gather(encoder_qkv, ("seq", "head"), axis=0, tiled=True),
            lax.all_gather(encoder_out, ("seq", "head"), axis=0, tiled=True),
            lax.all_gather(encoder_up, ("seq", "head"), axis=0, tiled=True),
            lax.all_gather(encoder_down, ("seq", "head"), axis=0, tiled=True),
            lax.all_gather(encoder_gains, ("seq", "head"), axis=1, tiled=True),
            lax.all_gather(encoder_biases, ("seq", "head"), axis=1, tiled=True),
            lax.all_gather(decoder_qkv, ("seq", "head"), axis=0, tiled=True),
            lax.all_gather(decoder_out, ("seq", "head"), axis=0, tiled=True),
            lax.all_gather(cross_query, ("seq", "head"), axis=0, tiled=True),
            lax.all_gather(cross_keyvalue, ("seq", "head"), axis=0, tiled=True),
            lax.all_gather(cross_out, ("seq", "head"), axis=0, tiled=True),
            lax.all_gather(decoder_up, ("seq", "head"), axis=0, tiled=True),
            lax.all_gather(decoder_down, ("seq", "head"), axis=0, tiled=True),
            lax.all_gather(decoder_gains, ("seq", "head"), axis=1, tiled=True),
            lax.all_gather(decoder_biases, ("seq", "head"), axis=1, tiled=True),
        )
        encoded, encoder_backward = encoder_forward(source[micro], full[:6], src_lengths[micro])
        encoded_low = encoded.astype(jnp.bfloat16)
        positions = my_index * src_local + jnp.arange(src_local, dtype=jnp.int32)
        select = (retrieved[micro][:, None] == positions[None, :]).astype(jnp.bfloat16)
        picked = jnp.dot(select, encoded_low, preferred_element_type=jnp.float32)
        fetched = lax.psum(picked, ("seq", "head")).astype(jnp.bfloat16)
        result, decoder_backward = decoder_forward(
            target[micro], fetched, full[6:], tgt_lengths[micro]
        )
        decoded_rows.append(result)
        grad_target_rows, grad_fetched_part, decoder_grads = decoder_backward(
            cotangent[micro].astype(jnp.float32)
        )
        grad_fetched = lax.psum(grad_fetched_part, ("seq", "head"))
        fetch_upper, fetch_lower = split_parts(grad_fetched)
        grad_encoded = contract_rows(select, fetch_upper) + contract_rows(select, fetch_lower)
        grad_source_rows, encoder_grads = encoder_backward(grad_encoded)
        source_grads.append(grad_source_rows)
        target_grads.append(grad_target_rows)
        local_grads = tuple(encoder_grads) + tuple(decoder_grads)
        reduced = (
            lax.psum_scatter(local_grads[0], ("seq", "head"), scatter_dimension=0, tiled=True),
            lax.psum_scatter(local_grads[1], ("seq", "head"), scatter_dimension=0, tiled=True),
            lax.psum_scatter(local_grads[2], ("seq", "head"), scatter_dimension=0, tiled=True),
            lax.psum_scatter(local_grads[3], ("seq", "head"), scatter_dimension=0, tiled=True),
            lax.psum_scatter(local_grads[4], ("seq", "head"), scatter_dimension=1, tiled=True),
            lax.psum_scatter(local_grads[5], ("seq", "head"), scatter_dimension=1, tiled=True),
            lax.psum_scatter(local_grads[6], ("seq", "head"), scatter_dimension=0, tiled=True),
            lax.psum_scatter(local_grads[7], ("seq", "head"), scatter_dimension=0, tiled=True),
            lax.psum_scatter(local_grads[8], ("seq", "head"), scatter_dimension=0, tiled=True),
            lax.psum_scatter(local_grads[9], ("seq", "head"), scatter_dimension=0, tiled=True),
            lax.psum_scatter(local_grads[10], ("seq", "head"), scatter_dimension=0, tiled=True),
            lax.psum_scatter(local_grads[11], ("seq", "head"), scatter_dimension=0, tiled=True),
            lax.psum_scatter(local_grads[12], ("seq", "head"), scatter_dimension=0, tiled=True),
            lax.psum_scatter(local_grads[13], ("seq", "head"), scatter_dimension=1, tiled=True),
            lax.psum_scatter(local_grads[14], ("seq", "head"), scatter_dimension=1, tiled=True),
        )
        if shard_totals is None:
            shard_totals = tuple(reduced)
        else:
            shard_totals = tuple((left + right for left, right in zip(shard_totals, reduced)))
    return (
        jnp.stack(decoded_rows),
        jnp.stack(source_grads),
        jnp.stack(target_grads),
        shard_totals[0],
        shard_totals[1],
        shard_totals[2],
        shard_totals[3],
        shard_totals[4],
        shard_totals[5],
        shard_totals[6],
        shard_totals[7],
        shard_totals[8],
        shard_totals[9],
        shard_totals[10],
        shard_totals[11],
        shard_totals[12],
        shard_totals[13],
        shard_totals[14],
    )


def solution(mesh):
    in_specs = (
        P(None, ("seq", "head"), None),
        P(None, ("seq", "head"), None),
        P(None, ("seq", "head"), None),
        P(),
        P(),
        P(),
        P(("seq", "head"), None),
        P(("seq", "head"), None),
        P(("seq", "head"), None),
        P(("seq", "head"), None),
        P(None, ("seq", "head")),
        P(None, ("seq", "head")),
        P(("seq", "head"), None),
        P(("seq", "head"), None),
        P(("seq", "head"), None),
        P(("seq", "head"), None),
        P(("seq", "head"), None),
        P(("seq", "head"), None),
        P(("seq", "head"), None),
        P(None, ("seq", "head")),
        P(None, ("seq", "head")),
    )
    out_specs = (
        P(None, ("seq", "head"), None),
        P(None, ("seq", "head"), None),
        P(None, ("seq", "head"), None),
        P(("seq", "head"), None),
        P(("seq", "head"), None),
        P(("seq", "head"), None),
        P(("seq", "head"), None),
        P(None, ("seq", "head")),
        P(None, ("seq", "head")),
        P(("seq", "head"), None),
        P(("seq", "head"), None),
        P(("seq", "head"), None),
        P(("seq", "head"), None),
        P(("seq", "head"), None),
        P(("seq", "head"), None),
        P(("seq", "head"), None),
        P(None, ("seq", "head")),
        P(None, ("seq", "head")),
    )
    return jax.shard_map(shards, mesh=mesh, in_specs=in_specs, out_specs=out_specs, check_vma=False)
```

profile of v0, /device:TPU:0, one launch (start us, length us, event | category | flops | bytes accessed | tf_op | source)
XLA Modules:
  0.0 2699.1 jit_solution(15785492716849700051)
XLA Ops:
  14.8 44.1 %all-gather.2 = bf16[32,24,10]{1,2,0:T(8,128)(2,1)S(1)} all-gather(bf16[1,24,10]{1,2,0:T(8,128)(2,1)} %bitcast.936), channel_id=1, replica_groups=mesh['seq'=8,'head'=4] {'seq','head'}, dimensions={0}, use_global_device_ids=true | all-gather | bytes 15840 | tf_op jit(solution)/shard_map/all_gather | solution.py:495
  59.9 37.3 %all-gather = bf16[32,24,14]{1,2,0:T(8,128)(2,1)S(1)} all-gather(bf16[1,24,14]{1,2,0:T(8,128)(2,1)} %bitcast.937), channel_id=1, replica_groups=mesh['seq'=8,'head'=4] {'seq','head'}, dimensions={0}, use_global_device_ids=true | all-gather | bytes 22176 | tf_op jit(solution)/shard_map/all_gather | solution.py:504
  97.6 38.3 %all-gather.1 = bf16[32,24,3]{1,2,0:T(4,128)(2,1)S(1)} all-gather(bf16[1,24,3]{1,2,0:T(4,128)(2,1)} %bitcast.938), channel_id=1, replica_groups=mesh['seq'=8,'head'=4] {'seq','head'}, dimensions={0}, use_global_device_ids=true | all-gather | bytes 4752 | tf_op jit(solution)/shard_map/all_gather | solution.py:503
  142.7 36.4 %all-gather.3 = bf16[32,24,2]{1,2,0:T(2,128)(2,1)S(1)} all-gather(bf16[1,24,2]{1,2,0:T(2,128)(2,1)S(1)} %bitcast.939), channel_id=1, replica_groups=mesh['seq'=8,'head'=4] {'seq','head'}, dimensions={0}, use_global_device_ids=true | all-gather | bytes 3168 | tf_op jit(solution)/shard_map/all_gather | solution.py:494
  346.2 14.2 while.178
  360.5 14.1 while.179
  382.3 15.2 while.180
  397.5 15.0 while.181
  433.6 11.6 multiply_convert_fusion.4
  453.0 11.1 multiply_convert_fusion.5
  469.0 160.9 %all-reduce.15 = (bf16[1024,768]{1,0:T(8,128)(2,1)}, bf16[1024,768]{1,0:T(8,128)(2,1)S(1)}) all-reduce(f32[1024,768]{1,0:T(8,128)} %fusion.114, f32[1024,768]{1,0:T(8,128)} %fusion.120), channel_id=1, replica_groups=mesh['seq'=8,'head'=4] {'seq','head'}, use_global_device_ids=true, to_apply=%region_61.62 | all-reduce | flops 1572864 | bytes 9437184 | tf_op jit(solution)/shard_map/psum | solution.py:511
  656.6 39.5 %all-gather.36.cloned.1.call-done = bf16[3072,768]{1,0:T(8,128)(2,1)} async-done(((bf16[96,768]{1,0:T(8,128)(2,1)}), bf16[3072,768]{1,0:T(8,128)(2,1)}) %all-gather.36.cloned.1.call-update) | async-done | bytes 4718608 | tf_op jit(solution)/shard_map/all_gather | solution.py:502
  813.5 16.6 while.183
  831.9 48.5 %while.185 = (s32[]{:T(128)}, f32[512,3,64]{0,2,1:T(8,128)}, f32[3,512,3,2,64]{1,4,3,2,0:T(8,128)}, s32[3]{0:T(128)S(1)}, s32[512]{0:T(512)S(1)}, /*index=5*/s32...) while((s32[]{:T(128)}, f32[512,3,64]{0,2,1:T(8,128)}, ...), condition=%wide.region_121.122_spmd.clone, body=%wide.region_115.121_spmd.clone.sunk | while | flops 514339424 | bytes 28968824 | solution.py:225
  835.6 11.8 conditional.25
  885.5 16.7 while.182
  903.9 44.8 %while.184 = (s32[]{:T(128)}, f32[512,3,64]{0,2,1:T(8,128)}, f32[3,512,3,2,64]{1,4,3,2,0:T(8,128)}, s32[3]{0:T(128)S(1)}, s32[512]{0:T(512)S(1)}, /*index=5*/s32...) while((s32[]{:T(128)}, f32[512,3,64]{0,2,1:T(8,128)}, ...), condition=%wide.region_105.106_spmd.clone, body=%wide.region_99.105_spmd.clone.sunk | while | flops 514339424 | bytes 28964732 | solution.py:225
  955.1 37.5 %collective-permute-done.4 = bf16[512,3,2,64]{0,3,2,1:T(8,128)(2,1)S(1)} collective-permute-done((bf16[512,3,2,64]{0,3,2,1:T(8,128)(2,1)S(1)}, bf16[512,3,2,64]{0,3,2,1:T(8,128)(2,1)S(1)}, u32[]{:S(2)}, u32[]{:S(2)}) %collective-permute-start.4) | collective-permute-done | bytes 393248 | tf_op jit(solution)/shard_map/ppermute | solution.py:22
  1006.8 15.2 collective-permute-done.5
  1102.3 12.2 multiply_reduce_fusion.1
  1314.3 30.7 %all-reduce.12.cloned.1.call-done = (f32[2,768]{1,0:T(2,128)}, f32[10,768]{1,0:T(8,128)}, f32[3,768]{1,0:T(4,128)}, f32[14,768]{1,0:T(8,128)}) async-done(((f32[2,768]{1,0:T(2,128)}, f32[10,768]{1,0:T(8,128)}, f32[3,768]{1,0:T(4,128)}, f32[14,768]{1,0:T(8,128)}), (f32[2,768]{1,0:T(2,128)}, f32[10,768]{1,0:T(8,128)}, f32[3,768]{1,0:T(4,128)}, f32[14,768]{1,0:T(8,128)})) %all-reduce.12.cloned.1.call-update) | async-done | bytes 89104
  1350.4 100.2 %reduce-scatter.26.cloned.1.call-done = f32[24,768]{1,0:T(8,128)} async-done(((f32[768,768]{1,0:T(8,128)}), f32[24,768]{1,0:T(8,128)}) %reduce-scatter.26.cloned.1.call-update) | async-done | bytes 73744 | tf_op jit(solution)/shard_map/reduce_scatter | solution.py:534
  1450.6 103.9 %reduce-scatter.28.cloned.1.call-done = f32[24,768]{1,0:T(8,128)} async-done(((f32[768,768]{1,0:T(8,128)}), f32[24,768]{1,0:T(8,128)}) %reduce-scatter.28.cloned.1.call-update) | async-done | bytes 73744 | tf_op jit(solution)/shard_map/reduce_scatter | solution.py:535
  1554.5 104.5 %reduce-scatter.32.cloned.1.call-done = f32[24,768]{1,0:T(8,128)} async-done(((f32[768,768]{1,0:T(8,128)}), f32[24,768]{1,0:T(8,128)}) %reduce-scatter.32.cloned.1.call-update) | async-done | bytes 73744 | tf_op jit(solution)/shard_map/reduce_scatter | solution.py:537
  1659.0 103.8 %reduce-scatter.20.cloned.1.call-done = f32[24,768]{1,0:T(8,128)} async-done(((f32[768,768]{1,0:T(8,128)}), f32[24,768]{1,0:T(8,128)}) %reduce-scatter.20.cloned.1.call-update) | async-done | bytes 73744 | tf_op jit(solution)/shard_map/reduce_scatter | solution.py:528
  1762.8 112.9 %reduce-scatter.30.cloned.1.call-done = f32[24,1536]{1,0:T(8,128)} async-done(((f32[768,1536]{1,0:T(8,128)}), f32[24,1536]{1,0:T(8,128)}) %reduce-scatter.30.cloned.1.call-update) | async-done | bytes 147472 | tf_op jit(solution)/shard_map/reduce_scatter | solution.py:536
  1875.6 124.5 %reduce-scatter.40.cloned.1.call-done = f32[24,2304]{1,0:T(8,128)} async-done(((f32[768,2304]{1,0:T(8,128)}), f32[24,2304]{1,0:T(8,128)}) %reduce-scatter.40.cloned.1.call-update) | async-done | bytes 221200
  2000.2 142.1 %reduce-scatter.34.cloned.1.call-done = f32[24,3072]{1,0:T(8,128)} async-done(((f32[768,3072]{1,0:T(8,128)}), f32[24,3072]{1,0:T(8,128)}) %reduce-scatter.34.cloned.1.call-update) | async-done | bytes 294928 | tf_op jit(solution)/shard_map/reduce_scatter | solution.py:538
  2142.3 141.1 %reduce-scatter.36.cloned.1.call-done = f32[96,768]{1,0:T(8,128)} async-done(((f32[3072,768]{1,0:T(8,128)}), f32[96,768]{1,0:T(8,128)}) %reduce-scatter.36.cloned.1.call-update) | async-done | bytes 294928 | tf_op jit(solution)/shard_map/reduce_scatter | solution.py:539
  2283.3 125.5 %reduce-scatter.38.cloned.1.call-done = f32[24,2304]{1,0:T(8,128)} async-done(((f32[768,2304]{1,0:T(8,128)}), f32[24,2304]{1,0:T(8,128)}) %reduce-scatter.38.cloned.1.call-update) | async-done | bytes 221200
  2408.8 141.4 %reduce-scatter.22.cloned.1.call-done = f32[24,3072]{1,0:T(8,128)} async-done(((f32[768,3072]{1,0:T(8,128)}), f32[24,3072]{1,0:T(8,128)}) %reduce-scatter.22.cloned.1.call-update) | async-done | bytes 294928 | tf_op jit(solution)/shard_map/reduce_scatter | solution.py:529
  2550.2 141.8 %reduce-scatter.24.cloned.1.call-done = f32[96,768]{1,0:T(8,128)} async-done(((f32[3072,768]{1,0:T(8,128)}), f32[96,768]{1,0:T(8,128)}) %reduce-scatter.24.cloned.1.call-update) | async-done | bytes 294928 | tf_op jit(solution)/shard_map/reduce_scatter | solution.py:530
  (1476 shorter events, 840.7 us)
Async XLA Ops:
  7.2 180.9 %all-gather.16.cloned.1.call-start = ((), (), s32[]{:S(2)}) async-start(), calls=%async_computation.27 | async-start | bytes 3649536 | tf_op jit(solution)/shard_map/all_gather | solution.py:496
  8.0 203.5 %all-gather.20.cloned.1.call-start = ((), (), s32[]{:S(2)}) async-start(), calls=%async_computation.29 | async-start | bytes 3649536 | tf_op jit(solution)/shard_map/all_gather | solution.py:490
  8.7 322.8 %all-gather.22.cloned.1.call-start = ((), (), s32[]{:S(2)}) async-start(), calls=%async_computation.30 | async-start | bytes 1216512 | tf_op jit(solution)/shard_map/all_gather | solution.py:491
  9.5 410.4 %all-gather.18.cloned.1.call-start = ((), (), s32[]{:S(2)}) async-start(), calls=%async_computation.28 | async-start | bytes 1216512 | tf_op jit(solution)/shard_map/all_gather | solution.py:497
  10.0 412.0 %all-gather.30.cloned.1.call-start = ((), (), s32[]{:S(2)}) async-start(), calls=%async_computation.34 | async-start | bytes 1216512 | tf_op jit(solution)/shard_map/all_gather | solution.py:498
  10.6 422.9 %all-gather.24.cloned.1.call-start = ((), (), s32[]{:S(2)}) async-start(), calls=%async_computation.31 | async-start | bytes 4866048 | tf_op jit(solution)/shard_map/all_gather | solution.py:492
  11.2 434.0 %all-gather.26.cloned.1.call-start = ((), (), s32[]{:S(2)}) async-start(), calls=%async_computation.32 | async-start | bytes 4866048 | tf_op jit(solution)/shard_map/all_gather | solution.py:493
  12.0 618.0 %all-gather.28.cloned.1.call-start = ((), (), s32[]{:S(2)}) async-start(), calls=%async_computation.33 | async-start | bytes 2433024 | tf_op jit(solution)/shard_map/all_gather | solution.py:499
  12.7 633.3 %all-gather.32.cloned.1.call-start = ((), (), s32[]{:S(2)}) async-start(), calls=%async_computation.35 | async-start | bytes 1216512 | tf_op jit(solution)/shard_map/all_gather | solution.py:500
  13.4 634.7 %all-gather.34.cloned.1.call-start = ((), (), s32[]{:S(2)}) async-start(), calls=%async_computation.36 | async-start | bytes 4866048 | tf_op jit(solution)/shard_map/all_gather | solution.py:501
  14.0 682.0 %all-gather.36.cloned.1.call-start = ((), (), s32[]{:S(2)}) async-start(), calls=%async_computation.37 | async-start | bytes 4866048 | tf_op jit(solution)/shard_map/all_gather | solution.py:502
  240.2 104.6 %collective-permute-start.1 = (bf16[512,3,2,64]{0,3,2,1:T(8,128)(2,1)}, bf16[512,3,2,64]{0,3,2,1:T(8,128)(2,1)}, u32[]{:S(2)}, u32[]{:S(2)}) collective-permute-start(bf16[512,3,2,64]{0,3,2,1:T(8,128)(2,1)} %collective-permute-done), channel_id=1, source_target_pairs={{0,4},{4,8},{8,12},{12,16},{16,20},{20,24},{24,28},{1,5},{5,9},{9,... | collective-permute-start | bytes 1179656 | tf_op jit(solution)/shard_map/ppermute | solution.py:22
  248.5 131.4 %collective-permute-start.3 = (bf16[512,3,2,64]{0,3,2,1:T(8,128)(2,1)}, bf16[512,3,2,64]{0,3,2,1:T(8,128)(2,1)}, u32[]{:S(2)}, u32[]{:S(2)}) collective-permute-start(bf16[512,3,2,64]{0,3,2,1:T(8,128)(2,1)} %collective-permute-done.2), channel_id=1, source_target_pairs={{0,4},{4,8},{8,12},{12,16},{16,20},{20,24},{24,28},{1,5},{5,9},{9,... | collective-permute-start | bytes 1179656 | tf_op jit(solution)/shard_map/ppermute | solution.py:22
  376.5 38.4 %all-to-all-start.1 = ((bf16[4,2,12288]{2,1,0:T(2,128)(2,1)}), bf16[4,2,12288]{2,1,0:T(2,128)(2,1)S(1)}, u32[]{:S(2)}, u32[]{:S(2)}) async-start(bf16[4,2,12288]{2,1,0:T(2,128)(2,1)} %reshape.1853), calls=%async_computation.1 | async-start | bytes 393216 | tf_op jit(solution)/shard_map/all_to_all | solution.py:79
  778.5 247.5 %all-reduce.14.cloned.1.call-start = ((), (), s32[]{:S(2)}) async-start(), calls=%async_computation.50 | async-start | bytes 12582912 | tf_op jit(solution)/shard_map/psum | solution.py:519
  808.2 75.5 %all-to-all-start.12 = ((bf16[128,4,192]{0,2,1:T(8,128)(2,1)}), bf16[128,4,192]{0,2,1:T(8,128)(2,1)}, u32[]{:S(2)}, u32[]{:S(2)}) async-start(bf16[128,4,192]{0,2,1:T(8,128)(2,1)} %bitcast.200), calls=%async_computation.12 | async-start | bytes 393216 | tf_op jit(solution)/shard_map/all_to_all | solution.py:75
  882.3 70.1 %collective-permute-start.6 = (bf16[512,3,2,64]{0,3,2,1:T(8,128)(2,1)}, bf16[512,3,2,64]{0,3,2,1:T(8,128)(2,1)}, u32[]{:S(2)}, u32[]{:S(2)}) collective-permute-start(bf16[512,3,2,64]{0,3,2,1:T(8,128)(2,1)} %fusion.225), channel_id=1, source_target_pairs={{4,0},{8,4},{12,8},{16,12},{20,16},{24,20},{28,24},{5,1},{9,5},{13... | collective-permute-start | bytes 1179656 | tf_op jit(solution)/shard_map/ppermute | solution.py:22
  950.1 42.5 %collective-permute-start.4 = (bf16[512,3,2,64]{0,3,2,1:T(8,128)(2,1)S(1)}, bf16[512,3,2,64]{0,3,2,1:T(8,128)(2,1)S(1)}, u32[]{:S(2)}, u32[]{:S(2)}) collective-permute-start(bf16[512,3,2,64]{0,3,2,1:T(8,128)(2,1)S(1)} %fusion.224), channel_id=1, source_target_pairs={{4,0},{8,4},{12,8},{16,12},{20,16},{24,20},{28,24},{5,1},{9,5},{13... | collective-permute-start | bytes 1179656 | tf_op jit(solution)/shard_map/ppermute | solution.py:22
  953.8 47.1 %collective-permute-start.7 = (bf16[512,3,2,64]{0,3,2,1:T(8,128)(2,1)S(1)}, bf16[512,3,2,64]{0,3,2,1:T(8,128)(2,1)S(1)}, u32[]{:S(2)}, u32[]{:S(2)}) collective-permute-start(bf16[512,3,2,64]{0,3,2,1:T(8,128)(2,1)S(1)} %fusion.191), channel_id=1, source_target_pairs={{4,0},{8,4},{12,8},{16,12},{20,16},{24,20},{28,24},{5,1},{9,5},{13... | collective-permute-start | bytes 1179656 | tf_op jit(solution)/shard_map/ppermute | solution.py:22
  1086.9 44.7 %all-to-all-start.15 = ((bf16[4,2,36864]{2,1,0:T(2,128)(2,1)}), bf16[4,2,36864]{2,1,0:T(2,128)(2,1)S(1)}, u32[]{:S(2)}, u32[]{:S(2)}) async-start(bf16[4,2,36864]{2,1,0:T(2,128)(2,1)} %reshape.1859), calls=%async_computation.15 | async-start | bytes 1179648 | tf_op jit(solution)/shard_map/all_to_all | solution.py:79
  1170.0 175.0 %all-reduce.12.cloned.1.call-start = ((), (), s32[]{:S(2)}) async-start(), calls=%async_computation.49 | async-start | bytes 233472
  1206.7 243.8 %reduce-scatter.26.cloned.1.call-start = ((), (), s32[]{:S(2)}) async-start(), calls=%async_computation.41 | async-start | bytes 2433024 | tf_op jit(solution)/shard_map/reduce_scatter | solution.py:534
  1210.6 343.9 %reduce-scatter.28.cloned.1.call-start = ((), (), s32[]{:S(2)}) async-start(), calls=%async_computation.42 | async-start | bytes 2433024 | tf_op jit(solution)/shard_map/reduce_scatter | solution.py:535
  1213.6 445.4 %reduce-scatter.32.cloned.1.call-start = ((), (), s32[]{:S(2)}) async-start(), calls=%async_computation.44 | async-start | bytes 2433024 | tf_op jit(solution)/shard_map/reduce_scatter | solution.py:537
  1216.5 546.3 %reduce-scatter.20.cloned.1.call-start = ((), (), s32[]{:S(2)}) async-start(), calls=%async_computation.38 | async-start | bytes 2433024 | tf_op jit(solution)/shard_map/reduce_scatter | solution.py:528
  1220.2 655.5 %reduce-scatter.30.cloned.1.call-start = ((), (), s32[]{:S(2)}) async-start(), calls=%async_computation.43 | async-start | bytes 4866048 | tf_op jit(solution)/shard_map/reduce_scatter | solution.py:536
  1240.1 760.1 %reduce-scatter.40.cloned.1.call-start = ((), (), s32[]{:S(2)}) async-start(), calls=%async_computation.48 | async-start | bytes 7299072
  1254.5 887.8 %reduce-scatter.34.cloned.1.call-start = ((), (), s32[]{:S(2)}) async-start(), calls=%async_computation.45 | async-start | bytes 9732096 | tf_op jit(solution)/shard_map/reduce_scatter | solution.py:538
  1262.5 1020.9 %reduce-scatter.36.cloned.1.call-start = ((), (), s32[]{:S(2)}) async-start(), calls=%async_computation.46 | async-start | bytes 9732096 | tf_op jit(solution)/shard_map/reduce_scatter | solution.py:539
  1270.2 1138.7 %reduce-scatter.38.cloned.1.call-start = ((), (), s32[]{:S(2)}) async-start(), calls=%async_computation.47 | async-start | bytes 7299072
  1285.2 1265.0 %reduce-scatter.22.cloned.1.call-start = ((), (), s32[]{:S(2)}) async-start(), calls=%async_computation.39 | async-start | bytes 9732096 | tf_op jit(solution)/shard_map/reduce_scatter | solution.py:529
  1293.7 1398.3 %reduce-scatter.24.cloned.1.call-start = ((), (), s32[]{:S(2)}) async-start(), calls=%async_computation.40 | async-start | bytes 9732096 | tf_op jit(solution)/shard_map/reduce_scatter | solution.py:530
  (380 other events, 6330.8 us)
Sparse Core Ops, SparseCore 0:
  11.0 63.2 all-gather.15
  77.2 58.8 all-gather.19
  139.0 52.9 all-gather.21
  194.7 56.1 all-gather.17
  253.7 54.0 all-gather.29
  310.5 61.7 all-gather.23
  375.2 63.1 all-gather.25
  441.2 55.6 all-gather.27
  499.8 55.5 all-gather.31
  558.1 72.4 all-gather.33
  633.5 62.4 all-gather.35
  807.7 158.2 all-reduce.13
  1206.8 138.1 all-reduce.11
  1351.6 98.9 reduce-scatter.25
  1456.3 98.1 reduce-scatter.27
  1561.1 97.9 reduce-scatter.31
  1664.7 97.9 reduce-scatter.19
  1769.6 106.0 reduce-scatter.29
  1881.9 118.2 reduce-scatter.39
  2007.5 134.7 reduce-scatter.33
  2148.7 134.5 reduce-scatter.35
  2290.5 118.2 reduce-scatter.37
  2415.3 134.8 reduce-scatter.21
  2557.5 134.4 reduce-scatter.23
where the time goes:
time: 2710 us; the launch traced here: 2700 us
  waiting for transfers between devices  1500 us (55%)
  matrix products  342 us (13%)
  blocking collectives  317 us (12%)
  local copies, waits for them, and re-layouts  227 us (8%)
  other arithmetic  143 us (5%)
  starting transfers between devices  85.9 us (3%)
  loops' own time  63 us (2%)
    unnamed x27, waiting for transfers between devices  288 us
    psum x1, blocking collectives, shards(): fetched = lax.psum(picked, ('seq', 'head')).astype(jnp.bfloat16)  161 us
    reduce_scatter x1, waiting for transfers between devices, shards(): lax.psum_scatter(local_grads[11], ('seq', 'head'), scatter_dimension=0, t...  142 us
    reduce_scatter x1, waiting for transfers between devices, shards(): lax.psum_scatter(local_grads[3], ('seq', 'head'), scatter_dimension=0, ti...  142 us
    reduce_scatter x1, waiting for transfers between devices, shards(): lax.psum_scatter(local_grads[2], ('seq', 'head'), scatter_dimension=0, ti...  141 us
    reduce_scatter x1, waiting for transfers between devices, shards(): lax.psum_scatter(local_grads[12], ('seq', 'head'), scatter_dimension=0, t...  141 us
    reduce_scatter x1, waiting for transfers between devices, shards(): lax.psum_scatter(local_grads[9], ('seq', 'head'), scatter_dimension=0, ti...  113 us
    reduce_scatter x1, waiting for transfers between devices, shards(): lax.psum_scatter(local_grads[10], ('seq', 'head'), scatter_dimension=0, t...  105 us
  transfers between devices with their start and end apart: 48, of which 23 were waited for; matrix products, arithmetic and copies ran while one was open for 21% of the time, Pallas kernels for 0%

commit v1 on v0

v1 whole, which is shorter than its diff:
```python
import functools

import jax
import jax.numpy as jnp
from jax import lax
from jax.experimental import pallas as pl
from jax.experimental.pallas import tpu as pltpu
from jax.sharding import PartitionSpec as P

D = 768
HEADS = 12
HEAD_DIM = 64
FF = 3072
MICRO = 2
STRETCH = 1024
REACH = 2
EVERY = ("seq", "head")

EPSILON = 1e-05
NEGATIVE = -1e30
MESH = pl.DeviceIdType.MESH
F32 = jnp.float32
BF16 = jnp.bfloat16


def place():
    seq, head = lax.axis_index("seq"), lax.axis_index("head")
    return seq // 2, seq % 2, head // 2, head % 2


def device(z, y, x, c):
    return (z * 2 + y, x * 2 + c)


def shard(z, y, x, c):
    return ((z * 2 + y) * 2 + x) * 2 + c


def greet(z, y, x, c):
    barrier = pltpu.get_barrier_semaphore()
    def tell(who):
        pl.semaphore_signal(barrier, inc=1, device_id=who, device_id_type=MESH)
    tell(device(z, y, x, 1 - c))
    tell(device(z, y, 1 - x, c))
    tell(device(z, 1 - y, x, c))
    @pl.when(z > 0)
    def _():
        tell(device(z - 1, y, x, c))
    @pl.when(z < 3)
    def _():
        tell(device(z + 1, y, x, c))
    pl.semaphore_wait(barrier, 3 + (z + 2) // 3 + (5 - z) // 3)


def gather_kernel(count, firsts, *refs):
    ins, outs = refs[:count], refs[count:2 * count]
    local_sem, recv_sem, send_sem = refs[2 * count:]
    z, y, x, c = place()
    greet(z, y, x, c)

    def spot(first, zo, f, l):
        return shard(zo, l, f, c) if first == "x" else shard(zo, f, l, c)

    def holder(first, zo, f, l, cc):
        return device(zo, l, f, cc) if first == "x" else device(zo, f, l, cc)

    def copy(a, src, where, who, kind, slot):
        return pltpu.make_async_remote_copy(
            src_ref=src, dst_ref=outs[a].at[where],
            send_sem=send_sem.at[a, kind, slot], recv_sem=recv_sem.at[a, where],
            device_id=who, device_id_type=MESH)

    def forward(a, zo, fo, lo, src, right, left, last):
        first = firsts[a]
        f, l = (x, y) if first == "x" else (y, x)
        where = spot(first, zo, fo, lo)
        if right:
            @pl.when((z < 3) if right is True else right & (z < 3))
            def _():
                copy(a, src, where, holder(first, z + 1, f, l, c), 1, where // 2).start()
        if left:
            @pl.when((z > 0))
            def _():
                copy(a, src, where, holder(first, z - 1, f, l, c), 2, where // 2).start()
        if last:
            copy(a, src, where, holder(first, z, f, 1 - l, c), 3, where // 2).start()
        copy(a, src, where, holder(first, z, f, l, 1 - c), 4, where // 2).start()

    def arrived(a, where):
        copy(a, outs[a].at[where], where, device(z, y, x, c), 0, 0).wait_recv()

    def axes(a):
        return (x, y) if firsts[a] == "x" else (y, x)

    locals_ = []
    for a in range(count):
        f, l = axes(a)
        first = firsts[a]
        me = spot(first, z, f, l)
        copy(a, ins[a], me, holder(first, z, 1 - f, l, c), 0, me // 2).start()
        forward(a, z, f, l, ins[a], True, True, True)
        own = pltpu.make_async_copy(ins[a], outs[a].at[me], local_sem.at[a])
        own.start()
        locals_.append(own)

    def last_arrival(zo, fsel):
        for a in range(count):
            f, l = axes(a)
            fo = f if fsel == 0 else 1 - f
            where = spot(firsts[a], zo, fo, 1 - l)
            arrived(a, where)
            forward(a, zo, fo, 1 - l, outs[a].at[where], False, False, False)

    for a in range(count):
        f, l = axes(a)
        where = spot(firsts[a], z, 1 - f, l)
        arrived(a, where)
        forward(a, z, 1 - f, l, outs[a].at[where], True, True, True)
    last_arrival(z, 0)
    last_arrival(z, 1)
    for dist in (1, 2, 3):
        for side in (0, 1):
            zo = z - dist if side == 0 else z + dist
            ok = (zo >= 0) if side == 0 else (zo <= 3)
            @pl.when(ok)
            def _():
                for fsel in (0, 1):
                    for a in range(count):
                        f, l = axes(a)
                        fo = f if fsel == 0 else 1 - f
                        where = spot(firsts[a], zo, fo, l)
                        arrived(a, where)
                        forward(a, zo, fo, l, outs[a].at[where], side == 0, side == 1, True)
        for side in (0, 1):
            zo = z - dist if side == 0 else z + dist
            ok = (zo >= 0) if side == 0 else (zo <= 3)
            @pl.when(ok)
            def _():
                last_arrival(zo, 0)
                last_arrival(zo, 1)
    def other(i, carry):
        for a in range(count):
            where = i * 2 + 1 - c
            pltpu.make_async_remote_copy(src_ref=outs[a].at[where], dst_ref=outs[a].at[where],
                send_sem=send_sem.at[a, 4, i], recv_sem=recv_sem.at[a, where],
                device_id=device(z, y, x, 1 - c), device_id_type=MESH).wait_recv()
        return carry
    lax.fori_loop(0, 16, other, 0)
    for a in range(count):
        locals_[a].wait()
        f, l = axes(a)
        first = firsts[a]
        def sent(where, kind):
            pltpu.make_async_remote_copy(src_ref=ins[a], dst_ref=outs[a].at[where],
                send_sem=send_sem.at[a, kind, where // 2], recv_sem=recv_sem.at[a, where],
                device_id=device(z, y, x, 1 - c), device_id_type=MESH).wait_send()
        sent(spot(first, z, f, l), 0)
        for zo in range(4):
            for fo in range(2):
                where = spot(first, zo, fo, l)
                sent(where, 3)
                @pl.when((zo <= z) & (z < 3))
                def _():
                    sent(where, 1)
                @pl.when((zo >= z) & (z > 0))
                def _():
                    sent(where, 2)
        def sent_core(i, carry):
            sent(i * 2 + c, 4)
            return carry
        lax.fori_loop(0, 16, sent_core, 0)


def gather_all(arrays, firsts, collective_id):
    count = len(arrays)
    return pl.pallas_call(
        functools.partial(gather_kernel, count, tuple(firsts)),
        out_shape=[jax.ShapeDtypeStruct((32,) + v.shape, v.dtype) for v in arrays],
        in_specs=[pl.BlockSpec(memory_space=pl.ANY)] * count,
        out_specs=[pl.BlockSpec(memory_space=pl.ANY)] * count,
        scratch_shapes=[pltpu.SemaphoreType.DMA((count,)), pltpu.SemaphoreType.DMA((count, 32)),
                        pltpu.SemaphoreType.DMA((count, 5, 16))],
        compiler_params=pltpu.CompilerParams(collective_id=collective_id, has_side_effects=True),
    )(*arrays)


def scatter_kernel(count, firsts, *refs):
    grads, outs = refs[:count], refs[count:2 * count]
    held, mine, near, right, left, last = [refs[(2 + k) * count:(3 + k) * count] for k in range(6)]
    mine_sem, core_sem, near_sem, right_sem, left_sem, last_sem = refs[8 * count:]
    z, y, x, c = place()
    greet(z, y, x, c)
    half = z // 2

    def axes(a):
        return (x, y) if firsts[a] == "x" else (y, x)

    def block(a, zt, f, l):
        return (zt * 2 + l) * 2 + f if firsts[a] == "x" else (zt * 2 + f) * 2 + l

    def remote(a, src, dst, sems, slot, who):
        return pltpu.make_async_remote_copy(
            src_ref=src, dst_ref=dst, send_sem=sems.at[a, 0, slot], recv_sem=sems.at[a, 1, slot],
            device_id=who, device_id_type=MESH)

    def core_copy(a, q):
        return remote(a, grads[a].at[q * 2 + 1 - c], held[a].at[q], core_sem, q, device(z, y, x, 1 - c))

    def mine_copy(a, q):
        return pltpu.make_async_copy(grads[a].at[q * 2 + c], mine[a].at[q], mine_sem.at[a, q])

    def near_copy(a, q, slot):
        who = device(z, y, 1 - x, c) if firsts[a] == "x" else device(z, 1 - y, x, c)
        return remote(a, held[a].at[q], near[a].at[slot], near_sem, slot, who)

    def right_copy(a, q, slot):
        return remote(a, held[a].at[q], right[a].at[slot], right_sem, slot, device(z + 1, y, x, c))

    def left_copy(a, q, slot):
        return remote(a, held[a].at[q], left[a].at[slot], left_sem, slot, device(z - 1, y, x, c))

    def last_copy(a, q):
        who = device(z, 1 - y, x, c) if firsts[a] == "x" else device(z, y, 1 - x, c)
        return remote(a, held[a].at[q], last[a].at[0], last_sem, 0, who)

    def far(k):
        return 3 - k + half * (2 * k - 3)

    def others(k):
        down = 3 - k - (k // 2) * z
        up = k + (k // 2) * (3 - z)
        return down + half * (up - down)

    def wide(ref, q):
        return ref[q].astype(jnp.float32)

    for side in (1, 0):
        def start(i, carry, side=side):
            for a in range(count):
                f, l = axes(a)
                q = block(a, far(i // 2), (1 - f) if side else f, i % 2)
                core_copy(a, q).start()
                mine_copy(a, q).start()
            return carry
        lax.fori_loop(0, 8, start, 0)

    def first_phase(i, carry):
        zt, lt = far(i // 2), i % 2
        for a in range(count):
            f, l = axes(a)
            q = block(a, zt, 1 - f, lt)
            core_copy(a, q).wait_recv()
            mine_copy(a, q).wait()
            held[a][q] = (wide(held[a], q) + wide(mine[a], q)).astype(jnp.bfloat16)
            near_copy(a, q, zt * 2 + lt).start()
        return carry
    lax.fori_loop(0, 8, first_phase, 0)

    def gathered(a, zt, lt):
        f, l = axes(a)
        q = block(a, zt, f, lt)
        core_copy(a, q).wait_recv()
        mine_copy(a, q).wait()
        near_copy(a, q, zt * 2 + lt).wait_recv()
        held[a][q] = (wide(held[a], q) + wide(mine[a], q) + wide(near[a], zt * 2 + lt)).astype(jnp.bfloat16)
        return q

    def z_phase(i, carry):
        zt, lt = others(i // 2), i % 2
        for a in range(count):
            q = gathered(a, zt, lt)
            @pl.when(zt > z)
            def _():
                slot = (zt - 1) * 2 + lt
                @pl.when(z > 0)
                def _():
                    right_copy(a, q, slot).wait_recv()
                    held[a][q] = (wide(held[a], q) + wide(right[a], slot)).astype(jnp.bfloat16)
                right_copy(a, q, slot).start()
            @pl.when(zt < z)
            def _():
                slot = zt * 2 + lt
                @pl.when(z < 3)
                def _():
                    left_copy(a, q, slot).wait_recv()
                    held[a][q] = (wide(held[a], q) + wide(left[a], slot)).astype(jnp.bfloat16)
                left_copy(a, q, slot).start()
        return carry
    lax.fori_loop(0, 6, z_phase, 0)

    for side in (1, 0):
        for a in range(count):
            f, l = axes(a)
            lt = (1 - l) if side else l
            q = gathered(a, z, lt)
            @pl.when(z > 0)
            def _():
                slot = (z - 1) * 2 + lt
                right_copy(a, q, slot).wait_recv()
                held[a][q] = (wide(held[a], q) + wide(right[a], slot)).astype(jnp.bfloat16)
            @pl.when(z < 3)
            def _():
                slot = z * 2 + lt
                left_copy(a, q, slot).wait_recv()
                held[a][q] = (wide(held[a], q) + wide(left[a], slot)).astype(jnp.bfloat16)
            if side:
                last_copy(a, q).start()
    for a in range(count):
        f, l = axes(a)
        q = block(a, z, f, l)
        last_copy(a, q).wait_recv()
        outs[a][...] = (wide(held[a], q) + wide(last[a], 0)).astype(outs[a].dtype)
    def sent(i, carry):
        for a in range(count):
            f, l = axes(a)
            core_copy(a, i).wait_send()
        return carry
    lax.fori_loop(0, 16, sent, 0)
    def sent_near(i, carry):
        for a in range(count):
            f, l = axes(a)
            near_copy(a, block(a, i // 2, 1 - f, i % 2), i).wait_send()
        return carry
    lax.fori_loop(0, 8, sent_near, 0)
    def sent_z(i, carry):
        zt, lt = others(i // 2), i % 2
        for a in range(count):
            f, l = axes(a)
            q = block(a, zt, f, lt)
            @pl.when(zt > z)
            def _():
                right_copy(a, q, (zt - 1) * 2 + lt).wait_send()
            @pl.when(zt < z)
            def _():
                left_copy(a, q, zt * 2 + lt).wait_send()
        return carry
    lax.fori_loop(0, 6, sent_z, 0)
    for a in range(count):
        f, l = axes(a)
        last_copy(a, block(a, z, f, 1 - l)).wait_send()


def scatter_sum(arrays, firsts, collective_id, out_dtype=jnp.float32):
    count = len(arrays)
    shapes = [v.shape[1:] for v in arrays]
    scratch = []
    for slots in (16, 16, 8, 6, 6, 1):
        scratch += [pltpu.VMEM((slots,) + s, jnp.bfloat16) for s in shapes]
    D = pltpu.SemaphoreType.DMA
    return pl.pallas_call(
        functools.partial(scatter_kernel, count, tuple(firsts)),
        out_shape=[jax.ShapeDtypeStruct(s, out_dtype) for s in shapes],
        in_specs=[pl.BlockSpec(memory_space=pl.ANY)] * count,
        out_specs=[pl.BlockSpec(memory_space=pltpu.VMEM)] * count,
        scratch_shapes=scratch + [D((count, 16)), D((count, 2, 16)), D((count, 2, 8)), D((count, 2, 6)), D((count, 2, 6)), D((count, 2, 1))],
        compiler_params=pltpu.CompilerParams(collective_id=collective_id, has_side_effects=True, vmem_limit_bytes=60 << 20),
    )(*arrays)


def known_mesh():
    return lax.axis_size("seq") == 8 and lax.axis_size("head") == 4


def gather(arrays, firsts, collective_id):
    if known_mesh():
        return gather_all(arrays, firsts, collective_id)
    return [lax.all_gather(v, EVERY, axis=0, tiled=False) for v in arrays]


def scatter(arrays, firsts, collective_id, out_dtype=F32):
    if known_mesh():
        return scatter_sum(arrays, firsts, collective_id, out_dtype)
    return [
        lax.psum_scatter(v, EVERY, scatter_dimension=0, tiled=False).astype(out_dtype)
        for v in arrays
    ]


def fill(target, refs, columns):
    at = 0
    for ref in refs:
        rows = ref.shape[2]
        for p in range(ref.shape[0]):
            target[at : at + rows] = ref[p, 0, :, columns]
            at += rows


def spill(value, refs, columns):
    at = 0
    for ref in refs:
        rows = ref.shape[2]
        for p in range(ref.shape[0]):
            ref[p, 0, :, columns] = value[at : at + rows].astype(ref.dtype)
            at += rows


def scores_of(keys, query, allowed):
    scores = lax.dot_general(keys, query, (((1,), (1,)), ((), ())), preferred_element_type=F32)
    return jnp.where(allowed, scores * 0.125, NEGATIVE)


def soft_columns(scores):
    weights = jnp.exp(scores - jnp.max(scores, axis=0, keepdims=True))
    return weights * (1.0 / jnp.sum(weights, axis=0, keepdims=True))


def allowed_pairs(key_ref, query_ref, start, tile, causal):
    doc_key, doc_query = key_ref[0, :, 0:1], query_ref[0, 0:1, pl.ds(start, tile)]
    allowed = doc_key == doc_query
    if causal:
        allowed &= key_ref[0, :, 1:2] <= query_ref[0, 1:2, pl.ds(start, tile)]
    return allowed


def attend_kernel(heads, tile, causal, *refs):
    key_ref, query_ref, own_ref = refs[:3]
    prior = refs[3:-5]
    out_ref, key_s, value_s, query_s, result_s = refs[-5:]
    group = query_s.shape[0]
    for h in range(heads):
        fill(key_s, (*prior, own_ref), slice(h * 128, h * 128 + 64))
        fill(value_s, (*prior, own_ref), slice(h * 128 + 64, h * 128 + 128))
        at = heads * 128 + h * 64
        fill(query_s, (own_ref,), slice(at, at + 64))

        def step(i, carry):
            start = pl.multiple_of(i * tile, tile)
            allowed = allowed_pairs(key_ref, query_ref, start, tile, causal)
            probs = soft_columns(scores_of(key_s[...], query_s[pl.ds(start, tile), :], allowed))
            out = lax.dot_general(
                probs.astype(BF16), value_s[...], (((0,), (0,)), ((), ())), preferred_element_type=F32
            )
            result_s[pl.ds(start, tile), :] = out.astype(BF16)
            return carry

        lax.fori_loop(0, group // tile, step, 0)
        spill(result_s[...], (out_ref,), slice(h * 64, h * 64 + 64))


def rows_spec(shape):
    return pl.BlockSpec((shape[0], 1) + shape[2:], lambda m: (0, m, 0, 0))


def whole_spec(shape):
    return pl.BlockSpec((1,) + shape[1:], lambda m: (m, 0, 0))


def attend(joined, prior, key_info, query_info, causal, tile=256):
    parts, micro, rows, columns = joined.shape
    heads, group = columns // 192, parts * rows
    keys = key_info.shape[1]
    out = (parts, micro, rows, heads * 64)
    return pl.pallas_call(
        functools.partial(attend_kernel, heads, tile, causal),
        grid=(micro,),
        out_shape=jax.ShapeDtypeStruct(out, BF16),
        in_specs=[whole_spec(key_info.shape), whole_spec(query_info.shape), rows_spec(joined.shape)]
        + [rows_spec(p.shape) for p in prior],
        out_specs=rows_spec(out),
        scratch_shapes=[
            pltpu.VMEM((keys, 64), BF16),
            pltpu.VMEM((keys, 64), BF16),
            pltpu.VMEM((group, 64), BF16),
            pltpu.VMEM((group, 64), BF16),
        ],
        compiler_params=pltpu.CompilerParams(vmem_limit_bytes=48 << 20),
        cost_estimate=pl.CostEstimate(
            flops=4 * micro * heads * group * keys * 128,
            transcendentals=micro * heads * group * keys,
            bytes_accessed=joined.size * 4,
        ),
        name="attend",
    )(key_info, query_info, joined, *prior)


def attend_back_kernel(heads, tile, causal, count, *refs):
    key_ref, query_ref, own_ref, grad_ref = refs[:4]
    prior = refs[4 : 4 + count]
    out_ref, *prior_out = refs[4 + count : 5 + 2 * count]
    key_s, value_s, query_s, grad_s, gk_s, gv_s, result_s = refs[5 + 2 * count :]
    group = query_s.shape[0]
    for h in range(heads):
        key_cut, value_cut = slice(h * 128, h * 128 + 64), slice(h * 128 + 64, h * 128 + 128)
        fill(key_s, (*prior, own_ref), key_cut)
        fill(value_s, (*prior, own_ref), value_cut)
        query_cut = slice(heads * 128 + h * 64, heads * 128 + h * 64 + 64)
        fill(query_s, (own_ref,), query_cut)
        fill(grad_s, (grad_ref,), slice(h * 64, h * 64 + 64))
        gk_s[...] = jnp.zeros_like(gk_s)
        gv_s[...] = jnp.zeros_like(gv_s)

        def step(i, carry):
            start = pl.multiple_of(i * tile, tile)
            here = pl.ds(start, tile)
            allowed = allowed_pairs(key_ref, query_ref, start, tile, causal)
            query, grad_out = query_s[here, :], grad_s[here, :]
            probs = soft_columns(scores_of(key_s[...], query, allowed))
            grad_probs = lax.dot_general(
                value_s[...], grad_out, (((1,), (1,)), ((), ())), preferred_element_type=F32
            )
            delta = jnp.sum(probs * grad_probs, axis=0, keepdims=True)
            grad_scores = (probs * (grad_probs - delta)).astype(BF16)
            gv_s[...] += jnp.dot(probs.astype(BF16), grad_out, preferred_element_type=F32)
            gk_s[...] += jnp.dot(grad_scores, query, preferred_element_type=F32)
            grad_query = lax.dot_general(
                grad_scores, key_s[...], (((0,), (0,)), ((), ())), preferred_element_type=F32
            )
            result_s[here, :] = grad_query * 0.125
            return carry

        lax.fori_loop(0, group // tile, step, 0)
        spill(result_s[...], (out_ref,), query_cut)
        spill(gk_s[...] * 0.125, (*prior_out, out_ref), key_cut)
        spill(gv_s[...], (*prior_out, out_ref), value_cut)


def attend_back(joined, prior, key_info, query_info, grad, causal, out_dtype, tile=256):
    parts, micro, rows, columns = joined.shape
    heads, group = columns // 192, parts * rows
    keys = key_info.shape[1]
    return pl.pallas_call(
        functools.partial(attend_back_kernel, heads, tile, causal, len(prior)),
        grid=(micro,),
        out_shape=[jax.ShapeDtypeStruct(joined.shape, out_dtype)]
        + [jax.ShapeDtypeStruct(p.shape, BF16) for p in prior],
        in_specs=[
            whole_spec(key_info.shape),
            whole_spec(query_info.shape),
            rows_spec(joined.shape),
            rows_spec(grad.shape),
        ]
        + [rows_spec(p.shape) for p in prior],
        out_specs=[rows_spec(joined.shape)] + [rows_spec(p.shape) for p in prior],
        scratch_shapes=[
            pltpu.VMEM((keys, 64), BF16),
            pltpu.VMEM((keys, 64), BF16),
            pltpu.VMEM((group, 64), BF16),
            pltpu.VMEM((group, 64), BF16),
            pltpu.VMEM((keys, 64), F32),
            pltpu.VMEM((keys, 64), F32),
            pltpu.VMEM((group, 64), F32),
        ],
        compiler_params=pltpu.CompilerParams(vmem_limit_bytes=48 << 20),
        cost_estimate=pl.CostEstimate(
            flops=10 * micro * heads * group * keys * 128,
            transcendentals=micro * heads * group * keys,
            bytes_accessed=joined.size * 6,
        ),
        name="attend_back",
    )(key_info, query_info, joined, grad, *prior)


def cross_kernel(query_ref, pairs_ref, out_ref):
    for i in range(D // 128):
        outs = []
        for h in range(2):
            at = i * 128 + h * 64
            query, keys = query_ref[0, :, at : at + 64], pairs_ref[0, :, at : at + 64]
            values = pairs_ref[0, :, D + at : D + at + 64]
            scores = lax.dot_general(keys, query, (((1,), (1,)), ((), ())), preferred_element_type=F32)
            probs = soft_columns(scores * 0.125)
            outs.append(
                lax.dot_general(
                    probs.astype(BF16), values, (((0,), (0,)), ((), ())), preferred_element_type=F32
                )
            )
        out_ref[0, :, i * 128 : i * 128 + 128] = jnp.concatenate(outs, axis=1).astype(BF16)


def cross(query, pairs):
    micro, rows, _ = query.shape
    keys = pairs.shape[1]
    return pl.pallas_call(
        cross_kernel,
        grid=(micro,),
        out_shape=jax.ShapeDtypeStruct(query.shape, BF16),
        in_specs=[whole_spec(query.shape), whole_spec(pairs.shape)],
        out_specs=whole_spec(query.shape),
        compiler_params=pltpu.CompilerParams(vmem_limit_bytes=48 << 20),
        cost_estimate=pl.CostEstimate(
            flops=4 * micro * HEADS * rows * keys * 128,
            transcendentals=micro * HEADS * rows * keys,
            bytes_accessed=pairs.size * 2,
        ),
        name="cross",
    )(query, pairs)


def cross_back_kernel(query_ref, pairs_ref, grad_ref, grad_query_ref, grad_pairs_ref):
    for i in range(D // 128):
        query_parts, key_parts, value_parts = [], [], []
        for h in range(2):
            at = i * 128 + h * 64
            query, keys = query_ref[0, :, at : at + 64], pairs_ref[0, :, at : at + 64]
            values, grad_out = pairs_ref[0, :, D + at : D + at + 64], grad_ref[0, :, at : at + 64]
            scores = lax.dot_general(keys, query, (((1,), (1,)), ((), ())), preferred_element_type=F32)
            probs = soft_columns(scores * 0.125)
            grad_probs = lax.dot_general(
                values, grad_out, (((1,), (1,)), ((), ())), preferred_element_type=F32
            )
            delta = jnp.sum(probs * grad_probs, axis=0, keepdims=True)
            grad_scores = (probs * (grad_probs - delta)).astype(BF16)
            value_parts.append(jnp.dot(probs.astype(BF16), grad_out, preferred_element_type=F32))
            key_parts.append(jnp.dot(grad_scores, query, preferred_element_type=F32) * 0.125)
            query_parts.append(
                lax.dot_general(
                    grad_scores, keys, (((0,), (0,)), ((), ())), preferred_element_type=F32
                )
                * 0.125
            )
        cut = slice(i * 128, i * 128 + 128)
        grad_query_ref[0, :, cut] = jnp.concatenate(query_parts, axis=1).astype(BF16)
        grad_pairs_ref[0, :, cut] = jnp.concatenate(key_parts, axis=1).astype(BF16)
        cut = slice(D + i * 128, D + i * 128 + 128)
        grad_pairs_ref[0, :, cut] = jnp.concatenate(value_parts, axis=1).astype(BF16)


def cross_back(query, pairs, grad):
    micro, rows, _ = query.shape
    keys = pairs.shape[1]
    return pl.pallas_call(
        cross_back_kernel,
        grid=(micro,),
        out_shape=[jax.ShapeDtypeStruct(query.shape, BF16), jax.ShapeDtypeStruct(pairs.shape, BF16)],
        in_specs=[whole_spec(query.shape), whole_spec(pairs.shape), whole_spec(grad.shape)],
        out_specs=[whole_spec(query.shape), whole_spec(pairs.shape)],
        compiler_params=pltpu.CompilerParams(vmem_limit_bytes=48 << 20),
        cost_estimate=pl.CostEstimate(
            flops=10 * micro * HEADS * rows * keys * 128,
            transcendentals=micro * HEADS * rows * keys,
            bytes_accessed=pairs.size * 4,
        ),
        name="cross_back",
    )(query, pairs, grad)


def norm(resid, gain, shift):
    center = resid - jnp.mean(resid, axis=-1, keepdims=True)
    scale = lax.rsqrt(jnp.mean(center * center, axis=-1, keepdims=True) + EPSILON)
    hat = center * scale
    return hat * gain + shift, (hat, scale)


def norm_back(grad, kept, gain):
    hat, scale = kept
    inner = grad * gain
    grad_resid = scale * (
        inner
        - jnp.mean(inner, axis=-1, keepdims=True)
        - hat * jnp.mean(inner * hat, axis=-1, keepdims=True)
    )
    return grad_resid, jnp.sum(grad * hat, axis=0), jnp.sum(grad, axis=0)


def gelu(value):
    return value * (1.0 + lax.erf(value * 0.7071067811865476)) * 0.5


def gelu_slope(value):
    bell = jnp.exp(value * value * -0.5) * 0.3989422804014327
    return 0.5 * (1.0 + lax.erf(value * 0.7071067811865476)) + value * bell


def mm(left, right):
    return jnp.dot(left, right, preferred_element_type=F32)


def mm_rows(left, right):
    return lax.dot_general(left, right, (((0,), (0,)), ((), ())), preferred_element_type=F32)


def mm_back(left, right):
    return lax.dot_general(left, right, (((1,), (1,)), ((), ())), preferred_element_type=F32)


def row_sum(value):
    return jnp.sum(value.astype(F32), axis=0)


def doc_starts(lengths):
    count = lengths.shape[1]
    before = jnp.arange(count)[None, :] < jnp.arange(count)[:, None]
    return jnp.sum(jnp.where(before[None], lengths[:, None, :], 0), axis=2)


def doc_ids(starts, positions):
    return jnp.sum((starts[:, None, :] <= positions[None, :, None]).astype(jnp.int32), axis=2) - 1


def key_and_query_info(starts, key_pos, query_pos):
    key_docs, query_docs = doc_ids(starts, key_pos), doc_ids(starts, query_pos)
    micro = starts.shape[0]
    key_info = jnp.stack(
        [key_docs, jnp.broadcast_to(key_pos, (micro,) + key_pos.shape)], axis=2
    )
    query_info = jnp.stack(
        [query_docs, jnp.broadcast_to(query_pos, (micro,) + query_pos.shape)], axis=1
    )
    return key_info, query_info


def head_columns(full, parts):
    rows = full.shape[0]
    width = full.shape[1] // parts
    mine = lax.dynamic_slice_in_dim(full, lax.axis_index("head") * width, width, 1)
    mine = mine.reshape(rows, width // 192, 3, HEAD_DIM)
    return jnp.concatenate(
        [mine[:, :, 1:].reshape(rows, -1), mine[:, :, 0].reshape(rows, -1)], axis=1
    )


def head_columns_back(grad, parts):
    rows, width = grad.shape
    heads = width // 192
    pairs = grad[:, : heads * 128].reshape(rows, heads, 2, HEAD_DIM)
    query = grad[:, heads * 128 :].reshape(rows, heads, 1, HEAD_DIM)
    mine = jnp.concatenate([query, pairs], axis=2).reshape(rows, width)
    full = jnp.zeros((rows, width * parts), grad.dtype)
    return lax.dynamic_update_slice_in_dim(full, mine, lax.axis_index("head") * width, 1)


def joined_bias(biases):
    query_part = biases[0].reshape(HEADS, HEAD_DIM)
    value_part = biases[1].reshape(HEADS, HEAD_DIM)
    return jnp.stack([query_part, jnp.zeros_like(query_part), value_part], axis=1).reshape(1, 3 * D)


def to_tokens(value):
    parts, micro, rows, columns = value.shape
    got = lax.all_to_all(value, "head", split_axis=0, concat_axis=0, tiled=True)
    return got.transpose(1, 2, 0, 3).reshape(micro * rows, parts * columns)


def to_heads(value, parts, micro):
    rows = value.shape[0] // micro
    split = value.reshape(micro, rows, parts, -1).transpose(2, 0, 1, 3)
    return lax.all_to_all(split, "head", split_axis=0, concat_axis=0, tiled=True)


def from_before(value, by):
    count = lax.axis_size("seq")
    return lax.ppermute(value, "seq", [(i, i + by) for i in range(count - by)])


def to_before(value, by):
    count = lax.axis_size("seq")
    return lax.ppermute(value, "seq", [(i + by, i) for i in range(count - by)])


def pack_rows(value, width):
    padded = jnp.pad(value, ((0, 0), (0, 8 * width - value.shape[1])))
    return padded.reshape(value.shape[0], 8, width)


def shards(
    source,
    target,
    cotangent,
    src_lengths,
    tgt_lengths,
    retrieved,
    encoder_qkv,
    encoder_out,
    encoder_up,
    encoder_down,
    encoder_gains,
    encoder_biases,
    decoder_qkv,
    decoder_out,
    cross_query,
    cross_keyvalue,
    cross_out,
    decoder_up,
    decoder_down,
    decoder_gains,
    decoder_biases,
):
    micro, src_rows, _ = source.shape
    tgt_rows = target.shape[1]
    parts = lax.axis_size("head")
    devices = parts * lax.axis_size("seq")
    seq, me = lax.axis_index("seq"), lax.axis_index(EVERY)
    src_group, tgt_group = src_rows * parts, tgt_rows * parts
    asked = retrieved.shape[1]
    source_rows = source.reshape(micro * src_rows, D)
    target_rows = target.reshape(micro * tgt_rows, D)

    source_all = lax.all_gather(source, "head", axis=0, tiled=False)
    target_all = lax.all_gather(target, "head", axis=0, tiled=False)

    small = jnp.concatenate([encoder_gains, encoder_biases, decoder_gains, decoder_biases], axis=0)
    small_rows, small_width = small.shape
    small_pack = pack_rows(small.reshape(1, small_rows * small_width), D)[0]
    encoder_full = gather(
        [encoder_qkv, encoder_out, encoder_up, encoder_down, small_pack], "xyyxx", 0
    )
    decoder_full = gather(
        [decoder_qkv, decoder_out, cross_query, cross_keyvalue, cross_out, decoder_up, decoder_down],
        "xyyxyyx",
        1,
    )
    e_qkv, e_out, e_up, e_down = [v.reshape(-1, v.shape[-1]) for v in encoder_full[:4]]
    d_qkv, d_out, c_query, c_pairs, c_out, d_up, d_down = [
        v.reshape(-1, v.shape[-1]) for v in decoder_full
    ]
    small_full = encoder_full[4].reshape(devices, -1)[:, : small_rows * small_width]
    small_full = (
        small_full.reshape(devices, small_rows, small_width).transpose(1, 0, 2).reshape(small_rows, D)
    ).astype(F32)
    e_gains, e_bias = small_full[0:2], small_full[2:12]
    d_gains, d_bias = small_full[12:15], small_full[15:29]

    src_pos = seq * src_group + jnp.arange(src_group, dtype=jnp.int32)
    src_info = key_and_query_info(doc_starts(src_lengths), src_pos, src_pos)
    tgt_pos = seq * tgt_group + jnp.arange(tgt_group, dtype=jnp.int32)
    tgt_key_pos = (seq - REACH) * tgt_group + jnp.arange((REACH + 1) * tgt_group, dtype=jnp.int32)
    tgt_info = key_and_query_info(doc_starts(tgt_lengths), tgt_key_pos, tgt_pos)

    e_qkv_here = head_columns(e_qkv, parts)
    e_joined = (
        mm(source_all.reshape(-1, D), e_qkv_here) + head_columns(joined_bias(e_bias), parts)
    ).astype(BF16)
    e_joined = e_joined.reshape(parts, micro, src_rows, -1)
    e_mixed = to_tokens(attend(e_joined, [], *src_info, False))
    e_first, e_kept_one = norm(
        source_rows.astype(F32) + mm(e_mixed, e_out) + e_bias[2], e_gains[0], e_bias[3]
    )
    e_first_low = e_first.astype(BF16)
    e_hidden = mm(e_first_low, e_up) + e_bias[4:8].reshape(FF)
    e_active = gelu(e_hidden).astype(BF16)
    e_result, e_kept_two = norm(
        e_first + mm(e_active, e_down) + e_bias[8], e_gains[1], e_bias[9]
    )

    d_qkv_here = head_columns(d_qkv, parts)
    d_joined = (
        mm(target_all.reshape(-1, D), d_qkv_here) + head_columns(joined_bias(d_bias), parts)
    ).astype(BF16)
    d_joined = d_joined.reshape(parts, micro, tgt_rows, -1)
    d_pairs = d_joined[..., : d_joined.shape[-1] // 3 * 2]
    d_prior = [from_before(d_pairs, by) for by in range(REACH, 0, -1)]
    d_mixed = to_tokens(attend(d_joined, d_prior, *tgt_info, True))
    d_first, d_kept_one = norm(
        target_rows.astype(F32) + mm(d_mixed, d_out) + d_bias[2], d_gains[0], d_bias[3]
    )
    d_first_low = d_first.astype(BF16)
    queries = (mm(d_first_low, c_query) + d_bias[4]).astype(BF16).reshape(micro, tgt_rows, D)

    src_own = me * src_rows + jnp.arange(src_rows, dtype=jnp.int32)
    select = (retrieved[:, :, None] == src_own[None, None, :]).astype(BF16)
    picked = jnp.einsum(
        "mrs,msd->mrd",
        select,
        e_result.astype(BF16).reshape(micro, src_rows, D),
        preferred_element_type=F32,
    ).astype(BF16)
    picked = [picked[m].reshape(devices, asked // devices, D) for m in range(micro)]
    fetched = gather(scatter(picked, "xy", 2, BF16), "xy", 3)
    fetched = jnp.concatenate([v.reshape(asked, D) for v in fetched], axis=0)
    pair_bias = jnp.concatenate([jnp.zeros((D,), F32), d_bias[5]])
    pairs = (mm(fetched, c_pairs) + pair_bias).astype(BF16).reshape(micro, asked, 2 * D)

    crossed = cross(queries, pairs).reshape(micro * tgt_rows, D)
    d_second, d_kept_two = norm(
        d_first + mm(crossed, c_out) + d_bias[6], d_gains[1], d_bias[7]
    )
    d_second_low = d_second.astype(BF16)
    d_hidden = mm(d_second_low, d_up) + d_bias[8:12].reshape(FF)
    d_active = gelu(d_hidden).astype(BF16)
    decoded, d_kept_three = norm(
        d_second + mm(d_active, d_down) + d_bias[12], d_gains[2], d_bias[13]
    )

    grad = cotangent.reshape(micro * tgt_rows, D).astype(F32)
    g_sum, d_gain_three, d_shift_three = norm_back(grad, d_kept_three, d_gains[2])
    g_third = g_sum.astype(BF16)
    w_d_down = mm_rows(d_active, g_third)
    g_hidden = (mm_back(g_third, d_down) * gelu_slope(d_hidden)).astype(BF16)
    w_d_up = mm_rows(d_second_low, g_hidden)
    g_second = g_sum + mm_back(g_hidden, d_up)
    g_sum_two, d_gain_two, d_shift_two = norm_back(g_second, d_kept_two, d_gains[1])
    g_branch_cross = g_sum_two.astype(BF16)
    w_c_out = mm_rows(crossed, g_branch_cross)
    g_crossed = mm_back(g_branch_cross, c_out).astype(BF16).reshape(micro, tgt_rows, D)
    g_queries, g_pairs = cross_back(queries, pairs, g_crossed)
    g_queries = g_queries.reshape(micro * tgt_rows, D)
    g_pairs = g_pairs.reshape(micro * asked, 2 * D)
    g_fetched = mm_back(g_pairs, c_pairs).astype(BF16).reshape(micro, asked, D)
    g_fetched = [g_fetched[m].reshape(devices, asked // devices, D) for m in range(micro)]
    g_fetched = gather(scatter(g_fetched, "xy", 4, BF16), "xy", 5)
    w_c_pairs = mm_rows(fetched, g_pairs)
    w_c_query = mm_rows(d_first_low, g_queries)
    g_first = g_sum_two + mm_back(g_queries, c_query)
    g_resid, d_gain_one, d_shift_one = norm_back(g_first, d_kept_one, d_gains[0])
    g_branch = g_resid.astype(BF16)
    w_d_out = mm_rows(d_mixed, g_branch)
    g_mixed = mm_back(g_branch, d_out).astype(BF16)
    g_attended = to_heads(g_mixed, parts, micro)
    g_own, *g_prior = attend_back(d_joined, d_prior, *tgt_info, g_attended, True, F32)
    width = d_pairs.shape[-1]
    g_back = sum(to_before(g, by).astype(F32) for g, by in zip(g_prior, range(REACH, 0, -1)))
    g_joined = jnp.concatenate(
        [(g_own[..., :width] + g_back).astype(BF16), g_own[..., width:].astype(BF16)], axis=-1
    ).reshape(parts * micro * tgt_rows, -1)
    w_d_qkv = mm_rows(target_all.reshape(-1, D), g_joined)
    g_target_all = mm_back(g_joined, d_qkv_here).astype(BF16)
    g_target = g_resid + lax.psum_scatter(
        g_target_all.reshape(parts, micro * tgt_rows, D), "head", scatter_dimension=0, tiled=False
    ).astype(F32)
    d_joined_sums = head_columns_back(row_sum(g_joined)[None], parts).reshape(HEADS, 3, HEAD_DIM)

    g_result = jnp.einsum(
        "mrs,mrd->msd",
        select,
        jnp.stack([v.reshape(asked, D) for v in g_fetched]),
        preferred_element_type=F32,
    ).reshape(micro * src_rows, D)
    g_sum, e_gain_two, e_shift_two = norm_back(g_result, e_kept_two, e_gains[1])
    g_second_low = g_sum.astype(BF16)
    w_e_down = mm_rows(e_active, g_second_low)
    ge_hidden = (mm_back(g_second_low, e_down) * gelu_slope(e_hidden)).astype(BF16)
    w_e_up = mm_rows(e_first_low, ge_hidden)
    g_first = g_sum + mm_back(ge_hidden, e_up)
    ge_resid, e_gain_one, e_shift_one = norm_back(g_first, e_kept_one, e_gains[0])
    ge_branch = ge_resid.astype(BF16)
    w_e_out = mm_rows(e_mixed, ge_branch)
    ge_mixed = mm_back(ge_branch, e_out).astype(BF16)
    ge_attended = to_heads(ge_mixed, parts, micro)
    (ge_joined,) = attend_back(e_joined, [], *src_info, ge_attended, False, BF16)
    ge_joined = ge_joined.reshape(parts * micro * src_rows, -1)
    w_e_qkv = mm_rows(source_all.reshape(-1, D), ge_joined)
    g_source_all = mm_back(ge_joined, e_qkv_here).astype(BF16)
    g_source = ge_resid + lax.psum_scatter(
        g_source_all.reshape(parts, micro * src_rows, D), "head", scatter_dimension=0, tiled=False
    ).astype(F32)
    e_joined_sums = head_columns_back(row_sum(ge_joined)[None], parts).reshape(HEADS, 3, HEAD_DIM)

    def pieces(value):
        return value.astype(BF16).reshape(devices, value.shape[0] // devices, value.shape[1])

    decoder_sums = scatter(
        [
            pieces(head_columns_back(w_d_qkv.astype(BF16), parts)),
            pieces(w_d_out),
            pieces(w_c_query),
            pieces(w_c_pairs),
            pieces(w_c_out),
            pieces(w_d_up),
            pieces(w_d_down),
        ],
        "xyyxyyx",
        6,
    )
    small_grads = jnp.concatenate(
        [
            e_gain_one[None],
            e_gain_two[None],
            e_joined_sums[:, 0].reshape(1, D),
            e_joined_sums[:, 2].reshape(1, D),
            row_sum(ge_branch)[None],
            e_shift_one[None],
            row_sum(ge_hidden).reshape(4, D),
            row_sum(g_second_low)[None],
            e_shift_two[None],
            d_gain_one[None],
            d_gain_two[None],
            d_gain_three[None],
            d_joined_sums[:, 0].reshape(1, D),
            d_joined_sums[:, 2].reshape(1, D),
            row_sum(g_branch)[None],
            d_shift_one[None],
            row_sum(g_queries)[None],
            row_sum(g_pairs[:, D:])[None],
            row_sum(g_branch_cross)[None],
            d_shift_two[None],
            row_sum(g_hidden).reshape(4, D),
            row_sum(g_third)[None],
            d_shift_three[None],
        ],
        axis=0,
    )
    small_pieces = (
        small_grads.astype(BF16)
        .reshape(small_rows, devices, small_width)
        .transpose(1, 0, 2)
        .reshape(devices, small_rows * small_width)
    )
    encoder_sums = scatter(
        [
            pieces(head_columns_back(w_e_qkv.astype(BF16), parts)),
            pieces(w_e_out),
            pieces(w_e_up),
            pieces(w_e_down),
            pack_rows(small_pieces, D),
        ],
        "xyyxx",
        7,
    )
    small_sums = encoder_sums[4].reshape(-1)[: small_rows * small_width]
    small_sums = small_sums.reshape(small_rows, small_width)
    return (
        decoded.reshape(micro, tgt_rows, D),
        g_source.reshape(micro, src_rows, D),
        g_target.reshape(micro, tgt_rows, D),
        *encoder_sums[:4],
        small_sums[0:2],
        small_sums[2:12],
        *decoder_sums,
        small_sums[12:15],
        small_sums[15:29],
    )


def solution(mesh):
    in_specs = (
        P(None, ("seq", "head"), None),
        P(None, ("seq", "head"), None),
        P(None, ("seq", "head"), None),
        P(),
        P(),
        P(),
        P(("seq", "head"), None),
        P(("seq", "head"), None),
        P(("seq", "head"), None),
        P(("seq", "head"), None),
        P(None, ("seq", "head")),
        P(None, ("seq", "head")),
        P(("seq", "head"), None),
        P(("seq", "head"), None),
        P(("seq", "head"), None),
        P(("seq", "head"), None),
        P(("seq", "head"), None),
        P(("seq", "head"), None),
        P(("seq", "head"), None),
        P(None, ("seq", "head")),
        P(None, ("seq", "head")),
    )
    out_specs = (
        P(None, ("seq", "head"), None),
        P(None, ("seq", "head"), None),
        P(None, ("seq", "head"), None),
        P(("seq", "head"), None),
        P(("seq", "head"), None),
        P(("seq", "head"), None),
        P(("seq", "head"), None),
        P(None, ("seq", "head")),
        P(None, ("seq", "head")),
        P(("seq", "head"), None),
        P(("seq", "head"), None),
        P(("seq", "head"), None),
        P(("seq", "head"), None),
        P(("seq", "head"), None),
        P(("seq", "head"), None),
        P(("seq", "head"), None),
        P(None, ("seq", "head")),
        P(None, ("seq", "head")),
    )
    return jax.shard_map(shards, mesh=mesh, in_specs=in_specs, out_specs=out_specs, check_vma=False)
```

time: 2710 us -> 1040 us (0.38)
  waiting for transfers between devices: 1500 us -> 53.7 us
  Pallas kernels: 0 us -> 631 us
  blocking collectives: 317 us -> 0 us
  matrix products: 342 us -> 120 us
  other arithmetic: 143 us -> 22.8 us
  local copies, waits for them, and re-layouts: 227 us -> 161 us
  loops' own time: 63 us -> 0 us
  starting transfers between devices: 85.9 us -> 24.4 us
    reduce_scatter x9 -> x2, waiting for transfers between devices: 1090 us -> 0.04 us  [the longest x1 0.02 us: shards(): lax.psum_scatter(g_target_all.reshape(parts, micro * tgt_rows, D), 'head'...]
    pallas_call x0 -> x14, Pallas kernels: none -> 631 us  [the longest x4 245 us: scatter_sum(): pl.pallas_call(functools.partial(scatter_kernel, count, tuple(firsts)), o...]
    unnamed x27 -> x4, waiting for transfers between devices: 288 us -> 1.41 us
    dot_general x118 -> x35, matrix products: 342 us -> 120 us  [the longest x11 41 us: mm_rows(): lax.dot_general(left, right, (((0,), (0,)), ((), ())), preferred_element_...]
    psum x1 -> x0, blocking collectives: 161 us -> none  [shards(): fetched = lax.psum(picked, ('seq', 'head')).astype(jnp.bfloat16)]
    all_gather x4 -> x0, blocking collectives: 156 us -> none  [the longest x1 44.1 us: shards(): lax.all_gather(encoder_biases, ('seq', 'head'), axis=1, tiled=True)]
    another operation x32 -> x0, loops' own time: 63 us -> none  [the longest x2 15.6 us: self_forward(): lax.fori_loop(0, count, out_step, jnp.zeros(query.shape, jnp.float32))]
    all_to_all x16 -> x4, starting transfers between devices: 64.4 us -> 16 us  [the longest x2 8.37 us: to_tokens(): got = lax.all_to_all(value, 'head', split_axis=0, concat_axis=0, tiled=True)]
  transfers between devices with their start and end apart: 48 -> 12, of which waited for: 23 -> 5; matrix products, arithmetic and copies ran while one was open for 21% -> 18% of each run, Pallas kernels for 0% -> 44%
where the time goes in v1:
time: 1040 us; the launch traced here: 1030 us
  Pallas kernels  631 us (61%)
  local copies, waits for them, and re-layouts  161 us (15%)
  matrix products  120 us (12%)
  waiting for transfers between devices  53.7 us (5%)
  starting transfers between devices  24.4 us (2%)
  other arithmetic  22.8 us (2%)
  between operations  16 us (2%)
    pallas_call x4, Pallas kernels, scatter_sum(): pl.pallas_call(functools.partial(scatter_kernel, count, tuple(firsts)), o...  245 us
    pallas_call x4, Pallas kernels, gather_all(): pl.pallas_call(functools.partial(gather_kernel, count, tuple(firsts)), ou...  229 us
    pallas_call x2, Pallas kernels, attend_back(): pl.pallas_call(functools.partial(attend_back_kernel, heads, tile, causal,...  74.4 us
    unnamed x309, local copies, waits for them, and re-layouts  55 us
    pallas_call x2, Pallas kernels, attend(): pl.pallas_call(functools.partial(attend_kernel, heads, tile, causal), gri...  50.5 us
    dot_general x11, matrix products, mm_rows(): lax.dot_general(left, right, (((0,), (0,)), ((), ())), preferred_element_...  41 us
    dot_general x11, matrix products, mm(): return jnp.dot(left, right, preferred_element_type=F32)  40.6 us
    dot_general x11, matrix products, mm_back(): lax.dot_general(left, right, (((1,), (1,)), ((), ())), preferred_element_...  33.3 us
  transfers between devices with their start and end apart: 12, of which 5 were waited for; matrix products, arithmetic and copies ran while one was open for 18% of the time, Pallas kernels for 44%

profile of v1, /device:TPU:0, one launch (start us, length us, event | category | flops | bytes accessed | tf_op | source)
XLA Modules:
  0.0 1028.9 jit_solution(331663450538175017)
XLA Ops:
  10.2 78.0 %shard_map.341 = (bf16[32,24,2304]{2,1,0:T(8,128)(2,1)}, bf16[32,24,768]{2,1,0:T(8,128)(2,1)}, bf16[32,24,3072]{2,1,0:T(8,128)(2,1)}, bf16[32,96,768]{2,1,0:T(8,128)(2,1)}, bf16[32,8,768]{2,1,0:T(8,128)(2,1)}) custom-call(bf16[24,2304]{1,0:T(8,128)(2,1)} %refs_0_.3, bf16[24,768]{1,0:T(8,128)(2,1)} %refs_1_.3, bf16[24,3072]{1,0:T(8,128)(2,1)} %refs_2_.3, ...), custom_call_target="tpu_custom_call" | custom-call | tf_op jit(solution)/shard_map/pallas_call | solution.py:176
  93.1 97.3 %shard_map.340 = (bf16[32,24,2304]{2,1,0:T(8,128)(2,1)}, bf16[32,24,768]{2,1,0:T(8,128)(2,1)}, bf16[32,24,768]{2,1,0:T(8,128)(2,1)}, bf16[32,24,1536]{2,1,0:T(8,...) custom-call(bf16[24,2304]{1,0:T(8,128)(2,1)} %refs_0_.2, ...), custom_call_target="tpu_custom_call" | custom-call | tf_op jit(solution)/shard_map/pallas_call | solution.py:176
  205.5 4.3 collective-permute-start.1
  229.8 22.5 %attend.2 = bf16[4,2,128,192]{3,2,1,0:T(8,128)(2,1)S(1)} custom-call(s32[2,1536,2]{2,1,0:T(8,128)S(1)} %pad_add_fusion.refs_0_, s32[2,2,512]{2,1,0:T(2,128)S(1)} %pad_add_fusion.3.refs_1_, bf16[4,2,128,576]{3,2,1,0:T(8,128)(2,1)S(1)} %bitcast.207, bf16[4,2,128,384]{3,2,1,0:T(8,128)(2,1)S(1)} %copy-done.6, ...), custom_call_target="tpu_custom_call" | custom-call | flops 2415919104 | bytes 2359296 | tf_op jit(solution)/shard_map/attend/pallas_call | solution.py:453
  258.3 7.4 all-to-all-done
  268.9 5.4 fusion.5
  274.2 4.3 copy.114
  281.5 28.0 %attend.3 = bf16[4,2,256,192]{3,2,1,0:T(8,128)(2,1)S(1)} custom-call(s32[2,1024,2]{2,1,0:T(8,128)S(1)} %copy-done.3, s32[2,2,1024]{2,1,0:T(2,128)S(1)} %pad_add_fusion.2.refs_1_, bf16[4,2,256,576]{3,2,1,0:T(8,128)(2,1)S(1)} %bitcast.210), custom_call_target="tpu_custom_call" | custom-call | flops 3221225472 | bytes 4718592 | tf_op jit(solution)/shard_map/attend/pallas_call | solution.py:453
  310.8 4.5 all-to-all-start.1
  317.7 9.4 all-to-all-done.1
  330.7 7.3 multiply_convert_fusion.1
  345.0 40.3 %shard_map.342 = (bf16[32,768]{1,0:T(8,128)(2,1)}, bf16[32,768]{1,0:T(8,128)(2,1)}) custom-call(bf16[32,32,768]{2,1,0:T(8,128)(2,1)} %bitcast.224, bf16[32,32,768]{2,1,0:T(8,128)(2,1)} %bitcast.223), custom_call_target="tpu_custom_call" | custom-call | tf_op jit(solution)/shard_map/pallas_call | solution.py:350
  385.4 27.1 %shard_map.343 = (bf16[32,32,768]{2,1,0:T(8,128)(2,1)}, bf16[32,32,768]{2,1,0:T(8,128)(2,1)}) custom-call(bf16[32,768]{1,0:T(8,128)(2,1)} %get-tuple-element.63.refs_0_, bf16[32,768]{1,0:T(8,128)(2,1)} %get-tuple-element.64.refs_1_), custom_call_target="tpu_custom_call" | custom-call | tf_op jit(solution)/shard_map/pallas_call | solution.py:176
  412.4 9.4 add_convert_fusion
  421.8 9.0 cross.1
  446.1 23.0 %cross_back.1 = (bf16[2,128,768]{2,1,0:T(8,128)(2,1)S(1)}, bf16[2,1024,1536]{2,1,0:T(8,128)(2,1)}) custom-call(bf16[2,128,768]{2,1,0:T(8,128)(2,1)S(1)} %bitcast.215, bf16[2,1024,1536]{2,1,0:T(8,128)(2,1)} %bitcast.222, bf16[2,128,768]{2,1,0:T(8,128)(2,1)S(1)} %bitcast.216), custom_call_target="tpu_custom_call" | custom-call | flops 4026531840 | bytes 12582912 | tf_op jit(solution)/shard_map/cross_back/pallas_call | solution.py:621
  475.4 5.3 convolution_convert_fusion.6
  482.5 27.1 %shard_map.344 = (bf16[32,768]{1,0:T(8,128)(2,1)}, bf16[32,768]{1,0:T(8,128)(2,1)}) custom-call(bf16[32,32,768]{2,1,0:T(8,128)(2,1)} %bitcast.226, bf16[32,32,768]{2,1,0:T(8,128)(2,1)} %bitcast.225), custom_call_target="tpu_custom_call" | custom-call | tf_op jit(solution)/shard_map/pallas_call | solution.py:350
  509.7 26.8 %shard_map.345 = (bf16[32,32,768]{2,1,0:T(8,128)(2,1)}, bf16[32,32,768]{2,1,0:T(8,128)(2,1)}) custom-call(bf16[32,768]{1,0:T(8,128)(2,1)} %get-tuple-element.72.refs_0_, bf16[32,768]{1,0:T(8,128)(2,1)} %get-tuple-element.73.refs_1_), custom_call_target="tpu_custom_call" | custom-call | tf_op jit(solution)/shard_map/pallas_call | solution.py:176
  541.4 8.6 fusion.74
  571.7 5.1 all-to-all-done.3
  582.4 34.1 %attend_back.3 = (f32[4,2,128,576]{3,2,1,0:T(8,128)}, bf16[4,2,128,384]{3,2,1,0:T(8,128)(2,1)S(1)}, bf16[4,2,128,384]{3,2,1,0:T(8,128)(2,1)S(1)}) custom-call(s32[2,1536,2]{2,1,0:T(8,128)} %copy-done.1, s32[2,2,512]{2,1,0:T(2,128)S(1)} %pad_add_fusion.3.refs_1_, bf16[4,2,128,576]{3,2,1,0:T(8,128)(2,1)S(1)} %bitcast.208, ...), custom_call_target="tpu_custom_call" | custom-call | flops 6039797760 | bytes 3538944 | tf_op jit(solution)/shard_map/attend_back/pallas_call | solution.py:521
  625.4 12.9 %collective-permute-done.3 = bf16[4,2,128,384]{3,2,1,0:T(8,128)(2,1)S(1)} collective-permute-done((bf16[4,2,128,384]{3,2,1,0:T(8,128)(2,1)S(1)}, bf16[4,2,128,384]{3,2,1,0:T(8,128)(2,1)S(1)}, u32[]{:S(2)}, u32[]{:S(2)}) %collective-permute-start.3) | collective-permute-done | bytes 786464 | tf_op jit(solution)/shard_map/ppermute | solution.py:747
  638.3 17.5 %collective-permute-done.2 = bf16[4,2,128,384]{3,2,1,0:T(8,128)(2,1)S(1)} collective-permute-done((bf16[4,2,128,384]{3,2,1,0:T(8,128)(2,1)S(1)}, bf16[4,2,128,384]{3,2,1,0:T(8,128)(2,1)S(1)}, u32[]{:S(2)}, u32[]{:S(2)}) %collective-permute-start.2) | collective-permute-done | bytes 786464 | tf_op jit(solution)/shard_map/ppermute | solution.py:747
  666.7 5.3 convolution_convert_fusion.3
  683.9 7.2 convolution_convert_fusion.2
  695.7 40.2 %attend_back.2 = bf16[4,2,256,576]{3,2,1,0:T(8,128)(2,1)S(1)} custom-call(s32[2,1024,2]{2,1,0:T(8,128)S(1)} %copy-done.4, s32[2,2,1024]{2,1,0:T(2,128)S(1)} %pad_add_fusion.2.refs_1_, bf16[4,2,256,576]{3,2,1,0:T(8,128)(2,1)} %bitcast.209, bf16[4,2,256,192]{3,2,1,0:T(8,128)(2,1)S(1)} %copy-done.2), custom_call_target="tpu_custom_call" | custom-call | flops 8053063680 | bytes 7077888 | tf_op jit(solution)/shard_map/attend_back/pallas_call | solution.py:521
  740.2 9.4 convolution_convert_fusion.4
  754.0 12.2 %dynamic_update_slice.12 = bf16[768,2304]{1,0:T(8,128)(2,1)S(1)} dynamic-update-slice(bf16[768,2304]{1,0:T(8,128)(2,1)S(1)} %broadcast.302.clone, bf16[768,576]{1,0:T(8,128)(2,1)} %copy.130, s32[]{:T(128)} %constant.28.clone.1, s32[]{:T(128)S(6)} %select_n.11) | dynamic-update-slice | bytes 1769476 | tf_op jit(solution)/shard_map/dynamic_update_slice | solution.py:719
  810.4 77.7 %shard_map.346 = (f32[24,2304]{1,0:T(8,128)}, f32[24,768]{1,0:T(8,128)}, f32[24,3072]{1,0:T(8,128)}, f32[96,768]{1,0:T(8,128)}, f32[8,768]{1,0:T(8,128)}) custom-call(bf16[32,24,2304]{2,1,0:T(8,128)(2,1)} %bitcast.219, bf16[32,24,768]{2,1,0:T(8,128)(2,1)} %bitcast.227, bf16[32,24,3072]{2,1,0:T(8,128)(2,1)} %bitcast.231, bf16[32,96,768]{2,1,0:T(8,128)(2,1)} %bitcast.232, ...), custom_call_target="tpu_custom_call" | custom-call | tf_op jit(solution)/shard_map/pallas_call | solution.py:350
  896.0 12.2 %dynamic_update_slice.15 = bf16[768,2304]{1,0:T(8,128)(2,1)S(1)} dynamic-update-slice(bf16[768,2304]{1,0:T(8,128)(2,1)S(1)} %broadcast.302.clone.1, bf16[768,576]{1,0:T(8,128)(2,1)} %copy.134, s32[]{:T(128)} %constant.28.clone.1, s32[]{:T(128)S(6)} %select_n.11) | dynamic-update-slice | bytes 1769476 | tf_op jit(solution)/shard_map/dynamic_update_slice | solution.py:719
  909.9 99.9 %shard_map.347 = (f32[24,2304]{1,0:T(8,128)}, f32[24,768]{1,0:T(8,128)}, f32[24,768]{1,0:T(8,128)}, f32[24,1536]{1,0:T(8,128)}, f32[24,768]{1,0:T(8,128)}, /*index=5*/f32[24,3072]{1,0:T(8,128)}, f32[96,768]{1,0:T(8,128)}) custom-call(bf16[32,24,2304]{2,1,0:T(8,128)(2,1)} %bitcast.220, bf16[32,24,768]{2,1,0:T(8,128)(2,1)} %bitcast.228, ...), custom_call_target="tpu_custom_call" | custom-call | tf_op jit(solution)/shard_map/pallas_call | solution.py:350
  (573 shorter events, 234.1 us)
Async XLA Ops:
  7.2 190.8 %all-gather.5.cloned.1.call-start = ((), (), s32[]{:S(2)}) async-start(), calls=%async_computation.8 | async-start | bytes 1966080 | tf_op jit(solution)/shard_map/all_gather | solution.py:789
  7.9 260.9 %all-gather.7.cloned.1.call-start = ((), (), s32[]{:S(2)}) async-start(), calls=%async_computation.9 | async-start | bytes 3932160 | tf_op jit(solution)/shard_map/all_gather | solution.py:788
  204.2 23.6 %collective-permute-start = (bf16[4,2,128,384]{3,2,1,0:T(8,128)(2,1)}, bf16[4,2,128,384]{3,2,1,0:T(8,128)(2,1)S(1)}, u32[]{:S(2)}, u32[]{:S(2)}) collective-permute-start(bf16[4,2,128,384]{3,2,1,0:T(8,128)(2,1)} %slice.313), channel_id=1, source_target_pairs={{0,8},{4,12},{8,16},{12,20},{16,24},{20,28},{1,9},{5,13},{9,17},{1... | collective-permute-start | bytes 2359304 | tf_op jit(solution)/shard_map/ppermute | solution.py:742
  205.5 23.2 %collective-permute-start.1 = (bf16[4,2,128,384]{3,2,1,0:T(8,128)(2,1)}, bf16[4,2,128,384]{3,2,1,0:T(8,128)(2,1)}, u32[]{:S(2)}, u32[]{:S(2)}) collective-permute-start(bf16[4,2,128,384]{3,2,1,0:T(8,128)(2,1)} %slice.313), channel_id=1, source_target_pairs={{0,4},{4,8},{8,12},{12,16},{16,20},{20,24},{24,28},{1,5},{5,9},{9,... | collective-permute-start | bytes 2359304 | tf_op jit(solution)/shard_map/ppermute | solution.py:742
  212.8 56.1 %copy-start.49 = (bf16[768,3,1,64]{0,3,2,1:T(8,128)(2,1)}, bf16[768,3,1,64]{0,3,2,1:T(8,128)(2,1)S(1)}, u32[]{:S(2)}) copy-start(bf16[768,3,1,64]{0,3,2,1:T(8,128)(2,1)S(1)} %slice.319) | copy-start | bytes 884740
  224.4 113.6 %copy-start.106 = (f32[768]{0:T(1024)}, f32[768]{0:T(1024)S(1)}, u32[]{:S(2)}) copy-start(f32[768]{0:T(1024)S(1)} %add.381) | copy-start | bytes 9220
  224.5 329.2 %copy-start.93 = (f32[768]{0:T(1024)}, f32[768]{0:T(1024)S(1)}, u32[]{:S(2)}) copy-start(f32[768]{0:T(1024)S(1)} %mul.353) | copy-start | bytes 9220
  224.8 211.2 %copy-start.63 = (f32[768]{0:T(1024)}, f32[768]{0:T(1024)S(1)}, u32[]{:S(2)}) copy-start(f32[768]{0:T(1024)S(1)} %add.403) | copy-start | bytes 9220
  224.9 219.8 %copy-start.60 = (f32[768]{0:T(1024)}, f32[768]{0:T(1024)S(1)}, u32[]{:S(2)}) copy-start(f32[768]{0:T(1024)S(1)} %mul.368) | copy-start | bytes 9220
  253.5 12.6 %copy-start.48 = (bf16[2,128,768]{2,1,0:T(8,128)(2,1)S(1)}, bf16[2,128,768]{2,1,0:T(8,128)(2,1)}, u32[]{:S(2)}) copy-start(bf16[2,128,768]{2,1,0:T(8,128)(2,1)} %param.22) | copy-start | bytes 1179652
  253.5 12.6 %copy-start.113 = (f32[768]{0:T(1024)S(1)}, f32[768]{0:T(1024)}, u32[]{:S(2)}) copy-start(f32[768]{0:T(1024)} %add.358) | copy-start | bytes 9220
  254.4 11.3 %all-to-all-start = ((bf16[4,2,128,192]{2,3,1,0:T(8,128)(2,1)}), bf16[4,2,128,192]{2,3,1,0:T(8,128)(2,1)S(1)}, u32[]{:S(2)}, u32[]{:S(2)}) async-start(bf16[4,2,128,192]{2,3,1,0:T(8,128)(2,1)} %copy.110), calls=%async_computation | async-start | bytes 786432 | tf_op jit(solution)/shard_map/all_to_all | solution.py:730
  310.8 16.2 %all-to-all-start.1 = ((bf16[4,2,256,192]{2,3,1,0:T(8,128)(2,1)}), bf16[4,2,256,192]{2,3,1,0:T(8,128)(2,1)}, u32[]{:S(2)}, u32[]{:S(2)}) async-start(bf16[4,2,256,192]{2,3,1,0:T(8,128)(2,1)} %copy.116), calls=%async_computation.1 | async-start | bytes 1572864 | tf_op jit(solution)/shard_map/all_to_all | solution.py:730
  431.5 13.3 %copy-start.20 = (f32[256,768]{1,0:T(8,128)}, f32[256,768]{1,0:T(8,128)S(1)}, u32[]{:S(2)}) copy-start(f32[256,768]{1,0:T(8,128)S(1)} %get-tuple-element.165) | copy-start | bytes 2359300
  445.6 23.5 %copy-start.16 = (f32[256,768]{1,0:T(8,128)}, f32[256,768]{1,0:T(8,128)S(1)}, u32[]{:S(2)}) copy-start(f32[256,768]{1,0:T(8,128)S(1)} %get-tuple-element.138) | copy-start | bytes 2359300
  446.1 23.0 %copy-start.40 = (bf16[32,24,768]{2,1,0:T(8,128)(2,1)S(1)}, bf16[32,24,768]{2,1,0:T(8,128)(2,1)}, u32[]{:S(2)}) copy-start(bf16[32,24,768]{2,1,0:T(8,128)(2,1)} %get-tuple-element.58) | copy-start | bytes 3538948
  565.6 11.2 %all-to-all-start.3 = ((bf16[4,2,128,192]{2,3,1,0:T(8,128)(2,1)}), bf16[4,2,128,192]{2,3,1,0:T(8,128)(2,1)S(1)}, u32[]{:S(2)}, u32[]{:S(2)}) async-start(bf16[4,2,128,192]{2,3,1,0:T(8,128)(2,1)} %copy.126), calls=%async_computation.4 | async-start | bytes 786432 | tf_op jit(solution)/shard_map/all_to_all | solution.py:737
  576.8 114.2 %all-to-all-start.2 = ((bf16[4,2,256,192]{2,3,1,0:T(8,128)(2,1)}), bf16[4,2,256,192]{2,3,1,0:T(8,128)(2,1)}, u32[]{:S(2)}, u32[]{:S(2)}) async-start(bf16[4,2,256,192]{2,3,1,0:T(8,128)(2,1)} %copy.122), calls=%async_computation.2 | async-start | bytes 1572864 | tf_op jit(solution)/shard_map/all_to_all | solution.py:737
  581.0 428.8 %reduce-scatter.5.cloned.1.call-start = ((), (), s32[]{:S(2)}) async-start(), calls=%async_computation.7 | async-start | bytes 1966080 | tf_op jit(solution)/shard_map/reduce_scatter | solution.py:907
  582.4 37.3 %copy-start.12 = (f32[512,768]{1,0:T(8,128)S(1)}, f32[512,768]{1,0:T(8,128)}, u32[]{:S(2)}) copy-start(f32[512,768]{1,0:T(8,128)} %copy-done.11) | copy-start | bytes 4718596
  582.4 37.3 %copy-start.32 = (bf16[96,8,2,256]{3,1,2,0:T(8,128)(2,1)S(1)}, bf16[96,8,2,256]{3,1,2,0:T(8,128)(2,1)}, u32[]{:S(2)}) copy-start(bf16[96,8,2,256]{3,1,2,0:T(8,128)(2,1)} %copy-done.31) | copy-start | bytes 2359300
  616.6 21.8 %collective-permute-start.3 = (bf16[4,2,128,384]{3,2,1,0:T(8,128)(2,1)S(1)}, bf16[4,2,128,384]{3,2,1,0:T(8,128)(2,1)S(1)}, u32[]{:S(2)}, u32[]{:S(2)}) collective-permute-start(bf16[4,2,128,384]{3,2,1,0:T(8,128)(2,1)S(1)} %get-tuple-element.79), channel_id=1, source_target_pairs={{4,0},{8,4},{12,8},{16,12},{20,16},{24,20},{28,24},{5,1},{9,5},{13... | collective-permute-start | bytes 2359304 | tf_op jit(solution)/shard_map/ppermute | solution.py:747
  617.8 37.9 %collective-permute-start.2 = (bf16[4,2,128,384]{3,2,1,0:T(8,128)(2,1)S(1)}, bf16[4,2,128,384]{3,2,1,0:T(8,128)(2,1)S(1)}, u32[]{:S(2)}, u32[]{:S(2)}) collective-permute-start(bf16[4,2,128,384]{3,2,1,0:T(8,128)(2,1)S(1)} %get-tuple-element.78), channel_id=1, source_target_pairs={{8,0},{12,4},{16,8},{20,12},{24,16},{28,20},{9,1},{13,5},{17,9},{2... | collective-permute-start | bytes 2359304 | tf_op jit(solution)/shard_map/ppermute | solution.py:747
  625.4 34.7 %copy-start.28 = (bf16[4,2,128,192]{3,2,1,0:T(8,128)(2,1)}, bf16[4,2,128,192]{3,2,1,0:T(8,128)(2,1)S(1)}, u32[]{:S(2)}) copy-start(bf16[4,2,128,192]{3,2,1,0:T(8,128)(2,1)S(1)} %slice.396) | copy-start | bytes 1179652
  660.1 352.1 %reduce-scatter.3.cloned.1.call-start = ((), (), s32[]{:S(2)}) async-start(), calls=%async_computation.6 | async-start | bytes 3932160 | tf_op jit(solution)/shard_map/reduce_scatter | solution.py:933
  666.7 12.2 %copy-start.100 = (bf16[768]{0:T(1024)(128)(2,1)S(1)}, bf16[768]{0:T(1024)(128)(2,1)}, u32[]{:S(2)}) copy-start(bf16[768]{0:T(1024)(128)(2,1)} %get-tuple-element.109) | copy-start | bytes 4612
  666.7 14.4 %copy-start.102 = (bf16[768]{0:T(1024)(128)(2,1)S(1)}, bf16[768]{0:T(1024)(128)(2,1)}, u32[]{:S(2)}) copy-start(bf16[768]{0:T(1024)(128)(2,1)} %get-tuple-element.137) | copy-start | bytes 4612
  666.7 15.1 %copy-start.114 = (bf16[768]{0:T(1024)(128)(2,1)S(1)}, bf16[768]{0:T(1024)(128)(2,1)}, u32[]{:S(2)}) copy-start(bf16[768]{0:T(1024)(128)(2,1)} %get-tuple-element.108) | copy-start | bytes 4612
  666.7 15.7 %copy-start.104 = (bf16[3072]{0:T(1024)(128)(2,1)S(1)}, bf16[3072]{0:T(1024)(128)(2,1)}, u32[]{:S(2)}) copy-start(bf16[3072]{0:T(1024)(128)(2,1)} %get-tuple-element.176) | copy-start | bytes 18436
  695.7 40.3 %copy-start.45 = (bf16[768,3,2,64]{0,3,2,1:T(8,128)(2,1)S(1)}, bf16[768,3,2,64]{0,3,2,1:T(8,128)(2,1)}, u32[]{:S(2)}) copy-start(bf16[768,3,2,64]{0,3,2,1:T(8,128)(2,1)} %slice.318) | copy-start | bytes 1769476
  695.7 40.3 %copy-start.50 = (bf16[768,3,1,64]{0,3,2,1:T(8,128)(2,1)S(1)}, bf16[768,3,1,64]{0,3,2,1:T(8,128)(2,1)}, u32[]{:S(2)}) copy-start(bf16[768,3,1,64]{0,3,2,1:T(8,128)(2,1)} %copy-done.49) | copy-start | bytes 884740
  766.3 44.1 %copy-start.10 = (bf16[768,2304]{1,0:T(8,128)(2,1)}, bf16[768,2304]{1,0:T(8,128)(2,1)S(1)}, u32[]{:S(2)}) copy-start(bf16[768,2304]{1,0:T(8,128)(2,1)S(1)} %dynamic_update_slice.12) | copy-start | bytes 10616836
  (115 other events, 540.6 us)
Sparse Core Ops, SparseCore 0:
  9.6 30.1 all-gather.4
  41.4 38.6 all-gather.6
  660.2 26.1 reduce-scatter.4
  740.3 35.9 reduce-scatter.2

commit v2 on v1

v2 whole, which is shorter than its diff:
```python
import functools

import jax
import jax.numpy as jnp
from jax import lax
from jax.experimental import pallas as pl
from jax.experimental.pallas import tpu as pltpu
from jax.sharding import PartitionSpec as P

D = 768
HEADS = 12
HEAD_DIM = 64
FF = 3072
MICRO = 2
STRETCH = 1024
REACH = 2
EVERY = ("seq", "head")

EPSILON = 1e-05
NEGATIVE = -1e30
MESH = pl.DeviceIdType.MESH
F32 = jnp.float32
BF16 = jnp.bfloat16


def place():
    seq, head = lax.axis_index("seq"), lax.axis_index("head")
    return seq // 2, seq % 2, head // 2, head % 2


def device(z, y, x, c):
    return (z * 2 + y, x * 2 + c)


def shard(z, y, x, c):
    return ((z * 2 + y) * 2 + x) * 2 + c


def greet(z, y, x, c):
    barrier = pltpu.get_barrier_semaphore()
    def tell(who):
        pl.semaphore_signal(barrier, inc=1, device_id=who, device_id_type=MESH)
    tell(device(z, y, x, 1 - c))
    tell(device(z, y, 1 - x, c))
    tell(device(z, 1 - y, x, c))
    @pl.when(z > 0)
    def _():
        tell(device(z - 1, y, x, c))
    @pl.when(z < 3)
    def _():
        tell(device(z + 1, y, x, c))
    pl.semaphore_wait(barrier, 3 + (z + 2) // 3 + (5 - z) // 3)


def gather_kernel(count, shared, orders, *refs):
    every = count + shared
    ins, outs = refs[:every], refs[every : 2 * every]
    own_sem, recv_sem, send_sem, group_recv, group_send = refs[2 * every :]
    z, y, x, c = place()
    greet(z, y, x, c)
    here = [(x, y) if order in "xX" else (y, x) for order in orders]

    def shard_of(a, zo, f, l):
        return shard(zo, l, f, c) if orders[a] in "xX" else shard(zo, f, l, c)

    def holder(a, zo, f, l, cc):
        return device(zo, l, f, cc) if orders[a] in "xX" else device(zo, f, l, cc)

    def copy(a, src, where, who, kind):
        return pltpu.make_async_remote_copy(
            src_ref=src,
            dst_ref=outs[a].at[where],
            send_sem=send_sem.at[a, kind, where // 2],
            recv_sem=recv_sem.at[a, where],
            device_id=who,
            device_id_type=MESH,
        )

    def forward(a, src, where, first, up, down):
        f, l = here[a]
        if first:
            copy(a, src, where, holder(a, z, 1 - f, l, c), 0).start()
        if up:

            @pl.when(z < 3)
            def _():
                copy(a, src, where, holder(a, z + 1, f, l, c), 1).start()

        if down:

            @pl.when(z > 0)
            def _():
                copy(a, src, where, holder(a, z - 1, f, l, c), 2).start()

        copy(a, src, where, holder(a, z, f, 1 - l, c), 3).start()
        copy(a, src, where, holder(a, z, f, l, 1 - c), 4).start()

    def arrived(a, where):
        copy(a, outs[a].at[where], where, device(z, y, x, 1 - c), 0).wait_recv()

    def pass_on(a, zo, fo, first, up, down):
        where = shard_of(a, zo, fo, here[a][1])
        arrived(a, where)
        forward(a, outs[a].at[where], where, first, up, down)

    def from_last(zo, other):
        for a in range(count):
            f, l = here[a]
            where = shard_of(a, zo, 1 - f if other else f, 1 - l)
            arrived(a, where)
            copy(a, outs[a].at[where], where, holder(a, z, f, l, 1 - c), 4).start()

    def group_copy(b, src, xo, co, kind, who):
        return pltpu.make_async_remote_copy(
            src_ref=src,
            dst_ref=outs[count + b].at[xo * 2 + co],
            send_sem=group_send.at[b, kind],
            recv_sem=group_recv.at[b, xo * 2 + co],
            device_id=who,
            device_id_type=MESH,
        )

    over, beside = device(z, y, 1 - x, c), device(z, y, x, 1 - c)
    kept = []
    for b in range(shared):
        group_copy(b, ins[count + b], x, c, 0, over).start()
        group_copy(b, ins[count + b], x, c, 1, beside).start()
        kept.append(
            pltpu.make_async_copy(
                ins[count + b], outs[count + b].at[x * 2 + c], own_sem.at[count + b]
            )
        )
        kept[-1].start()
    for a in range(count):
        me = shard_of(a, z, *here[a])
        forward(a, ins[a], me, True, True, True)
        kept.append(pltpu.make_async_copy(ins[a], outs[a].at[me], own_sem.at[a]))
        kept[-1].start()
    for a in range(count):
        early = orders[a] in "XY"
        pass_on(a, z, 1 - here[a][0], False, not early, not early)
    from_last(z, False)
    from_last(z, True)
    for b in range(shared):
        landed = outs[count + b].at[(1 - x) * 2 + c]
        group_copy(b, landed, 1 - x, c, 2, beside).wait_recv()
        group_copy(b, landed, 1 - x, c, 2, beside).start()
    for distance in (1, 2, 3):
        for below in (True, False):

            @pl.when((z >= distance) if below else (z + distance <= 3))
            def _():
                zo = z - distance if below else z + distance
                for a in range(count):
                    early = orders[a] in "XY"
                    pass_on(a, zo, here[a][0], early, below, not below)
                    if not early:
                        pass_on(a, zo, 1 - here[a][0], False, below, not below)

        for below in (True, False):

            @pl.when((z >= distance) if below else (z + distance <= 3))
            def _():
                zo = z - distance if below else z + distance
                for a in range(count):
                    if orders[a] in "XY":
                        pass_on(a, zo, 1 - here[a][0], False, False, False)
                from_last(zo, False)
                from_last(zo, True)

    def sent(a, where, kind):
        copy(a, ins[a], where, device(z, y, x, 1 - c), kind).wait_send()

    def cores(i, carry):
        for a in range(count):
            arrived(a, i * 2 + 1 - c)
            sent(a, i * 2 + c, 4)
        return carry

    lax.fori_loop(0, 16, cores, 0)
    for b in range(shared):
        first, landed = ins[count + b], outs[count + b].at[(1 - x) * 2 + c]
        group_copy(b, first, x, 1 - c, 1, beside).wait_recv()
        group_copy(b, first, 1 - x, 1 - c, 1, beside).wait_recv()
        group_copy(b, first, x, c, 0, over).wait_send()
        group_copy(b, first, x, c, 1, beside).wait_send()
        group_copy(b, landed, 1 - x, c, 2, beside).wait_send()
    for copied in kept:
        copied.wait()
    for a in range(count):
        f, l = here[a]
        early = orders[a] in "XY"
        if not early:
            sent(a, shard_of(a, z, f, l), 0)
        for zo in range(4):
            if early:
                sent(a, shard_of(a, zo, f, l), 0)
            for fo in range(2):
                sent(a, shard_of(a, zo, fo, l), 3)
            for fo in [f] if early else [0, 1]:

                @pl.when((zo <= z) & (z < 3))
                def _():
                    sent(a, shard_of(a, zo, fo, l), 1)

                @pl.when((zo >= z) & (z > 0))
                def _():
                    sent(a, shard_of(a, zo, fo, l), 2)


def traffic(arrays, share):
    size = sum(v.size * v.dtype.itemsize for v in arrays)
    return pl.CostEstimate(flops=0, transcendentals=0, bytes_accessed=size * share)


def gather_all(arrays, orders, collective_id, group_arrays=()):
    count, shared = len(arrays), len(group_arrays)
    every = [*arrays, *group_arrays]
    copies = [32] * count + [4] * shared
    D = pltpu.SemaphoreType.DMA
    return pl.pallas_call(
        functools.partial(gather_kernel, count, shared, orders),
        out_shape=[jax.ShapeDtypeStruct((n,) + v.shape, v.dtype) for n, v in zip(copies, every)],
        in_specs=[pl.BlockSpec(memory_space=pl.ANY)] * len(every),
        out_specs=[pl.BlockSpec(memory_space=pl.ANY)] * len(every),
        scratch_shapes=[
            D((len(every),)),
            D((count, 32)),
            D((count, 5, 16)),
            D((max(shared, 1), 4)),
            D((max(shared, 1), 3)),
        ],
        compiler_params=pltpu.CompilerParams(collective_id=collective_id, has_side_effects=True),
        cost_estimate=traffic(arrays, 500),
        name="gather_all",
    )(*every)


def scatter_kernel(count, shared, orders, *refs):
    every = count + shared
    grads, outs, refs = refs[:every], refs[every : 2 * every], refs[2 * every :]
    held, mine, near, mid, right, left = [refs[k * count : (k + 1) * count] for k in range(6)]
    refs = refs[6 * count :]
    mine_sem, core_sem, near_sem, mid_sem, right_sem, left_sem, group_sem, refs = (
        *refs[:7],
        refs[7:],
    )
    group_held, group_mine, group_last = [refs[k * shared : (k + 1) * shared] for k in range(3)]
    z, y, x, c = place()
    greet(z, y, x, c)
    half = z // 2
    here = [(x, y) if order in "xX" else (y, x) for order in orders]
    late = [order in "XY" for order in orders]

    def block(a, zt, f, l):
        return (zt * 2 + l) * 2 + f if orders[a] in "xX" else (zt * 2 + f) * 2 + l

    def remote(a, src, dst, sems, slot, who):
        return pltpu.make_async_remote_copy(
            src_ref=src,
            dst_ref=dst,
            send_sem=sems.at[a, 0, slot],
            recv_sem=sems.at[a, 1, slot],
            device_id=who,
            device_id_type=MESH,
        )

    def core_copy(a, q):
        who = device(z, y, x, 1 - c)
        return remote(a, grads[a].at[q * 2 + 1 - c], held[a].at[q], core_sem, q, who)

    def mine_copy(a, q):
        return pltpu.make_async_copy(grads[a].at[q * 2 + c], mine[a].at[q], mine_sem.at[a, q])

    def along(a, first):
        flip_x = (orders[a] in "xX") == first
        return device(z, y, 1 - x, c) if flip_x else device(z, 1 - y, x, c)

    def near_copy(a, q, slot):
        return remote(a, held[a].at[q], near[a].at[slot], near_sem, slot, along(a, True))

    def mid_copy(a, q, slot):
        return remote(a, held[a].at[q], mid[a].at[slot], mid_sem, slot, along(a, False))

    def right_copy(a, q, slot):
        return remote(a, held[a].at[q], right[a].at[slot], right_sem, slot, device(z + 1, y, x, c))

    def left_copy(a, q, slot):
        return remote(a, held[a].at[q], left[a].at[slot], left_sem, slot, device(z - 1, y, x, c))

    def far(k):
        return 3 - k + half * (2 * k - 3)

    def others(k):
        down = 3 - k - (k // 2) * z
        up = k + (k // 2) * (3 - z)
        return down + half * (up - down)

    def add(a, q, *terms):
        total = held[a][q].astype(F32)
        for ref, slot in terms:
            total = total + ref[slot].astype(F32)
        held[a][q] = total.astype(BF16)

    for side in (True, False):

        def start(i, carry, side=side):
            for a in range(count):
                f = here[a][0]
                q = block(a, far(i // 2), 1 - f if side else f, i % 2)
                core_copy(a, q).start()
                mine_copy(a, q).start()
            return carry

        lax.fori_loop(0, 8, start, 0)

    def group_copy(b, kind):
        if kind < 2:
            xt = 1 - x if kind == 0 else x
            return pltpu.make_async_remote_copy(
                src_ref=grads[count + b].at[xt * 2 + 1 - c],
                dst_ref=group_held[b].at[kind],
                send_sem=group_sem.at[b, 0, kind],
                recv_sem=group_sem.at[b, 1, kind],
                device_id=device(z, y, x, 1 - c),
                device_id_type=MESH,
            )
        if kind < 4:
            xt = 1 - x if kind == 2 else x
            return pltpu.make_async_copy(
                grads[count + b].at[xt * 2 + c], group_mine[b].at[kind - 2], group_sem.at[b, 0, kind]
            )
        return pltpu.make_async_remote_copy(
            src_ref=group_held[b].at[0],
            dst_ref=group_last[b],
            send_sem=group_sem.at[b, 0, 4],
            recv_sem=group_sem.at[b, 1, 4],
            device_id=device(z, y, 1 - x, c),
            device_id_type=MESH,
        )

    def in_pieces(rows, step):
        piece = rows // 8

        def body(i, carry):
            step(pl.ds(pl.multiple_of(i * piece, piece), piece))
            return carry

        lax.fori_loop(0, 8, body, 0)

    for b in range(shared):
        for kind in range(4):
            group_copy(b, kind).start()

    def first_step(i, carry):
        zt, lt = far(i // 2), i % 2
        for a in range(count):
            q = block(a, zt, 1 - here[a][0], lt)
            core_copy(a, q).wait_recv()
            mine_copy(a, q).wait()
            add(a, q, (mine[a], q))
            near_copy(a, q, zt * 2 + lt).start()
        return carry

    lax.fori_loop(0, 8, first_step, 0)
    for b in range(shared):
        group_copy(b, 0).wait_recv()
        group_copy(b, 2).wait()

        def to_other(cut, b=b):
            total = group_held[b][0, cut, :].astype(F32) + group_mine[b][0, cut, :].astype(F32)
            group_held[b][0, cut, :] = total.astype(BF16)

        in_pieces(group_last[b].shape[0], to_other)
        group_copy(b, 4).start()

    def summed(a, zt, lt):
        q = block(a, zt, here[a][0], lt)
        core_copy(a, q).wait_recv()
        mine_copy(a, q).wait()
        near_copy(a, q, zt * 2 + lt).wait_recv()
        add(a, q, (mine[a], q), (near[a], zt * 2 + lt))
        return q

    if any(late):

        def mid_step(i, carry):
            zt = far(i)
            for a in range(count):
                if late[a]:
                    mid_copy(a, summed(a, zt, 1 - here[a][1]), zt).start()
            return carry

        lax.fori_loop(0, 4, mid_step, 0)

    def slots(a, zt, lt):
        return (zt - 1, zt) if late[a] else ((zt - 1) * 2 + lt, zt * 2 + lt)

    def along_z(a, zt, lt):
        q = summed(a, zt, lt)
        if late[a]:
            mid_copy(a, q, zt).wait_recv()
            add(a, q, (mid[a], zt))
        up, down = slots(a, zt, lt)

        @pl.when(zt > z)
        def _():
            @pl.when(z > 0)
            def _():
                right_copy(a, q, up).wait_recv()
                add(a, q, (right[a], up))

            right_copy(a, q, up).start()

        @pl.when(zt < z)
        def _():
            @pl.when(z < 3)
            def _():
                left_copy(a, q, down).wait_recv()
                add(a, q, (left[a], down))

            left_copy(a, q, down).start()

    def z_step(k, carry):
        for a in range(count):
            if late[a]:
                along_z(a, others(k), here[a][1])
            else:
                along_z(a, others(k), 0)
                along_z(a, others(k), 1)
        return carry

    lax.fori_loop(0, 3, z_step, 0)

    def from_z(a, q, lt):
        up, down = slots(a, z, lt)

        @pl.when(z > 0)
        def _():
            right_copy(a, q, up).wait_recv()
            add(a, q, (right[a], up))

        @pl.when(z < 3)
        def _():
            left_copy(a, q, down).wait_recv()
            add(a, q, (left[a], down))

    for a in range(count):
        if not late[a]:
            lt = 1 - here[a][1]
            q = summed(a, z, lt)
            from_z(a, q, lt)
            mid_copy(a, q, 0).start()
    for a in range(count):
        lt = here[a][1]
        q = summed(a, z, lt)
        if late[a]:
            mid_copy(a, q, z).wait_recv()
            add(a, q, (mid[a], z))
        from_z(a, q, lt)
    for a in range(count):
        q = block(a, z, *here[a])
        total = held[a][q].astype(F32)
        if not late[a]:
            mid_copy(a, q, 0).wait_recv()
            total = total + mid[a][0].astype(F32)
        outs[a][...] = total.astype(outs[a].dtype)

    for b in range(shared):
        group_copy(b, 1).wait_recv()
        group_copy(b, 3).wait()
        group_copy(b, 4).wait_recv()

        def at_home(cut, b=b):
            total = group_held[b][1, cut, :].astype(F32) + group_mine[b][1, cut, :].astype(F32)
            outs[count + b][cut, :] = total + group_last[b][cut, :].astype(F32)

        in_pieces(group_last[b].shape[0], at_home)
        for kind in (0, 1, 4):
            group_copy(b, kind).wait_send()

    def sent_core(i, carry):
        for a in range(count):
            core_copy(a, i).wait_send()
        return carry

    lax.fori_loop(0, 16, sent_core, 0)

    def sent_near(i, carry):
        for a in range(count):
            near_copy(a, block(a, i // 2, 1 - here[a][0], i % 2), i).wait_send()
        return carry

    lax.fori_loop(0, 8, sent_near, 0)

    def sent_z(k, carry):
        zt = others(k)
        for a in range(count):
            for lt in [here[a][1]] if late[a] else [0, 1]:
                q = block(a, zt, here[a][0], lt)
                up, down = slots(a, zt, lt)

                @pl.when(zt > z)
                def _():
                    right_copy(a, q, up).wait_send()

                @pl.when(zt < z)
                def _():
                    left_copy(a, q, down).wait_send()

        return carry

    lax.fori_loop(0, 3, sent_z, 0)
    for a in range(count):
        f, l = here[a]
        if late[a]:
            for zt in range(4):
                mid_copy(a, block(a, zt, f, 1 - l), zt).wait_send()
        else:
            mid_copy(a, block(a, z, f, 1 - l), 0).wait_send()


def scatter_sum(arrays, orders, collective_id, out_dtype=F32, group_arrays=()):
    count, shared = len(arrays), len(group_arrays)
    shapes = [v.shape[1:] for v in (*arrays, *group_arrays)]
    late = [order in "XY" for order in orders]
    sizes = [[16, 16, 8, 4, 3, 3] if up else [16, 16, 8, 1, 6, 6] for up in late]
    scratch = []
    for k in range(6):
        scratch += [pltpu.VMEM((size[k],) + shape, BF16) for size, shape in zip(sizes, shapes)]
    scratch += [pltpu.SemaphoreType.DMA((count, 16))]
    scratch += [pltpu.SemaphoreType.DMA((count, 2, n)) for n in (16, 8, 4, 6, 6)]
    scratch += [pltpu.SemaphoreType.DMA((max(shared, 1), 2, 5))]
    scratch += [pltpu.VMEM((2,) + shape, BF16) for shape in shapes[count:]] * 2
    scratch += [pltpu.VMEM(shape, BF16) for shape in shapes[count:]]
    return pl.pallas_call(
        functools.partial(scatter_kernel, count, shared, orders),
        out_shape=[jax.ShapeDtypeStruct(shape, out_dtype) for shape in shapes],
        in_specs=[pl.BlockSpec(memory_space=pl.ANY)] * len(shapes),
        out_specs=[pl.BlockSpec(memory_space=pltpu.VMEM)] * len(shapes),
        scratch_shapes=scratch,
        compiler_params=pltpu.CompilerParams(
            collective_id=collective_id, has_side_effects=True, vmem_limit_bytes=60 << 20
        ),
        cost_estimate=traffic(arrays, 1),
        name="scatter_sum",
    )(*arrays, *group_arrays)


def known_mesh():
    return lax.axis_size("seq") == 8 and lax.axis_size("head") == 4


def gather(arrays, orders, collective_id, group_arrays=()):
    if known_mesh():
        return gather_all(arrays, orders, collective_id, group_arrays)
    return [lax.all_gather(v, EVERY, axis=0, tiled=False) for v in arrays] + [
        lax.all_gather(v, "head", axis=0, tiled=False) for v in group_arrays
    ]


def scatter(arrays, orders, collective_id, out_dtype=F32, group_arrays=()):
    if known_mesh():
        return scatter_sum(arrays, orders, collective_id, out_dtype, group_arrays)
    return [
        lax.psum_scatter(v, axes, scatter_dimension=0, tiled=False).astype(out_dtype)
        for v, axes in [(v, EVERY) for v in arrays] + [(v, "head") for v in group_arrays]
    ]


def fill(target, refs, columns, scale=None):
    at = 0
    for ref in refs:
        rows = ref.shape[2]
        for p in range(ref.shape[0]):
            piece = ref[p, 0, :, columns]
            target[at : at + rows] = piece if scale is None else piece * scale
            at += rows


def spill(value, refs, columns):
    at = 0
    for ref in refs:
        rows = ref.shape[2]
        for p in range(ref.shape[0]):
            ref[p, 0, :, columns] = value[at : at + rows].astype(ref.dtype)
            at += rows


def across(left, right):
    return lax.dot_general(left, right, (((1,), (1,)), ((), ())), preferred_element_type=F32)


def down(left, right):
    return lax.dot_general(left, right, (((0,), (0,)), ((), ())), preferred_element_type=F32)


def soft_columns(scores):
    peak = jnp.max(scores, axis=0, keepdims=True)
    weights = jnp.exp(scores - peak)
    total = jnp.sum(weights, axis=0, keepdims=True)
    return weights * (1.0 / total), peak + jnp.log(total)


def score_grads(probs, grad_probs):
    delta = jnp.sum(probs * grad_probs, axis=0, keepdims=True)
    return (probs * (grad_probs - delta)).astype(BF16)


def allowed_pairs(key_ref, query_ref, start, tile, causal):
    doc_key, doc_query = key_ref[0, :, 0:1], query_ref[0, 0:1, pl.ds(start, tile)]
    allowed = doc_key == doc_query
    if causal:
        allowed &= key_ref[0, :, 1:2] <= query_ref[0, 1:2, pl.ds(start, tile)]
    return allowed


def attend_kernel(heads, tile, causal, *refs):
    key_ref, query_ref, own_ref = refs[:3]
    prior = refs[3:-6]
    out_ref, log_ref, key_s, value_s, query_s, result_s = refs[-6:]
    group = query_s.shape[0]
    for h in range(heads):
        fill(key_s, (*prior, own_ref), slice(h * 128, h * 128 + 64))
        fill(value_s, (*prior, own_ref), slice(h * 128 + 64, h * 128 + 128))
        at = heads * 128 + h * 64
        fill(query_s, (own_ref,), slice(at, at + 64), 0.125)

        def step(i, carry):
            start = pl.multiple_of(i * tile, tile)
            allowed = allowed_pairs(key_ref, query_ref, start, tile, causal)
            scores = across(key_s[...], query_s[pl.ds(start, tile), :])
            probs, log_total = soft_columns(jnp.where(allowed, scores, NEGATIVE))
            result_s[pl.ds(start, tile), :] = down(probs.astype(BF16), value_s[...]).astype(BF16)
            log_ref[0, h : h + 1, pl.ds(start, tile)] = log_total
            return carry

        lax.fori_loop(0, group // tile, step, 0)
        spill(result_s[...], (out_ref,), slice(h * 64, h * 64 + 64))


def rows_spec(shape):
    return pl.BlockSpec((shape[0], 1) + shape[2:], lambda m: (0, m, 0, 0))


def whole_spec(shape):
    return pl.BlockSpec((1,) + shape[1:], lambda m: (m, 0, 0))


def attend(joined, prior, key_info, query_info, heads, causal, tile=256):
    parts, micro, rows, _ = joined.shape
    group = parts * rows
    keys = key_info.shape[1]
    out, logs = (parts, micro, rows, heads * 64), (micro, heads, group)
    return pl.pallas_call(
        functools.partial(attend_kernel, heads, tile, causal),
        grid=(micro,),
        out_shape=[jax.ShapeDtypeStruct(out, BF16), jax.ShapeDtypeStruct(logs, F32)],
        in_specs=[whole_spec(key_info.shape), whole_spec(query_info.shape), rows_spec(joined.shape)]
        + [rows_spec(p.shape) for p in prior],
        out_specs=[rows_spec(out), whole_spec(logs)],
        scratch_shapes=[
            pltpu.VMEM((keys, 64), BF16),
            pltpu.VMEM((keys, 64), BF16),
            pltpu.VMEM((group, 64), BF16),
            pltpu.VMEM((group, 64), BF16),
        ],
        compiler_params=pltpu.CompilerParams(vmem_limit_bytes=48 << 20),
        cost_estimate=pl.CostEstimate(
            flops=16 * micro * heads * group * keys * 128,
            transcendentals=micro * heads * group * keys,
            bytes_accessed=joined.size * 4,
        ),
        name="attend",
    )(key_info, query_info, joined, *prior)


def attend_back_kernel(heads, tile, causal, count, *refs):
    key_ref, query_ref, own_ref, log_ref, grad_ref = refs[:5]
    prior = refs[5 : 5 + count]
    out_ref, *prior_out = refs[5 + count : 6 + 2 * count]
    key_s, value_s, query_s, grad_s, gk_s, gv_s, result_s = refs[6 + 2 * count :]
    group = query_s.shape[0]
    for h in range(heads):
        key_cut, value_cut = slice(h * 128, h * 128 + 64), slice(h * 128 + 64, h * 128 + 128)
        fill(key_s, (*prior, own_ref), key_cut)
        fill(value_s, (*prior, own_ref), value_cut)
        query_cut = slice(heads * 128 + h * 64, heads * 128 + h * 64 + 64)
        fill(query_s, (own_ref,), query_cut, 0.125)
        fill(grad_s, (grad_ref,), slice(h * 64, h * 64 + 64))
        gk_s[...] = jnp.zeros_like(gk_s)
        gv_s[...] = jnp.zeros_like(gv_s)

        def step(i, carry):
            start = pl.multiple_of(i * tile, tile)
            here = pl.ds(start, tile)
            allowed = allowed_pairs(key_ref, query_ref, start, tile, causal)
            query, grad_out = query_s[here, :], grad_s[here, :]
            scores = jnp.where(allowed, across(key_s[...], query), NEGATIVE)
            probs = jnp.exp(scores - log_ref[0, h : h + 1, here])
            grad_scores = score_grads(probs, across(value_s[...], grad_out))
            gv_s[...] += jnp.dot(probs.astype(BF16), grad_out, preferred_element_type=F32)
            gk_s[...] += jnp.dot(grad_scores, query, preferred_element_type=F32)
            result_s[here, :] = down(grad_scores, key_s[...]) * 0.125
            return carry

        lax.fori_loop(0, group // tile, step, 0)
        spill(result_s[...], (out_ref,), query_cut)
        spill(gk_s[...], (*prior_out, out_ref), key_cut)
        spill(gv_s[...], (*prior_out, out_ref), value_cut)
    for p in range(out_ref.shape[0]):
        out_ref[p, 0, :, heads * 192 :] = jnp.zeros(
            (out_ref.shape[2], out_ref.shape[3] - heads * 192), out_ref.dtype
        )


def attend_back(
    joined, prior, key_info, query_info, logs, grad, heads, causal, out_dtype, tile=256
):
    parts, micro, rows, _ = joined.shape
    group = parts * rows
    keys = key_info.shape[1]
    return pl.pallas_call(
        functools.partial(attend_back_kernel, heads, tile, causal, len(prior)),
        grid=(micro,),
        out_shape=[jax.ShapeDtypeStruct(joined.shape, out_dtype)]
        + [jax.ShapeDtypeStruct(p.shape, BF16) for p in prior],
        in_specs=[
            whole_spec(key_info.shape),
            whole_spec(query_info.shape),
            rows_spec(joined.shape),
            whole_spec(logs.shape),
            rows_spec(grad.shape),
        ]
        + [rows_spec(p.shape) for p in prior],
        out_specs=[rows_spec(joined.shape)] + [rows_spec(p.shape) for p in prior],
        scratch_shapes=[
            pltpu.VMEM((keys, 64), BF16),
            pltpu.VMEM((keys, 64), BF16),
            pltpu.VMEM((group, 64), BF16),
            pltpu.VMEM((group, 64), BF16),
            pltpu.VMEM((keys, 64), F32),
            pltpu.VMEM((keys, 64), F32),
            pltpu.VMEM((group, 64), F32),
        ],
        compiler_params=pltpu.CompilerParams(vmem_limit_bytes=48 << 20),
        cost_estimate=pl.CostEstimate(
            flops=24 * micro * heads * group * keys * 128,
            transcendentals=micro * heads * group * keys,
            bytes_accessed=joined.size * 6,
        ),
        name="attend_back",
    )(key_info, query_info, joined, logs, grad, *prior)


def cross_kernel(query_ref, pairs_ref, out_ref, log_ref):
    for i in range(D // 128):
        outs = []
        for h in range(2):
            at = i * 128 + h * 64
            query, keys = query_ref[0, :, at : at + 64] * 0.125, pairs_ref[0, :, at : at + 64]
            values = pairs_ref[0, :, D + at : D + at + 64]
            probs, log_total = soft_columns(across(keys, query))
            outs.append(down(probs.astype(BF16), values))
            log_ref[0, i * 2 + h : i * 2 + h + 1, :] = log_total
        out_ref[0, :, i * 128 : i * 128 + 128] = jnp.concatenate(outs, axis=1).astype(BF16)


def cross(query, pairs):
    micro, rows, _ = query.shape
    keys = pairs.shape[1]
    logs = (micro, HEADS, rows)
    return pl.pallas_call(
        cross_kernel,
        grid=(micro,),
        out_shape=[jax.ShapeDtypeStruct(query.shape, BF16), jax.ShapeDtypeStruct(logs, F32)],
        in_specs=[whole_spec(query.shape), whole_spec(pairs.shape)],
        out_specs=[whole_spec(query.shape), whole_spec(logs)],
        compiler_params=pltpu.CompilerParams(vmem_limit_bytes=48 << 20),
        cost_estimate=pl.CostEstimate(
            flops=16 * micro * HEADS * rows * keys * 128,
            transcendentals=micro * HEADS * rows * keys,
            bytes_accessed=pairs.size * 2,
        ),
        name="cross",
    )(query, pairs)


def cross_back_kernel(
    query_ref, pairs_ref, log_ref, grad_ref, grad_query_ref, grad_pairs_ref
):
    for i in range(D // 128):
        query_parts, key_parts, value_parts = [], [], []
        for h in range(2):
            at = i * 128 + h * 64
            cut = slice(at, at + 64)
            query, keys = query_ref[0, :, cut] * 0.125, pairs_ref[0, :, cut]
            values, grad_out = pairs_ref[0, :, D + at : D + at + 64], grad_ref[0, :, cut]
            probs = jnp.exp(across(keys, query) - log_ref[0, i * 2 + h : i * 2 + h + 1, :])
            grad_scores = score_grads(probs, across(values, grad_out))
            value_parts.append(jnp.dot(probs.astype(BF16), grad_out, preferred_element_type=F32))
            key_parts.append(jnp.dot(grad_scores, query, preferred_element_type=F32))
            query_parts.append(down(grad_scores, keys) * 0.125)
        cut = slice(i * 128, i * 128 + 128)
        grad_query_ref[0, :, cut] = jnp.concatenate(query_parts, axis=1).astype(BF16)
        grad_pairs_ref[0, :, cut] = jnp.concatenate(key_parts, axis=1).astype(BF16)
        cut = slice(D + i * 128, D + i * 128 + 128)
        grad_pairs_ref[0, :, cut] = jnp.concatenate(value_parts, axis=1).astype(BF16)


def cross_back(query, pairs, logs, grad):
    micro, rows, _ = query.shape
    keys = pairs.shape[1]
    return pl.pallas_call(
        cross_back_kernel,
        grid=(micro,),
        out_shape=[jax.ShapeDtypeStruct(query.shape, BF16), jax.ShapeDtypeStruct(pairs.shape, BF16)],
        in_specs=[whole_spec(v.shape) for v in (query, pairs, logs, grad)],
        out_specs=[whole_spec(query.shape), whole_spec(pairs.shape)],
        compiler_params=pltpu.CompilerParams(vmem_limit_bytes=48 << 20),
        cost_estimate=pl.CostEstimate(
            flops=24 * micro * HEADS * rows * keys * 128,
            transcendentals=micro * HEADS * rows * keys,
            bytes_accessed=pairs.size * 4,
        ),
        name="cross_back",
    )(query, pairs, logs, grad)


SMALL_ROWS = 29
SINGLES = (4, 0, 5, 10, 1, 11, 17, 12, 18, 19, 21, 13, 22, 27, 14, 28)


def head_places(head, heads):
    base = head // heads * joined_width(heads) + head % heads * 64
    return base + head % heads * 64 + 64, base + heads * 128


def joined_width(heads):
    return (heads * 192 + 127) // 128 * 128


def unpack_kernel(width, heads, pack_ref, *refs):
    e_joined, e_hidden, d_joined, d_hidden, pair_bias = refs[:5]
    singles, full = refs[5:-1], refs[-1]
    for d in range(pack_ref.shape[0]):
        full[:, d * width : d * width + width] = pack_ref[d, :, 0:width].astype(F32)
    for target, row in ((e_joined, 2), (d_joined, 15)):
        target[...] = jnp.zeros_like(target)
        for head in range(HEADS):
            value_at, query_at = head_places(head, heads)
            cut = slice(head * 64, head * 64 + 64)
            target[:, query_at : query_at + 64] = full[row : row + 1, cut]
            target[:, value_at : value_at + 64] = full[row + 1 : row + 2, cut]
    for target, row in ((e_hidden, 6), (d_hidden, 23)):
        for k in range(FF // D):
            target[:, k * D : k * D + D] = full[row + k : row + k + 1, :]
    pair_bias[:, 0:D] = jnp.zeros((1, D), F32)
    pair_bias[:, D:] = full[20:21, :]
    for target, row in zip(singles, SINGLES):
        target[...] = full[row : row + 1, :]


def unpack_small(packs, heads):
    devices = packs.shape[0]
    joined = joined_width(heads) * (HEADS // heads)
    widths = [joined, FF, joined, FF, 2 * D] + [D] * len(SINGLES)
    return pl.pallas_call(
        functools.partial(unpack_kernel, D // devices, heads),
        out_shape=[jax.ShapeDtypeStruct((1, w), F32) for w in widths],
        scratch_shapes=[pltpu.VMEM((32, D), F32)],
        name="unpack_small",
    )(packs)


def pack_kernel(width, heads, count, *refs):
    e_joined, e_hidden, d_joined, d_hidden, pair_sum = refs[:5]
    singles, out_ref, full = refs[5 : 5 + count], refs[-2], refs[-1]
    full[...] = jnp.zeros_like(full)
    for source, row in ((e_joined, 2), (d_joined, 15)):
        for head in range(HEADS):
            value_at, query_at = head_places(head, heads)
            cut = slice(head * 64, head * 64 + 64)
            full[row : row + 1, cut] = source[:, query_at : query_at + 64]
            full[row + 1 : row + 2, cut] = source[:, value_at : value_at + 64]
    for source, row in ((e_hidden, 6), (d_hidden, 23)):
        for k in range(FF // D):
            full[row + k : row + k + 1, :] = source[:, k * D : k * D + D]
    full[20:21, :] = pair_sum[:, D:]
    for source, row in zip(singles, SINGLES):
        full[row : row + 1, :] = source[...]
    out_ref[...] = jnp.zeros_like(out_ref)
    for d in range(out_ref.shape[0]):
        out_ref[d, :, 0:width] = full[:, d * width : d * width + width].astype(BF16)


def pack_small(vectors, devices, heads):
    return pl.pallas_call(
        functools.partial(pack_kernel, D // devices, heads, len(SINGLES)),
        out_shape=jax.ShapeDtypeStruct((devices, 32, 128), BF16),
        scratch_shapes=[pltpu.VMEM((32, D), F32)],
        name="pack_small",
    )(*vectors)


def norm(resid, gain, shift):
    center = resid - jnp.mean(resid, axis=-1, keepdims=True)
    scale = lax.rsqrt(jnp.mean(center * center, axis=-1, keepdims=True) + EPSILON)
    hat = center * scale
    return hat * gain + shift, (hat, scale)


def norm_back(grad, kept, gain):
    hat, scale = kept
    inner = grad * gain
    grad_resid = scale * (
        inner
        - jnp.mean(inner, axis=-1, keepdims=True)
        - hat * jnp.mean(inner * hat, axis=-1, keepdims=True)
    )
    gain_sum = jnp.sum(grad * hat, axis=0, keepdims=True)
    return grad_resid, gain_sum, jnp.sum(grad, axis=0, keepdims=True)


def gelu(value):
    return value * (1.0 + lax.erf(value * 0.7071067811865476)) * 0.5


def gelu_slope(value):
    bell = jnp.exp(value * value * -0.5) * 0.3989422804014327
    return 0.5 * (1.0 + lax.erf(value * 0.7071067811865476)) + value * bell


def mm(left, right):
    return jnp.dot(left, right, preferred_element_type=F32)


def mm_rows(left, right):
    return lax.dot_general(left, right, (((0,), (0,)), ((), ())), preferred_element_type=F32)


def mm_back(left, right):
    return lax.dot_general(left, right, (((1,), (1,)), ((), ())), preferred_element_type=F32)


def row_sum(value):
    return jnp.sum(value.astype(F32), axis=0, keepdims=True)


def doc_starts(lengths):
    count = lengths.shape[1]
    before = jnp.arange(count)[None, :] < jnp.arange(count)[:, None]
    return jnp.sum(jnp.where(before[None], lengths[:, None, :], 0), axis=2)


def doc_ids(starts, positions):
    return jnp.sum((starts[:, None, :] <= positions[None, :, None]).astype(jnp.int32), axis=2) - 1


def key_and_query_info(starts, key_pos, query_pos):
    key_docs, query_docs = doc_ids(starts, key_pos), doc_ids(starts, query_pos)
    micro = starts.shape[0]
    key_info = jnp.stack(
        [key_docs, jnp.broadcast_to(key_pos, (micro,) + key_pos.shape)], axis=2
    )
    query_info = jnp.stack(
        [query_docs, jnp.broadcast_to(query_pos, (micro,) + query_pos.shape)], axis=1
    )
    return key_info, query_info


def by_group(weight, parts):
    rows = weight.shape[0]
    split = weight.reshape(rows, parts, HEADS // parts, 3, HEAD_DIM)
    pairs = split[:, :, :, 1:].reshape(rows, parts, -1)
    query = split[:, :, :, 0].reshape(rows, parts, -1)
    width = joined_width(HEADS // parts)
    blank = jnp.zeros((rows, parts, width - pairs.shape[2] - query.shape[2]), weight.dtype)
    return jnp.concatenate([pairs, query, blank], axis=2).reshape(rows, parts * width)


def by_head(grad, parts):
    rows, heads = grad.shape[0], HEADS // parts
    split = grad.reshape(rows, parts, -1)
    pairs = split[:, :, : heads * 128].reshape(rows, parts, heads, 2, HEAD_DIM)
    query = split[:, :, heads * 128 : heads * 192].reshape(rows, parts, heads, 1, HEAD_DIM)
    return jnp.concatenate([query, pairs], axis=3).reshape(rows, 3 * D)


def to_beside_rows(grad, devices):
    split = grad.reshape(devices, FF // D, -1, D)
    return split.transpose(0, 2, 1, 3).reshape(D, FF)


def my_columns(full, parts):
    width = full.shape[1] // parts
    return lax.dynamic_slice_in_dim(full, lax.axis_index("head") * width, width, 1)


def all_columns(mine, parts):
    rows, width = mine.shape
    full = jnp.zeros((rows, width * parts), mine.dtype)
    return lax.dynamic_update_slice_in_dim(full, mine, lax.axis_index("head") * width, 1)


def to_tokens(value):
    parts, micro, rows, columns = value.shape
    got = lax.all_to_all(value, "head", split_axis=0, concat_axis=0, tiled=True)
    return got.transpose(1, 2, 0, 3).reshape(micro * rows, parts * columns)


def to_heads(value, parts, micro):
    rows = value.shape[0] // micro
    split = value.reshape(micro, rows, parts, -1).transpose(2, 0, 1, 3)
    return lax.all_to_all(split, "head", split_axis=0, concat_axis=0, tiled=True)


def from_before(value, by):
    count = lax.axis_size("seq")
    return lax.ppermute(value, "seq", [(i, i + by) for i in range(count - by)])


def to_before(value, by):
    count = lax.axis_size("seq")
    return lax.ppermute(value, "seq", [(i + by, i) for i in range(count - by)])


def shards(
    source,
    target,
    cotangent,
    src_lengths,
    tgt_lengths,
    retrieved,
    encoder_qkv,
    encoder_out,
    encoder_up,
    encoder_down,
    encoder_gains,
    encoder_biases,
    decoder_qkv,
    decoder_out,
    cross_query,
    cross_keyvalue,
    cross_out,
    decoder_up,
    decoder_down,
    decoder_gains,
    decoder_biases,
):
    micro, src_rows, _ = source.shape
    tgt_rows = target.shape[1]
    parts = lax.axis_size("head")
    devices = parts * lax.axis_size("seq")
    seq, me = lax.axis_index("seq"), lax.axis_index(EVERY)
    src_group, tgt_group = src_rows * parts, tgt_rows * parts
    asked = retrieved.shape[1]
    source_rows = source.reshape(micro * src_rows, D)
    target_rows = target.reshape(micro * tgt_rows, D)

    heads = HEADS // parts
    small = jnp.concatenate([encoder_gains, encoder_biases, decoder_gains, decoder_biases], axis=0)
    small = jnp.pad(small, ((0, 32 - SMALL_ROWS), (0, 128 - small.shape[1])))
    encoder_full = gather(
        [by_group(encoder_qkv, parts), encoder_out, encoder_up, encoder_down, small],
        "xyxyx",
        0,
        [source, target],
    )
    source_all, target_all = encoder_full[5:]
    decoder_parts = [
        by_group(decoder_qkv, parts),
        decoder_out,
        cross_query,
        cross_keyvalue,
        cross_out,
        decoder_up,
    ]
    decoder_pack, small_full = lax.optimization_barrier(
        (jnp.concatenate(decoder_parts, axis=1), encoder_full[4])
    )
    decoder_full = lax.all_gather(decoder_pack, EVERY, axis=0, tiled=True)
    d_down = lax.all_gather(decoder_down, EVERY, axis=0, tiled=True)
    e_qkv, e_out, e_up, e_down = [v.reshape(-1, v.shape[-1]) for v in encoder_full[:4]]
    e_bias, e_hidden_bias, d_bias, d_hidden_bias, pair_bias, *singles = unpack_small(
        small_full, heads
    )
    e_b2, e_g0, e_b3, e_b8, e_g1, e_b9 = singles[:6]
    d_b2, d_g0, d_b3, d_b4, d_b6, d_g1, d_b7, d_b12, d_g2, d_b13 = singles[6:]

    src_pos = seq * src_group + jnp.arange(src_group, dtype=jnp.int32)
    src_info = key_and_query_info(doc_starts(src_lengths), src_pos, src_pos)
    tgt_pos = seq * tgt_group + jnp.arange(tgt_group, dtype=jnp.int32)
    tgt_key_pos = (seq - REACH) * tgt_group + jnp.arange((REACH + 1) * tgt_group, dtype=jnp.int32)
    tgt_info = key_and_query_info(doc_starts(tgt_lengths), tgt_key_pos, tgt_pos)

    e_qkv_here = my_columns(e_qkv, parts)
    e_joined = (mm(source_all.reshape(-1, D), e_qkv_here) + my_columns(e_bias, parts)).astype(BF16)
    e_joined = e_joined.reshape(parts, micro, src_rows, -1)
    e_attended, e_logs = attend(e_joined, [], *src_info, heads, False)
    e_mixed = to_tokens(e_attended)
    e_first, e_kept_one = norm(
        source_rows.astype(F32) + mm(e_mixed, e_out) + e_b2, e_g0, e_b3
    )
    e_first_low = e_first.astype(BF16)
    e_hidden = mm(e_first_low, e_up) + e_hidden_bias
    e_active = gelu(e_hidden).astype(BF16)
    e_result, e_kept_two = norm(e_first + mm(e_active, e_down) + e_b8, e_g1, e_b9)

    src_own = me * src_rows + jnp.arange(src_rows, dtype=jnp.int32)
    select = (retrieved[:, :, None] == src_own[None, None, :]).astype(BF16)
    picked = jnp.einsum(
        "mrs,msd->mrd",
        select,
        e_result.astype(BF16).reshape(micro, src_rows, D),
        preferred_element_type=F32,
    ).astype(BF16)
    picked = [picked[m].reshape(devices, asked // devices, D) for m in range(micro)]
    fetched = gather(scatter(picked, "xy", 2, BF16), "xy", 3)
    fetched = jnp.concatenate([v.reshape(asked, D) for v in fetched], axis=0)
    decoder_full, fetched = lax.optimization_barrier((decoder_full, fetched))
    ends = [0]
    for part in decoder_parts:
        ends.append(ends[-1] + part.shape[1])
    d_qkv, d_out, c_query, c_pairs, c_out, d_up = [
        decoder_full[:, start:end] for start, end in zip(ends, ends[1:])
    ]

    d_qkv_here = my_columns(d_qkv, parts)
    d_joined = (mm(target_all.reshape(-1, D), d_qkv_here) + my_columns(d_bias, parts)).astype(BF16)
    d_joined = d_joined.reshape(parts, micro, tgt_rows, -1)
    d_pairs = d_joined[..., : heads * 128]
    d_prior = [from_before(d_pairs, by) for by in range(REACH, 0, -1)]
    d_attended, d_logs = attend(d_joined, d_prior, *tgt_info, heads, True)
    d_mixed = to_tokens(d_attended)
    d_first, d_kept_one = norm(
        target_rows.astype(F32) + mm(d_mixed, d_out) + d_b2, d_g0, d_b3
    )
    d_first_low = d_first.astype(BF16)
    queries = (mm(d_first_low, c_query) + d_b4).astype(BF16).reshape(micro, tgt_rows, D)

    pairs = (mm(fetched, c_pairs) + pair_bias).astype(BF16).reshape(micro, asked, 2 * D)

    crossed_rows, cross_logs = cross(queries, pairs)
    crossed = crossed_rows.reshape(micro * tgt_rows, D)
    d_second, d_kept_two = norm(d_first + mm(crossed, c_out) + d_b6, d_g1, d_b7)
    d_second_low = d_second.astype(BF16)
    d_hidden = mm(d_second_low, d_up) + d_hidden_bias
    d_active = gelu(d_hidden).astype(BF16)
    decoded, d_kept_three = norm(d_second + mm(d_active, d_down) + d_b12, d_g2, d_b13)

    grad = cotangent.reshape(micro * tgt_rows, D).astype(F32)
    g_sum, d_gain_three, d_shift_three = norm_back(grad, d_kept_three, d_g2)
    g_third = g_sum.astype(BF16)
    w_d_down = mm_rows(d_active, g_third)
    g_hidden = (mm_back(g_third, d_down) * gelu_slope(d_hidden)).astype(BF16)
    w_d_up = mm_rows(d_second_low, g_hidden)
    g_second = g_sum + mm_back(g_hidden, d_up)
    g_sum_two, d_gain_two, d_shift_two = norm_back(g_second, d_kept_two, d_g1)
    g_branch_cross = g_sum_two.astype(BF16)
    w_c_out = mm_rows(crossed, g_branch_cross)
    g_crossed = mm_back(g_branch_cross, c_out).astype(BF16).reshape(micro, tgt_rows, D)
    g_queries, g_pairs = cross_back(queries, pairs, cross_logs, g_crossed)
    g_queries = g_queries.reshape(micro * tgt_rows, D)
    g_pairs = g_pairs.reshape(micro * asked, 2 * D)
    g_fetched = mm_back(g_pairs, c_pairs).astype(BF16).reshape(micro, asked, D)
    g_fetched = [g_fetched[m].reshape(devices, asked // devices, D) for m in range(micro)]
    g_fetched = gather(scatter(g_fetched, "xy", 4, BF16), "xy", 5)
    w_c_pairs = mm_rows(fetched, g_pairs)
    w_c_query = mm_rows(d_first_low, g_queries)
    decoder_grads = [w_c_query, w_c_pairs, w_c_out, w_d_up]
    decoder_grads = [g.astype(BF16) for g in decoder_grads]
    decoder_grads.append(to_beside_rows(w_d_down.astype(BF16), devices))
    decoder_pack, *g_fetched = lax.optimization_barrier(
        (jnp.concatenate(decoder_grads, axis=1), *g_fetched)
    )
    decoder_sums = lax.psum_scatter(decoder_pack, EVERY, scatter_dimension=0, tiled=True)
    g_first = g_sum_two + mm_back(g_queries, c_query)
    g_resid, d_gain_one, d_shift_one = norm_back(g_first, d_kept_one, d_g0)
    g_branch = g_resid.astype(BF16)
    w_d_out = mm_rows(d_mixed, g_branch)
    g_mixed = mm_back(g_branch, d_out).astype(BF16)
    g_attended = to_heads(g_mixed, parts, micro)
    g_own, *g_prior = attend_back(
        d_joined, d_prior, *tgt_info, d_logs, g_attended, heads, True, F32
    )
    g_back = [to_before(g, by) for g, by in zip(g_prior, range(REACH, 0, -1))]

    g_result = jnp.einsum(
        "mrs,mrd->msd",
        select,
        jnp.stack([v.reshape(asked, D) for v in g_fetched]),
        preferred_element_type=F32,
    ).reshape(micro * src_rows, D)
    g_sum, e_gain_two, e_shift_two = norm_back(g_result, e_kept_two, e_g1)
    g_second_low = g_sum.astype(BF16)
    w_e_down = mm_rows(e_active, g_second_low)
    ge_hidden = (mm_back(g_second_low, e_down) * gelu_slope(e_hidden)).astype(BF16)
    w_e_up = mm_rows(e_first_low, ge_hidden)
    g_first = g_sum + mm_back(ge_hidden, e_up)
    ge_resid, e_gain_one, e_shift_one = norm_back(g_first, e_kept_one, e_g0)
    ge_branch = ge_resid.astype(BF16)
    w_e_out = mm_rows(e_mixed, ge_branch)
    ge_mixed = mm_back(ge_branch, e_out).astype(BF16)
    ge_attended = to_heads(ge_mixed, parts, micro)
    (ge_joined,) = attend_back(
        e_joined, [], *src_info, e_logs, ge_attended, heads, False, BF16
    )
    ge_joined = ge_joined.reshape(parts * micro * src_rows, -1)
    w_e_qkv = mm_rows(source_all.reshape(-1, D), ge_joined)
    g_source_all = mm_back(ge_joined, e_qkv_here).astype(BF16)

    *g_back, ge_joined = lax.optimization_barrier((*g_back, ge_joined))
    width = heads * 128
    g_pairs_own = g_own[..., :width] + sum(g.astype(F32) for g in g_back)
    g_joined = jnp.concatenate([g_pairs_own.astype(BF16), g_own[..., width:].astype(BF16)], axis=-1)
    g_joined = g_joined.reshape(parts * micro * tgt_rows, -1)
    w_d_qkv = mm_rows(target_all.reshape(-1, D), g_joined)
    g_target_all = mm_back(g_joined, d_qkv_here).astype(BF16)

    def pieces(value):
        return value.astype(BF16).reshape(devices, value.shape[0] // devices, value.shape[1])

    ends = [0]
    for part in decoder_grads:
        ends.append(ends[-1] + part.shape[1])
    decoder_sums = [decoder_sums[:, start:end].astype(F32) for start, end in zip(ends, ends[1:])]
    decoder_sums[4] = decoder_sums[4].reshape(-1, FF // D, D).transpose(1, 0, 2).reshape(-1, D)
    small_grads = pack_small(
        [
            all_columns(row_sum(ge_joined), parts),
            row_sum(ge_hidden),
            all_columns(row_sum(g_joined), parts),
            row_sum(g_hidden),
            row_sum(g_pairs),
            row_sum(ge_branch),
            e_gain_one,
            e_shift_one,
            row_sum(g_second_low),
            e_gain_two,
            e_shift_two,
            row_sum(g_branch),
            d_gain_one,
            d_shift_one,
            row_sum(g_queries),
            row_sum(g_branch_cross),
            d_gain_two,
            d_shift_two,
            row_sum(g_third),
            d_gain_three,
            d_shift_three,
        ],
        devices,
        heads,
    )
    encoder_sums = scatter(
        [
            pieces(all_columns(w_e_qkv.astype(BF16), parts)),
            pieces(w_e_out),
            pieces(w_e_up),
            pieces(w_e_down),
            small_grads,
            pieces(all_columns(w_d_qkv.astype(BF16), parts)),
            pieces(w_d_out),
        ],
        "xyyxxyx",
        7,
        F32,
        [v.reshape(parts, -1, D) for v in (g_source_all, g_target_all)],
    )
    g_source, g_target = ge_resid + encoder_sums[7], g_resid + encoder_sums[8]
    small_sums = encoder_sums[4][:, : encoder_gains.shape[1]]
    return (
        decoded.reshape(micro, tgt_rows, D),
        g_source.reshape(micro, src_rows, D),
        g_target.reshape(micro, tgt_rows, D),
        by_head(encoder_sums[0], parts),
        *encoder_sums[1:4],
        small_sums[0:2],
        small_sums[2:12],
        by_head(encoder_sums[5], parts),
        encoder_sums[6],
        *decoder_sums,
        small_sums[12:15],
        small_sums[15:SMALL_ROWS],
    )


def solution(mesh):
    in_specs = (
        P(None, ("seq", "head"), None),
        P(None, ("seq", "head"), None),
        P(None, ("seq", "head"), None),
        P(),
        P(),
        P(),
        P(("seq", "head"), None),
        P(("seq", "head"), None),
        P(("seq", "head"), None),
        P(("seq", "head"), None),
        P(None, ("seq", "head")),
        P(None, ("seq", "head")),
        P(("seq", "head"), None),
        P(("seq", "head"), None),
        P(("seq", "head"), None),
        P(("seq", "head"), None),
        P(("seq", "head"), None),
        P(("seq", "head"), None),
        P(("seq", "head"), None),
        P(None, ("seq", "head")),
        P(None, ("seq", "head")),
    )
    out_specs = (
        P(None, ("seq", "head"), None),
        P(None, ("seq", "head"), None),
        P(None, ("seq", "head"), None),
        P(("seq", "head"), None),
        P(("seq", "head"), None),
        P(("seq", "head"), None),
        P(("seq", "head"), None),
        P(None, ("seq", "head")),
        P(None, ("seq", "head")),
        P(("seq", "head"), None),
        P(("seq", "head"), None),
        P(("seq", "head"), None),
        P(("seq", "head"), None),
        P(("seq", "head"), None),
        P(("seq", "head"), None),
        P(("seq", "head"), None),
        P(None, ("seq", "head")),
        P(None, ("seq", "head")),
    )
    return jax.shard_map(shards, mesh=mesh, in_specs=in_specs, out_specs=out_specs, check_vma=False)
```

time: 1040 us -> 825 us (0.79)
  Pallas kernels: 631 us -> 516 us
  local copies, waits for them, and re-layouts: 161 us -> 81.2 us
  waiting for transfers between devices: 53.7 us -> 30 us
    pallas_call x9, Pallas kernels: 483 us -> 389 us  [the longest x3 215 us: scatter_sum(): pl.pallas_call(functools.partial(scatter_kernel, count, shared, orders),...]
    unnamed x309 -> x200, local copies, waits for them, and re-layouts: 55 us -> 22.2 us
    ppermute x2, waiting for transfers between devices: 30.4 us -> 0.01 us  [to_before(): return lax.ppermute(value, 'seq', [(i + by, i) for i in range(count - by)])]
    dynamic_update_slice x4 -> x2, local copies, waits for them, and re-layouts: 24.7 us -> 0.03 us  [all_columns(): lax.dynamic_update_slice_in_dim(full, mine, lax.axis_index('head') * widt...]
    ppermute x2, waiting for transfers between devices: 0.01 us -> 19.2 us  [from_before(): return lax.ppermute(value, 'seq', [(i, i + by) for i in range(count - by)])]
    pallas_call x2, Pallas kernels: 74.4 us -> 59.9 us  [attend_back(): pl.pallas_call(functools.partial(attend_back_kernel, heads, tile, causal,...]
    concatenate x25 -> x3, local copies, waits for them, and re-layouts: 16.2 us -> 4.91 us  [the longest x1 4.83 us: shards(): jnp.concatenate(decoder_grads, axis=1)]
    dot_general x11, matrix products: 33.3 us -> 44.1 us  [mm_back(): lax.dot_general(left, right, (((1,), (1,)), ((), ())), preferred_element_...]
  transfers between devices with their start and end apart: 12 -> 11, of which waited for: 5 -> 2; matrix products, arithmetic and copies ran while one was open for 18% -> 18% of each run, Pallas kernels for 44% -> 38%
where the time goes in v2:
time: 825 us; the launch traced here: 819 us
  Pallas kernels  516 us (63%)
  matrix products  127 us (15%)
  local copies, waits for them, and re-layouts  81.2 us (10%)
  waiting for transfers between devices  30 us (4%)
  other arithmetic  25.5 us (3%)
  starting transfers between devices  23.9 us (3%)
  between operations  15.9 us (2%)
    pallas_call x3, Pallas kernels, scatter_sum(): pl.pallas_call(functools.partial(scatter_kernel, count, shared, orders),...  215 us
    pallas_call x3, Pallas kernels, gather_all(): pl.pallas_call(functools.partial(gather_kernel, count, shared, orders), o...  161 us
    pallas_call x2, Pallas kernels, attend_back(): pl.pallas_call(functools.partial(attend_back_kernel, heads, tile, causal,...  59.9 us
    pallas_call x2, Pallas kernels, attend(): pl.pallas_call(functools.partial(attend_kernel, heads, tile, causal), gri...  50.4 us
    dot_general x11, matrix products, mm_back(): lax.dot_general(left, right, (((1,), (1,)), ((), ())), preferred_element_...  44.1 us
    dot_general x11, matrix products, mm(): return jnp.dot(left, right, preferred_element_type=F32)  42.9 us
    dot_general x11, matrix products, mm_rows(): lax.dot_general(left, right, (((0,), (0,)), ((), ())), preferred_element_...  35.5 us
    unnamed x200, local copies, waits for them, and re-layouts  22.2 us
  transfers between devices with their start and end apart: 11, of which 2 were waited for; matrix products, arithmetic and copies ran while one was open for 18% of the time, Pallas kernels for 38%

profile of v2, /device:TPU:0, one launch (start us, length us, event | category | flops | bytes accessed | tf_op | source)
XLA Modules:
  0.0 819.4 jit_solution(5421608097178856080)
XLA Ops:
  13.2 101.5 %gather_all.3 = (bf16[32,24,2560]{2,1,0:T(8,128)(2,1)}, bf16[32,24,768]{2,1,0:T(8,128)(2,1)}, bf16[32,24,3072]{2,1,0:T(8,128)(2,1)}, bf16[32,96,768]{2,1,0:T(8,1...) custom-call(bf16[24,2560]{1,0:T(8,128)(2,1)} %bitcast.211, ...), custom_call_target="tpu_custom_call" | custom-call | bytes 231424000 | tf_op jit(solution)/shard_map/gather_all/pallas_call | solution.py:221
  118.2 4.8 add_convert_fusion.1
  123.0 28.1 %attend.2 = (bf16[4,2,256,192]{3,2,1,0:T(8,128)(2,1)S(1)}, f32[2,3,1024]{2,1,0:T(4,128)S(1)}) custom-call(s32[2,1024,2]{2,1,0:T(8,128)S(1)} %copy.109.refs_0_, s32[2,2,1024]{2,1,0:T(2,128)S(1)} %pad_add_fusion.2.refs_1_, bf16[4,2,256,640]{3,2,1,0:T(8,128)(2,1)S(1)} %bitcast.170), custom_call_target="tpu_custom_call" | custom-call | flops 12884901888 | bytes 5242880 | tf_op jit(solution)/shard_map/attend/pallas_call | solution.py:655
  152.4 3.6 all-to-all-start
  157.4 10.2 %all-to-all-done = bf16[4,2,256,192]{2,3,1,0:T(8,128)(2,1)S(1)} async-done(((bf16[4,2,256,192]{2,3,1,0:T(8,128)(2,1)}), bf16[4,2,256,192]{2,3,1,0:T(8,128)(2,1)S(1)}, u32[]{:S(2)}, u32[]{:S(2)}) %all-to-all-start) | async-done | bytes 786464 | tf_op jit(solution)/shard_map/all_to_all | solution.py:1008
  170.0 7.4 multiply_convert_fusion.1
  184.6 39.7 %scatter_sum.3 = (bf16[32,768]{1,0:T(8,128)(2,1)}, bf16[32,768]{1,0:T(8,128)(2,1)}) custom-call(bf16[32,32,768]{2,1,0:T(8,128)(2,1)} %bitcast.186, bf16[32,32,768]{2,1,0:T(8,128)(2,1)} %bitcast.185), custom_call_target="tpu_custom_call" | custom-call | bytes 3145728 | tf_op jit(solution)/shard_map/scatter_sum/pallas_call | solution.py:536
  224.3 30.4 %gather_all.4 = (bf16[32,32,768]{2,1,0:T(8,128)(2,1)}, bf16[32,32,768]{2,1,0:T(8,128)(2,1)}) custom-call(bf16[32,768]{1,0:T(8,128)(2,1)} %get-tuple-element.102.refs_0_, bf16[32,768]{1,0:T(8,128)(2,1)} %get-tuple-element.103.refs_1_), custom_call_target="tpu_custom_call" | custom-call | bytes 49152000 | tf_op jit(solution)/shard_map/gather_all/pallas_call | solution.py:221
  254.8 3.8 pad_maximum_fusion
  271.4 19.2 %collective-permute-done.refs_3_.refs_5_ = bf16[4,2,128,384]{3,2,1,0:T(8,128)(2,1)} collective-permute-done((bf16[4,2,128,384]{3,2,1,0:T(8,128)(2,1)}, bf16[4,2,128,384]{3,2,1,0:T(8,128)(2,1)}, u32[]{:S(2)}, u32[]{:S(2)}) %collective-permute-start) | collective-permute-done | bytes 786464 | tf_op jit(solution)/shard_map/ppermute | solution.py:1020
  290.6 22.4 %attend.3 = (bf16[4,2,128,192]{3,2,1,0:T(8,128)(2,1)S(1)}, f32[2,3,512]{2,1,0:T(4,128)S(1)}) custom-call(s32[2,1536,2]{2,1,0:T(8,128)S(1)} %pad_add_fusion.refs_0_, s32[2,2,512]{2,1,0:T(2,128)S(1)} %pad_add_fusion.3.refs_1_, bf16[4,2,128,640]{3,2,1,0:T(8,128)(2,1)S(1)} %bitcast.165, bf16[4,2,128,384]{3,2,1,0:T(8,128)(2,1)} %collective-permute-done.refs_3_.refs_5_, ...), custom_call_target="tpu_custom_call" | custom-call | flops 9663676416 | bytes 2621440 | tf_op jit(solution)/shard_map/attend/pallas_call | solution.py:655
  317.9 9.0 %add_convert_fusion = bf16[2048,1536]{1,0:T(8,128)(2,1)} fusion(bf16[2048,768]{1,0:T(8,128)(2,1)} %pad_maximum_fusion, f32[1536]{0:T(1024)S(1)} %reduce.21, bf16[768,9472]{1,0:T(8,128)(2,1)} %all-gather.3.cloned.1.call-done), kind=kOutput, calls=%fused_computation.1 | convolution fusion | flops 4838129664 | bytes 11802624 | tf_op jit(solution)/shard_map/dot_general | solution.py:935
  331.6 8.4 %cross.1 = (bf16[2,128,768]{2,1,0:T(8,128)(2,1)S(1)}, f32[2,12,128]{2,1,0:T(8,128)S(1)}) custom-call(bf16[2,128,768]{2,1,0:T(8,128)(2,1)S(1)} %bitcast.172, bf16[2,1024,1536]{2,1,0:T(8,128)(2,1)} %bitcast.241), custom_call_target="tpu_custom_call" | custom-call | flops 6442450944 | bytes 6291456 | tf_op jit(solution)/shard_map/cross/pallas_call | solution.py:773
  342.8 6.3 multiply_convert_fusion.2
  349.1 4.5 fusion.104
  360.8 4.6 multiply_reduce_fusion.7
  369.4 16.9 %cross_back.1 = (bf16[2,128,768]{2,1,0:T(8,128)(2,1)S(1)}, bf16[2,1024,1536]{2,1,0:T(8,128)(2,1)}) custom-call(bf16[2,128,768]{2,1,0:T(8,128)(2,1)S(1)} %bitcast.173, bf16[2,1024,1536]{2,1,0:T(8,128)(2,1)} %bitcast.242, f32[2,12,128]{2,1,0:T(8,128)S(1)} %get-tuple-element.123.log_ref, bf16[2,128,768]{2,1,0:T(8,128)(2,1)S(1)} %bitcast.169), custom_call_target="tpu_custom_call" | custom-call | flops 9663676416 | bytes 12582912 | tf_op jit(solution)/shard_map/cross_back/pallas_call | solution.py:814
  386.3 7.9 convolution_convert_fusion.6
  410.6 9.9 %fusion.9 = bf16[768,9216]{1,0:T(8,128)(2,1)} fusion(bf16[768,9216]{1,0:T(8,128)(2,1)} %constant_dynamic-update-slice_fusion.8, bf16[2048,768]{1,0:T(8,128)(2,1)} %pad_maximum_fusion, bf16[2048,1536]{1,0:T(8,128)(2,1)} %bitcast.180), kind=kOutput, calls=%fused_computation.22 | convolution fusion | flops 4833017856 | bytes 11796480 | tf_op jit(solution)/shard_map/dot_general | solution.py:939
  421.8 3.8 fusion
  425.6 57.1 %scatter_sum.4 = (bf16[32,768]{1,0:T(8,128)(2,1)}, bf16[32,768]{1,0:T(8,128)(2,1)}) custom-call(bf16[32,32,768]{2,1,0:T(8,128)(2,1)} %bitcast.184, bf16[32,32,768]{2,1,0:T(8,128)(2,1)} %bitcast.183), custom_call_target="tpu_custom_call" | custom-call | bytes 3145728 | tf_op jit(solution)/shard_map/scatter_sum/pallas_call | solution.py:536
  482.7 29.5 %gather_all.5 = (bf16[32,32,768]{2,1,0:T(8,128)(2,1)}, bf16[32,32,768]{2,1,0:T(8,128)(2,1)}) custom-call(bf16[32,768]{1,0:T(8,128)(2,1)} %get-tuple-element.126.refs_0_, bf16[32,768]{1,0:T(8,128)(2,1)} %get-tuple-element.127.refs_1_), custom_call_target="tpu_custom_call" | custom-call | bytes 49152000 | tf_op jit(solution)/shard_map/gather_all/pallas_call | solution.py:221
  512.2 4.8 constant_dynamic-update-slice_fusion.6
  523.7 4.3 all-to-all-start.3
  532.5 8.6 %convert_reduce_fusion.1 = (f32[3072]{0:T(1024)}, bf16[512,3072]{1,0:T(8,128)(2,1)S(1)}) fusion(f32[512,3072]{1,0:T(8,128)} %get-tuple-element.196, f32[3072]{0:T(1024)S(1)} %bitcast.239, bf16[3072,768]{1,0:T(8,128)(2,1)} %bitcast.224, f32[512,768]{1,0:T(8,128)S(1)} %get-tuple-element.177), kind=kOutput, calls=%fused_computation.2 | convolution fusion | flops 2436756480 | bytes 15753216 | tf_op jit(solution)/shard_map/dot_general | solution.py:943
  551.3 4.4 convolution_convert_fusion
  555.7 5.2 convolution_convert_fusion.1
  581.2 26.1 %attend_back.3 = (f32[4,2,128,640]{3,2,1,0:T(8,128)}, bf16[4,2,128,384]{3,2,1,0:T(8,128)(2,1)}, bf16[4,2,128,384]{3,2,1,0:T(8,128)(2,1)}) custom-call(s32[2,1536,2]{2,1,0:T(8,128)} %copy-done, s32[2,2,512]{2,1,0:T(2,128)S(1)} %pad_add_fusion.3.refs_1_, bf16[4,2,128,640]{3,2,1,0:T(8,128)(2,1)S(1)} %bitcast.166, f32[2,3,512]{2,1,0:T(4,128)S(1)} %get-tuple-element.133.refs_3_, ...), custom_call_target="tpu_custom_call" | custom-call | flops 14495514624 | bytes 3932160 | tf_op jit(solution)/shard_map/attend_back/pallas_call | solution.py:723
  611.9 33.8 %attend_back.2 = bf16[4,2,256,640]{3,2,1,0:T(8,128)(2,1)S(1)} custom-call(s32[2,1024,2]{2,1,0:T(8,128)S(1)} %copy-done.2, s32[2,2,1024]{2,1,0:T(2,128)S(1)} %copy-done.4, bf16[4,2,256,640]{3,2,1,0:T(8,128)(2,1)} %bitcast.171, f32[2,3,1024]{2,1,0:T(4,128)S(1)} %get-tuple-element.132.refs_3_, bf16[4,2,256,192]{3,2,1,0:T(8,128)(2,1)S(1)} %copy.121.refs_4_), custom_call_target="tpu_custom_call" | custom-call | flops 19327352832 | bytes 7864320 | tf_op jit(solution)/shard_map/attend_back/pallas_call | solution.py:723
  645.8 5.4 convolution_convert_fusion.4
  662.1 3.8 convolution_convert_fusion.7
  671.2 118.4 %scatter_sum.5 = (f32[24,2560]{1,0:T(8,128)}, f32[24,768]{1,0:T(8,128)}, f32[24,3072]{1,0:T(8,128)}, f32[96,768]{1,0:T(8,128)}, f32[32,128]{1,0:T(8,128)}, /*ind...) custom-call(bf16[32,24,2560]{2,1,0:T(8,128)(2,1)} %bitcast.178, ...), custom_call_target="tpu_custom_call" | custom-call | bytes 19922944 | tf_op jit(solution)/shard_map/scatter_sum/pallas_call | solution.py:536
  (415 shorter events, 159.7 us)
Async XLA Ops:
  7.3 251.3 %all-gather.3.cloned.1.call-start = ((), (), s32[]{:S(2)}) async-start(), calls=%async_computation.5 | async-start | bytes 15003648 | tf_op jit(solution)/shard_map/all_gather | solution.py:1082
  10.4 106.2 %copy-start.70 = (s32[2,16]{1,0:T(2,128)S(1)}, s32[2,16]{1,0:T(2,128)}, u32[]{:S(2)}) copy-start(s32[2,16]{1,0:T(2,128)} %param.24) | copy-start | bytes 388
  12.5 102.2 %copy-start.36 = (bf16[24,9472]{1,0:T(8,128)(2,1)}, bf16[24,9472]{1,0:T(8,128)(2,1)S(1)}, u32[]{:S(2)}) copy-start(bf16[24,9472]{1,0:T(8,128)(2,1)S(1)} %constant_dynamic-update-slice_fusion) | copy-start | bytes 1363972
  122.9 28.1 %copy-start.5 = (bf16[2048,640]{1,0:T(8,128)(2,1)}, bf16[2048,640]{1,0:T(8,128)(2,1)S(1)}, u32[]{:S(2)}) copy-start(bf16[2048,640]{1,0:T(8,128)(2,1)S(1)} %add_convert_fusion.1) | copy-start | bytes 7864324
  152.4 16.3 %copy-start.35 = (bf16[2,256,768]{2,1,0:T(8,128)(2,1)S(1)}, bf16[2,256,768]{2,1,0:T(8,128)(2,1)}, u32[]{:S(2)}) copy-start(bf16[2,256,768]{2,1,0:T(8,128)(2,1)} %refs_5_.1) | copy-start | bytes 2359300
  152.4 16.3 %copy-start.75 = (bf16[32,24,768]{2,1,0:T(8,128)(2,1)S(1)}, bf16[32,24,768]{2,1,0:T(8,128)(2,1)}, u32[]{:S(2)}) copy-start(bf16[32,24,768]{2,1,0:T(8,128)(2,1)} %get-tuple-element.92) | copy-start | bytes 3538948
  152.4 15.3 %all-to-all-start = ((bf16[4,2,256,192]{2,3,1,0:T(8,128)(2,1)}), bf16[4,2,256,192]{2,3,1,0:T(8,128)(2,1)S(1)}, u32[]{:S(2)}, u32[]{:S(2)}) async-start(bf16[4,2,256,192]{2,3,1,0:T(8,128)(2,1)} %copy.110), calls=%async_computation | async-start | bytes 1572864 | tf_op jit(solution)/shard_map/all_to_all | solution.py:1008
  156.0 193.1 %all-gather.5.cloned.1.call-start = ((), (), s32[]{:S(2)}) async-start(), calls=%async_computation.6 | async-start | bytes 4866048 | tf_op jit(solution)/shard_map/all_gather | solution.py:1083
  261.2 8.4 %copy-start.49 = (f32[1,1536]{1,0:T(1,128)S(1)}, f32[1,1536]{1,0:T(1,128)}, u32[]{:S(2)}) copy-start(f32[1,1536]{1,0:T(1,128)} %get-tuple-element.114) | copy-start | bytes 18436
  264.0 26.6 %collective-permute-start = (bf16[4,2,128,384]{3,2,1,0:T(8,128)(2,1)}, bf16[4,2,128,384]{3,2,1,0:T(8,128)(2,1)}, u32[]{:S(2)}, u32[]{:S(2)}) collective-permute-start(bf16[4,2,128,384]{3,2,1,0:T(8,128)(2,1)} %slice.134), channel_id=1, source_target_pairs={{0,8},{4,12},{8,16},{12,20},{16,24},{20,28},{1,9},{5,13},{9,17},{1... | collective-permute-start | bytes 2359304 | tf_op jit(solution)/shard_map/ppermute | solution.py:1020
  266.2 24.4 %collective-permute-start.1 = (bf16[4,2,128,384]{3,2,1,0:T(8,128)(2,1)}, bf16[4,2,128,384]{3,2,1,0:T(8,128)(2,1)}, u32[]{:S(2)}, u32[]{:S(2)}) collective-permute-start(bf16[4,2,128,384]{3,2,1,0:T(8,128)(2,1)} %slice.134), channel_id=1, source_target_pairs={{0,4},{4,8},{8,12},{12,16},{16,20},{20,24},{24,28},{1,5},{5,9},{9,... | collective-permute-start | bytes 2359304 | tf_op jit(solution)/shard_map/ppermute | solution.py:1020
  271.4 41.6 %copy-start = (s32[2,1536,2]{2,1,0:T(8,128)}, s32[2,1536,2]{2,1,0:T(8,128)S(1)}, u32[]{:S(2)}) copy-start(s32[2,1536,2]{2,1,0:T(8,128)S(1)} %pad_add_fusion.refs_0_) | copy-start | bytes 73732
  313.9 13.0 %all-to-all-start.1 = ((bf16[4,2,128,192]{2,3,1,0:T(8,128)(2,1)}), bf16[4,2,128,192]{2,3,1,0:T(8,128)(2,1)S(1)}, u32[]{:S(2)}, u32[]{:S(2)}) async-start(bf16[4,2,128,192]{2,3,1,0:T(8,128)(2,1)} %copy.113), calls=%async_computation.1 | async-start | bytes 786432 | tf_op jit(solution)/shard_map/all_to_all | solution.py:1008
  317.4 486.8 %reduce-scatter.2.cloned.1.call-start = ((), (), s32[]{:S(2)}) async-start(), calls=%async_computation.7 | async-start | bytes 14598144 | tf_op jit(solution)/shard_map/reduce_scatter | solution.py:1177
  365.7 20.5 %copy-start.14 = (f32[256,768]{1,0:T(8,128)}, f32[256,768]{1,0:T(8,128)S(1)}, u32[]{:S(2)}) copy-start(f32[256,768]{1,0:T(8,128)S(1)} %get-tuple-element.173) | copy-start | bytes 2359300
  410.6 9.9 %copy-start.22 = (bf16[768,768]{1,0:T(8,128)(2,1)S(1)}, bf16[768,768]{1,0:T(8,128)(2,1)}, u32[]{:S(2)}) copy-start(bf16[768,768]{1,0:T(8,128)(2,1)} %copy.117) | copy-start | bytes 3538948
  410.6 11.2 %copy-start.30 = (f32[256,768]{1,0:T(8,128)S(1)}, f32[256,768]{1,0:T(8,128)}, u32[]{:S(2)}) copy-start(f32[256,768]{1,0:T(8,128)} %copy-done.28) | copy-start | bytes 2359300
  410.6 11.2 %copy-start.80 = (bf16[256,3072]{1,0:T(8,128)(2,1)S(1)}, bf16[256,3072]{1,0:T(8,128)(2,1)}, u32[]{:S(2)}) copy-start(bf16[256,3072]{1,0:T(8,128)(2,1)} %copy-done.79) | copy-start | bytes 4718596
  520.5 54.5 %copy-start.12 = (f32[256,768]{1,0:T(8,128)}, f32[256,768]{1,0:T(8,128)S(1)}, u32[]{:S(2)}) copy-start(f32[256,768]{1,0:T(8,128)S(1)} %get-tuple-element.175) | copy-start | bytes 2359300
  523.7 52.9 %all-to-all-start.3 = ((bf16[4,2,128,192]{2,3,1,0:T(8,128)(2,1)}), bf16[4,2,128,192]{2,3,1,0:T(8,128)(2,1)}, u32[]{:S(2)}, u32[]{:S(2)}) async-start(bf16[4,2,128,192]{2,3,1,0:T(8,128)(2,1)} %copy.124), calls=%async_computation.3 | async-start | bytes 786432 | tf_op jit(solution)/shard_map/all_to_all | solution.py:1015
  531.4 9.7 %slice-start.2 = ((s8[4718592]{0:T(1024)(128)(4,1)}), s8[4194304]{0:T(1024)(128)(4,1)S(1)}, s32[]{:S(2)}) async-start(s8[4718592]{0:T(1024)(128)(4,1)} %bitcast.221), calls=%async_computation.10 | async-start | bytes 8388608
  532.5 8.6 %copy-start.19 = (f32[512,768]{1,0:T(8,128)S(1)}, f32[512,768]{1,0:T(8,128)}, u32[]{:S(2)}) copy-start(f32[512,768]{1,0:T(8,128)} %copy-done.18) | copy-start | bytes 4718596
  532.5 8.6 %slice-start.3 = ((s8[4718592]{0:T(1024)(128)(4,1)}), s8[524288]{0:T(1024)(128)(4,1)S(1)}, s32[]{:S(2)}) async-start(s8[4718592]{0:T(1024)(128)(4,1)} %bitcast.221), calls=%async_computation.11 | async-start | bytes 1048576
  532.5 16.6 %slice-start = ((s8[6291456]{0:T(1024)(128)(4,1)}), s8[4194304]{0:T(1024)(128)(4,1)S(1)}, s32[]{:S(2)}) async-start(s8[6291456]{0:T(1024)(128)(4,1)} %bitcast.181), calls=%async_computation.8 | async-start | bytes 8388608
  541.1 8.0 slice-start.1
  560.9 14.1 %copy-start.33 = (bf16[2,128,4,192]{1,0,3,2:T(2,128)(2,1)S(1)}, bf16[2,128,4,192]{1,0,3,2:T(2,128)(2,1)}, u32[]{:S(2)}) copy-start(bf16[2,128,4,192]{1,0,3,2:T(2,128)(2,1)} %copy-done.32) | copy-start | bytes 1179652
  576.5 34.9 %all-to-all-start.2 = ((bf16[4,2,256,192]{2,3,1,0:T(8,128)(2,1)}), bf16[4,2,256,192]{2,3,1,0:T(8,128)(2,1)S(1)}, u32[]{:S(2)}, u32[]{:S(2)}) async-start(bf16[4,2,256,192]{2,3,1,0:T(8,128)(2,1)} %copy.119), calls=%async_computation.2 | async-start | bytes 1572864 | tf_op jit(solution)/shard_map/all_to_all | solution.py:1015
  607.4 48.5 %collective-permute-start.2 = (bf16[4,2,128,384]{3,2,1,0:T(8,128)(2,1)}, bf16[4,2,128,384]{3,2,1,0:T(8,128)(2,1)}, u32[]{:S(2)}, u32[]{:S(2)}) collective-permute-start(bf16[4,2,128,384]{3,2,1,0:T(8,128)(2,1)} %get-tuple-element.134), channel_id=1, source_target_pairs={{8,0},{12,4},{16,8},{20,12},{24,16},{28,20},{9,1},{13,5},{17,9},{2... | collective-permute-start | bytes 2359304 | tf_op jit(solution)/shard_map/ppermute | solution.py:1025
  608.8 47.0 %collective-permute-start.3 = (bf16[4,2,128,384]{3,2,1,0:T(8,128)(2,1)}, bf16[4,2,128,384]{3,2,1,0:T(8,128)(2,1)}, u32[]{:S(2)}, u32[]{:S(2)}) collective-permute-start(bf16[4,2,128,384]{3,2,1,0:T(8,128)(2,1)} %get-tuple-element.135), channel_id=1, source_target_pairs={{4,0},{8,4},{12,8},{16,12},{20,16},{24,20},{28,24},{5,1},{9,5},{13... | collective-permute-start | bytes 2359304 | tf_op jit(solution)/shard_map/ppermute | solution.py:1025
  611.4 50.6 %copy-start.20 = (bf16[4,2,128,256]{3,2,1,0:T(8,128)(2,1)}, bf16[4,2,128,256]{3,2,1,0:T(8,128)(2,1)S(1)}, u32[]{:S(2)}) copy-start(bf16[4,2,128,256]{3,2,1,0:T(8,128)(2,1)S(1)} %slice.180) | copy-start | bytes 1572868
  791.8 8.8 %copy-start.13 = (f32[256,768]{1,0:T(8,128)S(1)}, f32[256,768]{1,0:T(8,128)}, u32[]{:S(2)}) copy-start(f32[256,768]{1,0:T(8,128)} %copy-done.12) | copy-start | bytes 2359300
  804.2 7.8 copy-start.41
  (71 other events, 308.6 us)
Sparse Core Ops, SparseCore 0:
  114.9 124.2 all-gather.2
  242.1 72.8 all-gather.4
  517.1 179.9 reduce-scatter.1

commit v3 on v2

--- a/solution.py
+++ b/solution.py
@@ -36,7 +36,7 @@
     return ((z * 2 + y) * 2 + x) * 2 + c
 
 
-def greet(z, y, x, c):
+def greet(z, y, x, c, ahead=False):
     barrier = pltpu.get_barrier_semaphore()
     def tell(who):
         pl.semaphore_signal(barrier, inc=1, device_id=who, device_id_type=MESH)
@@ -49,15 +49,29 @@
     @pl.when(z < 3)
     def _():
         tell(device(z + 1, y, x, c))
-    pl.semaphore_wait(barrier, 3 + (z + 2) // 3 + (5 - z) // 3)
-
-
-def gather_kernel(count, shared, orders, *refs):
+    if ahead:
+
+        @pl.when((y == 1) & (z < 3))
+        def _():
+            tell(device(z + 1, 0, x, c))
+
+        @pl.when((y == 0) & (z > 0))
+        def _():
+            tell(device(z - 1, 1, x, c))
+
+    below, above = (z + 2) // 3, (5 - z) // 3
+    count = 3 + below + above
+    if ahead:
+        count = count + y * above + (1 - y) * below
+    pl.semaphore_wait(barrier, count)
+
+
+def gather_kernel(count, shared, reach, orders, *refs):
     every = count + shared
-    ins, outs = refs[:every], refs[every : 2 * every]
-    own_sem, recv_sem, send_sem, group_recv, group_send = refs[2 * every :]
+    ins, outs, refs = refs[:every], refs[every : 2 * every + reach], refs[2 * every + reach :]
+    own_sem, recv_sem, send_sem, group_recv, group_send, ahead_send = refs
     z, y, x, c = place()
-    greet(z, y, x, c)
+    greet(z, y, x, c, reach > 0)
     here = [(x, y) if order in "xX" else (y, x) for order in orders]
 
     def shard_of(a, zo, f, l):
@@ -121,10 +135,44 @@
         )
 
     over, beside = device(z, y, 1 - x, c), device(z, y, x, 1 - c)
+    seq = z * 2 + y
+
+    def ahead_copy(by):
+        return pltpu.make_async_remote_copy(
+            src_ref=ins[every - 1],
+            dst_ref=outs[every + by - 1].at[x * 2 + c],
+            send_sem=ahead_send.at[by - 1],
+            recv_sem=group_recv.at[shared + by - 1, x * 2 + c],
+            device_id=(seq + by, x * 2 + c),
+            device_id_type=MESH,
+        )
+
+    def spread(b, source):
+        group_copy(b, source, x, c, 0, over).start()
+        group_copy(b, source, x, c, 1, beside).start()
+
+    def spread_on(b):
+        landed = outs[count + b].at[(1 - x) * 2 + c]
+        group_copy(b, landed, 1 - x, c, 2, beside).wait_recv()
+        group_copy(b, landed, 1 - x, c, 2, beside).start()
+
+    def spread_done(b, source):
+        landed = outs[count + b].at[(1 - x) * 2 + c]
+        group_copy(b, source, x, 1 - c, 1, beside).wait_recv()
+        group_copy(b, source, 1 - x, 1 - c, 1, beside).wait_recv()
+        group_copy(b, source, x, c, 0, over).wait_send()
+        group_copy(b, source, x, c, 1, beside).wait_send()
+        group_copy(b, landed, 1 - x, c, 2, beside).wait_send()
+
+    for by in range(1, reach + 1):
+
+        @pl.when(seq + by <= 7)
+        def _():
+            ahead_copy(by).start()
+
     kept = []
     for b in range(shared):
-        group_copy(b, ins[count + b], x, c, 0, over).start()
-        group_copy(b, ins[count + b], x, c, 1, beside).start()
+        spread(b, ins[count + b])
         kept.append(
             pltpu.make_async_copy(
                 ins[count + b], outs[count + b].at[x * 2 + c], own_sem.at[count + b]
@@ -142,9 +190,14 @@
     from_last(z, False)
     from_last(z, True)
     for b in range(shared):
-        landed = outs[count + b].at[(1 - x) * 2 + c]
-        group_copy(b, landed, 1 - x, c, 2, beside).wait_recv()
-        group_copy(b, landed, 1 - x, c, 2, beside).start()
+        spread_on(b)
+    for by in range(1, reach + 1):
+
+        @pl.when(seq >= by)
+        def _():
+            ahead_copy(by).wait_recv()
+            spread(shared + by - 1, outs[every + by - 1].at[x * 2 + c])
+
     for distance in (1, 2, 3):
         for below in (True, False):
 
@@ -178,13 +231,19 @@
         return carry
 
     lax.fori_loop(0, 16, cores, 0)
+    for by in range(1, reach + 1):
+
+        @pl.when(seq >= by)
+        def _():
+            spread_on(shared + by - 1)
+            spread_done(shared + by - 1, outs[every + by - 1].at[x * 2 + c])
+
+        @pl.when(seq + by <= 7)
+        def _():
+            ahead_copy(by).wait_send()
+
     for b in range(shared):
-        first, landed = ins[count + b], outs[count + b].at[(1 - x) * 2 + c]
-        group_copy(b, first, x, 1 - c, 1, beside).wait_recv()
-        group_copy(b, first, 1 - x, 1 - c, 1, beside).wait_recv()
-        group_copy(b, first, x, c, 0, over).wait_send()
-        group_copy(b, first, x, c, 1, beside).wait_send()
-        group_copy(b, landed, 1 - x, c, 2, beside).wait_send()
+        spread_done(b, ins[count + b])
     for copied in kept:
         copied.wait()
     for a in range(count):
@@ -213,22 +272,25 @@
     return pl.CostEstimate(flops=0, transcendentals=0, bytes_accessed=size * share)
 
 
-def gather_all(arrays, orders, collective_id, group_arrays=()):
+def gather_all(arrays, orders, collective_id, group_arrays=(), reach=0):
     count, shared = len(arrays), len(group_arrays)
     every = [*arrays, *group_arrays]
-    copies = [32] * count + [4] * shared
+    results = [(32, v) for v in arrays] + [(4, v) for v in group_arrays]
+    results += [(4, v) for v in every[-1:] * reach]
+    spreads = max(shared + reach, 1)
     D = pltpu.SemaphoreType.DMA
     return pl.pallas_call(
-        functools.partial(gather_kernel, count, shared, orders),
-        out_shape=[jax.ShapeDtypeStruct((n,) + v.shape, v.dtype) for n, v in zip(copies, every)],
+        functools.partial(gather_kernel, count, shared, reach, orders),
+        out_shape=[jax.ShapeDtypeStruct((n,) + v.shape, v.dtype) for n, v in results],
         in_specs=[pl.BlockSpec(memory_space=pl.ANY)] * len(every),
-        out_specs=[pl.BlockSpec(memory_space=pl.ANY)] * len(every),
+        out_specs=[pl.BlockSpec(memory_space=pl.ANY)] * len(results),
         scratch_shapes=[
             D((len(every),)),
             D((count, 32)),
             D((count, 5, 16)),
-            D((max(shared, 1), 4)),
-            D((max(shared, 1), 3)),
+            D((spreads, 4)),
+            D((spreads, 3)),
+            D((max(reach, 1),)),
         ],
         compiler_params=pltpu.CompilerParams(collective_id=collective_id, has_side_effects=True),
         cost_estimate=traffic(arrays, 500),
@@ -551,12 +613,12 @@
     return lax.axis_size("seq") == 8 and lax.axis_size("head") == 4
 
 
-def gather(arrays, orders, collective_id, group_arrays=()):
+def gather(arrays, orders, collective_id, group_arrays=(), reach=0):
     if known_mesh():
-        return gather_all(arrays, orders, collective_id, group_arrays)
-    return [lax.all_gather(v, EVERY, axis=0, tiled=False) for v in arrays] + [
-        lax.all_gather(v, "head", axis=0, tiled=False) for v in group_arrays
-    ]
+        return gather_all(arrays, orders, collective_id, group_arrays, reach)
+    every = [lax.all_gather(v, EVERY, axis=0, tiled=False) for v in arrays]
+    group = [lax.all_gather(v, "head", axis=0, tiled=False) for v in group_arrays]
+    return every + group + [from_before(group[-1], by) for by in range(1, reach + 1)]
 
 
 def scatter(arrays, orders, collective_id, out_dtype=F32, group_arrays=()):
@@ -625,13 +687,15 @@
         fill(value_s, (*prior, own_ref), slice(h * 128 + 64, h * 128 + 128))
         at = heads * 128 + h * 64
         fill(query_s, (own_ref,), slice(at, at + 64), 0.125)
+        values = value_s[...].T
 
         def step(i, carry):
             start = pl.multiple_of(i * tile, tile)
             allowed = allowed_pairs(key_ref, query_ref, start, tile, causal)
             scores = across(key_s[...], query_s[pl.ds(start, tile), :])
             probs, log_total = soft_columns(jnp.where(allowed, scores, NEGATIVE))
-            result_s[pl.ds(start, tile), :] = down(probs.astype(BF16), value_s[...]).astype(BF16)
+            made = jnp.dot(values, probs.astype(BF16), preferred_element_type=F32)
+            result_s[pl.ds(start, tile), :] = made.astype(BF16).T
             log_ref[0, h : h + 1, pl.ds(start, tile)] = log_total
             return carry
 
@@ -690,6 +754,7 @@
         fill(grad_s, (grad_ref,), slice(h * 64, h * 64 + 64))
         gk_s[...] = jnp.zeros_like(gk_s)
         gv_s[...] = jnp.zeros_like(gv_s)
+        keys = key_s[...].T
 
         def step(i, carry):
             start = pl.multiple_of(i * tile, tile)
@@ -701,7 +766,8 @@
             grad_scores = score_grads(probs, across(value_s[...], grad_out))
             gv_s[...] += jnp.dot(probs.astype(BF16), grad_out, preferred_element_type=F32)
             gk_s[...] += jnp.dot(grad_scores, query, preferred_element_type=F32)
-            result_s[here, :] = down(grad_scores, key_s[...]) * 0.125
+            made = jnp.dot(keys, grad_scores, preferred_element_type=F32)
+            result_s[here, :] = made.T * 0.125
             return carry
 
         lax.fori_loop(0, group // tile, step, 0)
@@ -800,9 +866,10 @@
             grad_scores = score_grads(probs, across(values, grad_out))
             value_parts.append(jnp.dot(probs.astype(BF16), grad_out, preferred_element_type=F32))
             key_parts.append(jnp.dot(grad_scores, query, preferred_element_type=F32))
-            query_parts.append(down(grad_scores, keys) * 0.125)
+            query_parts.append(jnp.dot(keys.T, grad_scores, preferred_element_type=F32))
         cut = slice(i * 128, i * 128 + 128)
-        grad_query_ref[0, :, cut] = jnp.concatenate(query_parts, axis=1).astype(BF16)
+        made = jnp.concatenate(query_parts, axis=0).T * 0.125
+        grad_query_ref[0, :, cut] = made.astype(BF16)
         grad_pairs_ref[0, :, cut] = jnp.concatenate(key_parts, axis=1).astype(BF16)
         cut = slice(D + i * 128, D + i * 128 + 128)
         grad_pairs_ref[0, :, cut] = jnp.concatenate(value_parts, axis=1).astype(BF16)
@@ -885,10 +952,10 @@
             full[row + 1 : row + 2, cut] = source[:, value_at : value_at + 64]
     for source, row in ((e_hidden, 6), (d_hidden, 23)):
         for k in range(FF // D):
-            full[row + k : row + k + 1, :] = source[:, k * D : k * D + D]
-    full[20:21, :] = pair_sum[:, D:]
+            full[row + k : row + k + 1, :] = source[k * D : k * D + D].reshape(1, D)
+    full[20:21, :] = pair_sum[D:].reshape(1, D)
     for source, row in zip(singles, SINGLES):
-        full[row : row + 1, :] = source[...]
+        full[row : row + 1, :] = source[...].reshape(1, D)
     out_ref[...] = jnp.zeros_like(out_ref)
     for d in range(out_ref.shape[0]):
         out_ref[d, :, 0:width] = full[:, d * width : d * width + width].astype(BF16)
@@ -903,6 +970,36 @@
     )(*vectors)
 
 
+def finish_kernel(heads, *refs):
+    late, pack, outs = refs[:7], refs[7], refs[8:]
+    for k in (0, 4):
+        for head in range(HEADS):
+            value_at, query_at = head_places(head, heads)
+            for n, at in enumerate((query_at, value_at - 64, value_at)):
+                start = head * 192 + n * 64
+                outs[k][:, start : start + 64] = late[k][:, at : at + 64]
+    for k in (1, 2, 3, 5, 6):
+        outs[k][...] = late[k][...]
+    at = 0
+    for target in outs[7:]:
+        width = target.shape[1]
+        target[...] = pack[:, at : at + width].astype(F32)
+        at += width
+
+
+def finish(late, early, heads):
+    rows = late[0].shape[0]
+    shapes = [v.shape for v in late]
+    shapes[0] = shapes[4] = (rows, 3 * D)
+    shapes += [(rows, width) for width in (D, 2 * D, D, FF, FF)]
+    return pl.pallas_call(
+        functools.partial(finish_kernel, heads),
+        out_shape=[jax.ShapeDtypeStruct(shape, F32) for shape in shapes],
+        compiler_params=pltpu.CompilerParams(vmem_limit_bytes=48 << 20),
+        name="finish",
+    )(*late, early)
+
+
 def norm(resid, gain, shift):
     center = resid - jnp.mean(resid, axis=-1, keepdims=True)
     scale = lax.rsqrt(jnp.mean(center * center, axis=-1, keepdims=True) + EPSILON)
@@ -918,8 +1015,7 @@
         - jnp.mean(inner, axis=-1, keepdims=True)
         - hat * jnp.mean(inner * hat, axis=-1, keepdims=True)
     )
-    gain_sum = jnp.sum(grad * hat, axis=0, keepdims=True)
-    return grad_resid, gain_sum, jnp.sum(grad, axis=0, keepdims=True)
+    return grad_resid, jnp.sum(grad * hat, axis=0), jnp.sum(grad, axis=0)
 
 
 def gelu(value):
@@ -944,7 +1040,7 @@
 
 
 def row_sum(value):
-    return jnp.sum(value.astype(F32), axis=0, keepdims=True)
+    return jnp.sum(value.astype(F32), axis=0)
 
 
 def doc_starts(lengths):
@@ -985,11 +1081,6 @@
     pairs = split[:, :, : heads * 128].reshape(rows, parts, heads, 2, HEAD_DIM)
     query = split[:, :, heads * 128 : heads * 192].reshape(rows, parts, heads, 1, HEAD_DIM)
     return jnp.concatenate([query, pairs], axis=3).reshape(rows, 3 * D)
-
-
-def to_beside_rows(grad, devices):
-    split = grad.reshape(devices, FF // D, -1, D)
-    return split.transpose(0, 2, 1, 3).reshape(D, FF)
 
 
 def my_columns(full, parts):
@@ -1063,11 +1154,12 @@
     small = jnp.pad(small, ((0, 32 - SMALL_ROWS), (0, 128 - small.shape[1])))
     encoder_full = gather(
         [by_group(encoder_qkv, parts), encoder_out, encoder_up, encoder_down, small],
-        "xyxyx",
+        "yxxxx",
         0,
         [source, target],
-    )
-    source_all, target_all = encoder_full[5:]
+        REACH,
+    )
+    source_all, target_all, *target_before = encoder_full[5:]
     decoder_parts = [
         by_group(decoder_qkv, parts),
         decoder_out,
@@ -1129,8 +1221,12 @@
     d_qkv_here = my_columns(d_qkv, parts)
     d_joined = (mm(target_all.reshape(-1, D), d_qkv_here) + my_columns(d_bias, parts)).astype(BF16)
     d_joined = d_joined.reshape(parts, micro, tgt_rows, -1)
-    d_pairs = d_joined[..., : heads * 128]
-    d_prior = [from_before(d_pairs, by) for by in range(REACH, 0, -1)]
+    pair_weights, pair_shift = d_qkv_here[:, : heads * 128], my_columns(d_bias, parts)[:, : heads * 128]
+    d_prior = []
+    for by in range(REACH, 0, -1):
+        before = (mm(target_before[by - 1].reshape(-1, D), pair_weights) + pair_shift).astype(BF16)
+        before = jnp.where(seq >= by, before, jnp.zeros_like(before))
+        d_prior.append(before.reshape(parts, micro, tgt_rows, -1))
     d_attended, d_logs = attend(d_joined, d_prior, *tgt_info, heads, True)
     d_mixed = to_tokens(d_attended)
     d_first, d_kept_one = norm(
@@ -1168,13 +1264,6 @@
     g_fetched = gather(scatter(g_fetched, "xy", 4, BF16), "xy", 5)
     w_c_pairs = mm_rows(fetched, g_pairs)
     w_c_query = mm_rows(d_first_low, g_queries)
-    decoder_grads = [w_c_query, w_c_pairs, w_c_out, w_d_up]
-    decoder_grads = [g.astype(BF16) for g in decoder_grads]
-    decoder_grads.append(to_beside_rows(w_d_down.astype(BF16), devices))
-    decoder_pack, *g_fetched = lax.optimization_barrier(
-        (jnp.concatenate(decoder_grads, axis=1), *g_fetched)
-    )
-    decoder_sums = lax.psum_scatter(decoder_pack, EVERY, scatter_dimension=0, tiled=True)
     g_first = g_sum_two + mm_back(g_queries, c_query)
     g_resid, d_gain_one, d_shift_one = norm_back(g_first, d_kept_one, d_g0)
     g_branch = g_resid.astype(BF16)
@@ -1201,6 +1290,11 @@
     ge_resid, e_gain_one, e_shift_one = norm_back(g_first, e_kept_one, e_g0)
     ge_branch = ge_resid.astype(BF16)
     w_e_out = mm_rows(e_mixed, ge_branch)
+    early_grads = [g.astype(BF16) for g in (w_c_query, w_c_pairs, w_c_out, w_d_up, w_e_up)]
+    early_pack, ge_branch = lax.optimization_barrier(
+        (jnp.concatenate(early_grads, axis=1), ge_branch)
+    )
+    early_sums = lax.psum_scatter(early_pack, EVERY, scatter_dimension=0, tiled=True)
     ge_mixed = mm_back(ge_branch, e_out).astype(BF16)
     ge_attended = to_heads(ge_mixed, parts, micro)
     (ge_joined,) = attend_back(
@@ -1221,16 +1315,11 @@
     def pieces(value):
         return value.astype(BF16).reshape(devices, value.shape[0] // devices, value.shape[1])
 
-    ends = [0]
-    for part in decoder_grads:
-        ends.append(ends[-1] + part.shape[1])
-    decoder_sums = [decoder_sums[:, start:end].astype(F32) for start, end in zip(ends, ends[1:])]
-    decoder_sums[4] = decoder_sums[4].reshape(-1, FF // D, D).transpose(1, 0, 2).reshape(-1, D)
     small_grads = pack_small(
         [
-            all_columns(row_sum(ge_joined), parts),
+            all_columns(row_sum(ge_joined)[None], parts),
             row_sum(ge_hidden),
-            all_columns(row_sum(g_joined), parts),
+            all_columns(row_sum(g_joined)[None], parts),
             row_sum(g_hidden),
             row_sum(g_pairs),
             row_sum(ge_branch),
@@ -1253,34 +1342,54 @@
         devices,
         heads,
     )
-    encoder_sums = scatter(
+    late_sums = scatter(
         [
             pieces(all_columns(w_e_qkv.astype(BF16), parts)),
             pieces(w_e_out),
-            pieces(w_e_up),
             pieces(w_e_down),
             small_grads,
             pieces(all_columns(w_d_qkv.astype(BF16), parts)),
             pieces(w_d_out),
+            pieces(w_d_down),
         ],
-        "xyyxxyx",
+        "xyxyyxy",
         7,
         F32,
         [v.reshape(parts, -1, D) for v in (g_source_all, g_target_all)],
     )
-    g_source, g_target = ge_resid + encoder_sums[7], g_resid + encoder_sums[8]
-    small_sums = encoder_sums[4][:, : encoder_gains.shape[1]]
+    g_source, g_target = ge_resid + late_sums[7], g_resid + late_sums[8]
+    (
+        e_qkv_sum,
+        e_out_sum,
+        e_down_sum,
+        small_sums,
+        d_qkv_sum,
+        d_out_sum,
+        d_down_sum,
+        c_query_sum,
+        c_pairs_sum,
+        c_out_sum,
+        d_up_sum,
+        e_up_sum,
+    ) = finish(late_sums[:7], early_sums, heads)
+    small_sums = small_sums[:, : encoder_gains.shape[1]]
     return (
         decoded.reshape(micro, tgt_rows, D),
         g_source.reshape(micro, src_rows, D),
         g_target.reshape(micro, tgt_rows, D),
-        by_head(encoder_sums[0], parts),
-        *encoder_sums[1:4],
+        e_qkv_sum,
+        e_out_sum,
+        e_up_sum,
+        e_down_sum,
         small_sums[0:2],
         small_sums[2:12],
-        by_head(encoder_sums[5], parts),
-        encoder_sums[6],
-        *decoder_sums,
+        d_qkv_sum,
+        d_out_sum,
+        c_query_sum,
+        c_pairs_sum,
+        c_out_sum,
+        d_up_sum,
+        d_down_sum,
         small_sums[12:15],
         small_sums[15:SMALL_ROWS],
     )

time: 825 us -> 778 us (0.943)
  local copies, waits for them, and re-layouts: 81.2 us -> 44.2 us
  waiting for transfers between devices: 30 us -> 17.9 us
    ppermute x2 -> x0, waiting for transfers between devices: 19.2 us -> none  [from_before(): return lax.ppermute(value, 'seq', [(i, i + by) for i in range(count - by)])]
    broadcast_in_dim x17 -> x0, local copies, waits for them, and re-layouts: 9.99 us -> none  [the longest x7 4.11 us: row_sum(): return jnp.sum(value.astype(F32), axis=0, keepdims=True)]
    pallas_call x3 -> x4, Pallas kernels: 161 us -> 167 us  [the longest x3 166 us: gather_all(): pl.pallas_call(functools.partial(gather_kernel, count, shared, reach, ord...]
    unnamed x200 -> x229, local copies, waits for them, and re-layouts: 22.2 us -> 16.8 us
    dot_general x11 -> x13, matrix products: 42.9 us -> 45 us  [mm(): return jnp.dot(left, right, preferred_element_type=F32)]
  transfers between devices with their start and end apart: 11 -> 9, of which waited for: 2 -> 3; matrix products, arithmetic and copies ran while one was open for 18% -> 14% of each run, Pallas kernels for 38% -> 43%
where the time goes in v3:
time: 778 us; the launch traced here: 773 us
  Pallas kernels  515 us (66%)
  matrix products  131 us (17%)
  local copies, waits for them, and re-layouts  44.2 us (6%)
  other arithmetic  29.2 us (4%)
  starting transfers between devices  19.1 us (2%)
  waiting for transfers between devices  17.9 us (2%)
  between operations  15.9 us (2%)
    pallas_call x3, Pallas kernels, scatter_sum(): pl.pallas_call(functools.partial(scatter_kernel, count, shared, orders),...  220 us
    pallas_call x3, Pallas kernels, gather_all(): pl.pallas_call(functools.partial(gather_kernel, count, shared, reach, ord...  166 us
    pallas_call x2, Pallas kernels, attend_back(): pl.pallas_call(functools.partial(attend_back_kernel, heads, tile, causal,...  54.3 us
    dot_general x11, matrix products, mm_back(): lax.dot_general(left, right, (((1,), (1,)), ((), ())), preferred_element_...  46 us
    pallas_call x2, Pallas kernels, attend(): pl.pallas_call(functools.partial(attend_kernel, heads, tile, causal), gri...  45.5 us
    dot_general x13, matrix products, mm(): return jnp.dot(left, right, preferred_element_type=F32)  45 us
    dot_general x11, matrix products, mm_rows(): lax.dot_general(left, right, (((0,), (0,)), ((), ())), preferred_element_...  35.6 us
    unnamed x229, local copies, waits for them, and re-layouts  16.8 us
  transfers between devices with their start and end apart: 9, of which 3 were waited for; matrix products, arithmetic and copies ran while one was open for 14% of the time, Pallas kernels for 43%

profile of v3, /device:TPU:0, one launch (start us, length us, event | category | flops | bytes accessed | tf_op | source)
XLA Modules:
  0.0 772.8 jit_solution(390973259067551908)
XLA Ops:
  13.3 109.4 %gather_all.3 = (bf16[32,24,2560]{2,1,0:T(8,128)(2,1)}, bf16[32,24,768]{2,1,0:T(8,128)(2,1)}, bf16[32,24,3072]{2,1,0:T(8,128)(2,1)}, bf16[32,96,768]{2,1,0:T(8,1...) custom-call(bf16[24,2560]{1,0:T(8,128)(2,1)} %bitcast.210, ...), custom_call_target="tpu_custom_call" | custom-call | bytes 231424000 | tf_op jit(solution)/shard_map/gather_all/pallas_call | solution.py:282
  126.3 4.8 add_convert_fusion.1
  131.1 25.5 %attend.2 = (bf16[4,2,256,192]{3,2,1,0:T(8,128)(2,1)S(1)}, f32[2,3,1024]{2,1,0:T(4,128)S(1)}) custom-call(s32[2,1024,2]{2,1,0:T(8,128)S(1)} %copy.93.refs_0_, s32[2,2,1024]{2,1,0:T(2,128)S(1)} %pad_add_fusion.2.refs_1_, bf16[4,2,256,640]{3,2,1,0:T(8,128)(2,1)S(1)} %bitcast.166), custom_call_target="tpu_custom_call" | custom-call | flops 12884901888 | bytes 5242880 | tf_op jit(solution)/shard_map/attend/pallas_call | solution.py:719
  158.1 4.2 all-to-all-start
  166.7 10.9 %all-to-all-done = bf16[4,2,256,192]{2,3,1,0:T(8,128)(2,1)} async-done(((bf16[4,2,256,192]{2,3,1,0:T(8,128)(2,1)}), bf16[4,2,256,192]{2,3,1,0:T(8,128)(2,1)}, u32[]{:S(2)}, u32[]{:S(2)}) %all-to-all-start) | async-done | bytes 786464 | tf_op jit(solution)/shard_map/all_to_all | solution.py:1099
  181.2 7.4 multiply_convert_fusion.1
  195.8 40.7 %scatter_sum.3 = (bf16[32,768]{1,0:T(8,128)(2,1)}, bf16[32,768]{1,0:T(8,128)(2,1)}) custom-call(bf16[32,32,768]{2,1,0:T(8,128)(2,1)} %bitcast.186, bf16[32,32,768]{2,1,0:T(8,128)(2,1)} %bitcast.185), custom_call_target="tpu_custom_call" | custom-call | bytes 3145728 | tf_op jit(solution)/shard_map/scatter_sum/pallas_call | solution.py:598
  236.5 29.8 %gather_all.4 = (bf16[32,32,768]{2,1,0:T(8,128)(2,1)}, bf16[32,32,768]{2,1,0:T(8,128)(2,1)}) custom-call(bf16[32,768]{1,0:T(8,128)(2,1)} %get-tuple-element.115.refs_0_, bf16[32,768]{1,0:T(8,128)(2,1)} %get-tuple-element.116.refs_1_), custom_call_target="tpu_custom_call" | custom-call | bytes 49152000 | tf_op jit(solution)/shard_map/gather_all/pallas_call | solution.py:282
  266.3 3.8 pad_maximum_fusion
  278.1 20.0 %attend.3 = (bf16[4,2,128,192]{3,2,1,0:T(8,128)(2,1)S(1)}, f32[2,3,512]{2,1,0:T(4,128)S(1)}) custom-call(s32[2,1536,2]{2,1,0:T(8,128)S(1)} %pad_add_fusion.refs_0_, s32[2,2,512]{2,1,0:T(2,128)S(1)} %pad_add_fusion.3.refs_1_, bf16[4,2,128,640]{3,2,1,0:T(8,128)(2,1)S(1)} %bitcast.168, bf16[4,2,128,384]{3,2,1,0:T(8,128)(2,1)S(1)} %bitcast.172, ...), custom_call_target="tpu_custom_call" | custom-call | flops 9663676416 | bytes 2621440 | tf_op jit(solution)/shard_map/attend/pallas_call | solution.py:719
  302.7 9.1 %add_convert_fusion = bf16[2048,1536]{1,0:T(8,128)(2,1)} fusion(bf16[2048,768]{1,0:T(8,128)(2,1)} %pad_maximum_fusion, f32[1536]{0:T(1024)S(1)} %reduce.22, bf16[768,9472]{1,0:T(8,128)(2,1)} %all-gather.3.cloned.1.call-done), kind=kOutput, calls=%fused_computation.1 | convolution fusion | flops 4838129664 | bytes 11802624 | tf_op jit(solution)/shard_map/dot_general | solution.py:1031
  318.7 8.2 %cross.1 = (bf16[2,128,768]{2,1,0:T(8,128)(2,1)S(1)}, f32[2,12,128]{2,1,0:T(8,128)S(1)}) custom-call(bf16[2,128,768]{2,1,0:T(8,128)(2,1)S(1)} %bitcast.174, bf16[2,1024,1536]{2,1,0:T(8,128)(2,1)} %bitcast.239), custom_call_target="tpu_custom_call" | custom-call | flops 6442450944 | bytes 6291456 | tf_op jit(solution)/shard_map/cross/pallas_call | solution.py:839
  329.1 6.4 multiply_convert_fusion.2
  335.4 4.5 fusion.113
  345.7 5.2 multiply_reduce_fusion.7
  353.6 16.2 %cross_back.1 = (bf16[2,128,768]{2,1,0:T(8,128)(2,1)S(1)}, bf16[2,1024,1536]{2,1,0:T(8,128)(2,1)}) custom-call(bf16[2,128,768]{2,1,0:T(8,128)(2,1)S(1)} %bitcast.175, bf16[2,1024,1536]{2,1,0:T(8,128)(2,1)} %bitcast.240, f32[2,12,128]{2,1,0:T(8,128)S(1)} %get-tuple-element.138.log_ref, bf16[2,128,768]{2,1,0:T(8,128)(2,1)S(1)} %bitcast.163), custom_call_target="tpu_custom_call" | custom-call | flops 9663676416 | bytes 12582912 | tf_op jit(solution)/shard_map/cross_back/pallas_call | solution.py:881
  369.8 7.9 %convolution_convert_fusion.6 = bf16[2048,768]{1,0:T(8,128)(2,1)S(1)} fusion(bf16[2048,1536]{1,0:T(8,128)(2,1)} %bitcast.179, bf16[768,9472]{1,0:T(8,128)(2,1)} %all-gather.3.cloned.1.call-done), kind=kOutput, calls=%fused_computation.24 | convolution fusion | flops 4833411072 | bytes 11796480 | tf_op jit(solution)/shard_map/dot_general | solution.py:1039
  379.6 27.5 %scatter_sum.4 = (bf16[32,768]{1,0:T(8,128)(2,1)}, bf16[32,768]{1,0:T(8,128)(2,1)}) custom-call(bf16[32,32,768]{2,1,0:T(8,128)(2,1)} %bitcast.188, bf16[32,32,768]{2,1,0:T(8,128)(2,1)} %bitcast.187), custom_call_target="tpu_custom_call" | custom-call | bytes 3145728 | tf_op jit(solution)/shard_map/scatter_sum/pallas_call | solution.py:598
  407.1 26.6 %gather_all.5 = (bf16[32,32,768]{2,1,0:T(8,128)(2,1)}, bf16[32,32,768]{2,1,0:T(8,128)(2,1)}) custom-call(bf16[32,768]{1,0:T(8,128)(2,1)} %get-tuple-element.140.refs_0_, bf16[32,768]{1,0:T(8,128)(2,1)} %get-tuple-element.141.refs_1_), custom_call_target="tpu_custom_call" | custom-call | bytes 49152000 | tf_op jit(solution)/shard_map/gather_all/pallas_call | solution.py:282
  439.8 8.4 %convert_reduce_fusion.1 = (f32[3072]{0:T(1024)}, bf16[512,3072]{1,0:T(8,128)(2,1)S(1)}) fusion(f32[512,3072]{1,0:T(8,128)} %get-tuple-element.218, f32[3072]{0:T(1024)S(1)} %bitcast.237, bf16[3072,768]{1,0:T(8,128)(2,1)} %bitcast.220, f32[512,768]{1,0:T(8,128)S(1)} %get-tuple-element.203), kind=kOutput, calls=%fused_computation.2 | convolution fusion | flops 2436756480 | bytes 15753216 | tf_op jit(solution)/shard_map/dot_general | solution.py:1039
  448.2 4.8 multiply_reduce_fusion
  455.3 6.7 fusion.10
  463.7 3.8 fusion.1
  467.5 4.8 fusion
  496.6 4.4 convolution_convert_fusion.1
  507.0 4.5 all-to-all-start.2
  515.1 25.2 %attend_back.3 = (f32[4,2,128,640]{3,2,1,0:T(8,128)}, bf16[4,2,128,384]{3,2,1,0:T(8,128)(2,1)}, bf16[4,2,128,384]{3,2,1,0:T(8,128)(2,1)S(1)}) custom-call(s32[2,1536,2]{2,1,0:T(8,128)} %copy-done, s32[2,2,512]{2,1,0:T(2,128)S(1)} %pad_add_fusion.3.refs_1_, bf16[4,2,128,640]{3,2,1,0:T(8,128)(2,1)S(1)} %bitcast.169, ...), custom_call_target="tpu_custom_call" | custom-call | flops 14495514624 | bytes 3932160 | tf_op jit(solution)/shard_map/attend_back/pallas_call | solution.py:789
  546.1 29.0 %attend_back.2 = bf16[4,2,256,640]{3,2,1,0:T(8,128)(2,1)S(1)} custom-call(s32[2,1024,2]{2,1,0:T(8,128)S(1)} %copy-done.2, s32[2,2,1024]{2,1,0:T(2,128)S(1)} %copy-done.12, bf16[4,2,256,640]{3,2,1,0:T(8,128)(2,1)} %bitcast.167, f32[2,3,1024]{2,1,0:T(4,128)S(1)} %get-tuple-element.144.refs_3_, bf16[4,2,256,192]{3,2,1,0:T(8,128)(2,1)S(1)} %copy.104.refs_4_), custom_call_target="tpu_custom_call" | custom-call | flops 19327352832 | bytes 7864320 | tf_op jit(solution)/shard_map/attend_back/pallas_call | solution.py:789
  575.1 5.8 convolution_convert_fusion.4
  585.6 4.5 collective-permute-done
  595.1 3.8 convolution_convert_fusion.7
  604.2 151.7 %scatter_sum.5 = (f32[24,2560]{1,0:T(8,128)}, f32[24,768]{1,0:T(8,128)}, f32[96,768]{1,0:T(8,128)}, f32[32,128]{1,0:T(8,128)}, f32[24,2560]{1,0:T(8,128)}, /*ind...) custom-call(bf16[32,24,2560]{2,1,0:T(8,128)(2,1)} %bitcast.178, ...), custom_call_target="tpu_custom_call" | custom-call | bytes 19922944 | tf_op jit(solution)/shard_map/scatter_sum/pallas_call | solution.py:598
  (405 shorter events, 131.6 us)
Async XLA Ops:
  7.3 262.8 %all-gather.3.cloned.1.call-start = ((), (), s32[]{:S(2)}) async-start(), calls=%async_computation.5 | async-start | bytes 15003648 | tf_op jit(solution)/shard_map/all_gather | solution.py:1174
  10.3 112.5 %copy-start.84 = (s32[2,16]{1,0:T(2,128)S(1)}, s32[2,16]{1,0:T(2,128)}, u32[]{:S(2)}) copy-start(s32[2,16]{1,0:T(2,128)} %param.24) | copy-start | bytes 388
  12.5 110.2 %copy-start.53 = (bf16[24,9472]{1,0:T(8,128)(2,1)}, bf16[24,9472]{1,0:T(8,128)(2,1)S(1)}, u32[]{:S(2)}) copy-start(bf16[24,9472]{1,0:T(8,128)(2,1)S(1)} %constant_dynamic-update-slice_fusion) | copy-start | bytes 1363972
  131.0 25.5 %copy-start.13 = (bf16[2048,640]{1,0:T(8,128)(2,1)}, bf16[2048,640]{1,0:T(8,128)(2,1)S(1)}, u32[]{:S(2)}) copy-start(bf16[2048,640]{1,0:T(8,128)(2,1)S(1)} %add_convert_fusion.1) | copy-start | bytes 7864324
  156.7 8.3 %copy-start.69 = (f32[1,768]{1,0:T(1,128)S(1)}, f32[1,768]{1,0:T(1,128)}, u32[]{:S(2)}) copy-start(f32[1,768]{1,0:T(1,128)} %get-tuple-element.127) | copy-start | bytes 9220
  156.8 8.3 %copy-start.68 = (f32[1,768]{1,0:T(1,128)S(1)}, f32[1,768]{1,0:T(1,128)}, u32[]{:S(2)}) copy-start(f32[1,768]{1,0:T(1,128)} %get-tuple-element.131) | copy-start | bytes 9220
  156.8 8.3 %copy-start.67 = (f32[1,768]{1,0:T(1,128)S(1)}, f32[1,768]{1,0:T(1,128)}, u32[]{:S(2)}) copy-start(f32[1,768]{1,0:T(1,128)} %get-tuple-element.135) | copy-start | bytes 9220
  156.8 8.4 %copy-start.66 = (f32[1,768]{1,0:T(1,128)S(1)}, f32[1,768]{1,0:T(1,128)}, u32[]{:S(2)}) copy-start(f32[1,768]{1,0:T(1,128)} %get-tuple-element.137) | copy-start | bytes 9220
  156.8 8.4 %copy-start.63 = (f32[1,1536]{1,0:T(1,128)S(1)}, f32[1,1536]{1,0:T(1,128)}, u32[]{:S(2)}) copy-start(f32[1,1536]{1,0:T(1,128)} %get-tuple-element.129) | copy-start | bytes 18436
  156.8 8.4 %copy-start.34 = (bf16[2,128,768]{2,1,0:T(8,128)(2,1)S(1)}, bf16[2,128,768]{2,1,0:T(8,128)(2,1)}, u32[]{:S(2)}) copy-start(bf16[2,128,768]{2,1,0:T(8,128)(2,1)} %param.23) | copy-start | bytes 1179652
  158.1 19.6 %all-to-all-start = ((bf16[4,2,256,192]{2,3,1,0:T(8,128)(2,1)}), bf16[4,2,256,192]{2,3,1,0:T(8,128)(2,1)}, u32[]{:S(2)}, u32[]{:S(2)}) async-start(bf16[4,2,256,192]{2,3,1,0:T(8,128)(2,1)} %copy.94), calls=%async_computation | async-start | bytes 1572864 | tf_op jit(solution)/shard_map/all_to_all | solution.py:1099
  162.3 173.2 %all-gather.5.cloned.1.call-start = ((), (), s32[]{:S(2)}) async-start(), calls=%async_computation.6 | async-start | bytes 4866048 | tf_op jit(solution)/shard_map/all_gather | solution.py:1175
  166.7 111.4 %copy-start = (s32[2,1536,2]{2,1,0:T(8,128)}, s32[2,1536,2]{2,1,0:T(8,128)S(1)}, u32[]{:S(2)}) copy-start(s32[2,1536,2]{2,1,0:T(8,128)S(1)} %pad_add_fusion.refs_0_) | copy-start | bytes 73732
  166.7 13.1 %copy-start.51 = (bf16[2,256,768]{2,1,0:T(8,128)(2,1)S(1)}, bf16[2,256,768]{2,1,0:T(8,128)(2,1)}, u32[]{:S(2)}) copy-start(bf16[2,256,768]{2,1,0:T(8,128)(2,1)} %refs_5_.1) | copy-start | bytes 2359300
  278.1 20.0 %copy-start.14 = (bf16[1024,640]{1,0:T(8,128)(2,1)}, bf16[1024,640]{1,0:T(8,128)(2,1)S(1)}, u32[]{:S(2)}) copy-start(bf16[1024,640]{1,0:T(8,128)(2,1)S(1)} %add_convert_fusion.2) | copy-start | bytes 3932164
  299.0 15.0 %all-to-all-start.1 = ((bf16[4,2,128,192]{2,3,1,0:T(8,128)(2,1)}), bf16[4,2,128,192]{2,3,1,0:T(8,128)(2,1)S(1)}, u32[]{:S(2)}, u32[]{:S(2)}) async-start(bf16[4,2,128,192]{2,3,1,0:T(8,128)(2,1)} %copy.97), calls=%async_computation.1 | async-start | bytes 786432 | tf_op jit(solution)/shard_map/all_to_all | solution.py:1099
  302.5 11.9 %copy-start.54 = (bf16[2,128,768]{2,1,0:T(8,128)(2,1)S(1)}, bf16[2,128,768]{2,1,0:T(8,128)(2,1)}, u32[]{:S(2)}) copy-start(bf16[2,128,768]{2,1,0:T(8,128)(2,1)} %refs_6_.1) | copy-start | bytes 1179652
  302.5 458.8 %reduce-scatter.2.cloned.1.call-start = ((), (), s32[]{:S(2)}) async-start(), calls=%async_computation.7 | async-start | bytes 14598144 | tf_op jit(solution)/shard_map/reduce_scatter | solution.py:1297
  316.5 10.4 %copy-start.40 = (f32[256,768]{1,0:T(8,128)}, f32[256,768]{1,0:T(8,128)S(1)}, u32[]{:S(2)}) copy-start(f32[256,768]{1,0:T(8,128)S(1)} %get-tuple-element.222) | copy-start | bytes 2359300
  328.8 22.1 %copy-start.43 = (f32[256,768]{1,0:T(8,128)}, f32[256,768]{1,0:T(8,128)S(1)}, u32[]{:S(2)}) copy-start(f32[256,768]{1,0:T(8,128)S(1)} %get-tuple-element.224) | copy-start | bytes 2359300
  437.5 10.6 %slice-start.4 = ((s8[4718592]{0:T(1024)(128)(4,1)}), s8[4194304]{0:T(1024)(128)(4,1)S(1)}, s32[]{:S(2)}) async-start(s8[4718592]{0:T(1024)(128)(4,1)} %bitcast.217), calls=%async_computation.12 | async-start | bytes 8388608
  439.8 8.4 %copy-start.49 = (f32[512,768]{1,0:T(8,128)}, f32[512,768]{1,0:T(8,128)S(1)}, u32[]{:S(2)}) copy-start(f32[512,768]{1,0:T(8,128)S(1)} %get-tuple-element.203) | copy-start | bytes 4718596
  439.8 8.4 %copy-start.28 = (f32[512,768]{1,0:T(8,128)S(1)}, f32[512,768]{1,0:T(8,128)}, u32[]{:S(2)}) copy-start(f32[512,768]{1,0:T(8,128)} %copy-done.27) | copy-start | bytes 4718596
  439.8 8.4 %slice-start.5 = ((s8[4718592]{0:T(1024)(128)(4,1)}), s8[524288]{0:T(1024)(128)(4,1)S(1)}, s32[]{:S(2)}) async-start(s8[4718592]{0:T(1024)(128)(4,1)} %bitcast.217), calls=%async_computation.13 | async-start | bytes 1048576
  455.3 8.4 %copy-start.44 = (f32[256,768]{1,0:T(8,128)S(1)}, f32[256,768]{1,0:T(8,128)}, u32[]{:S(2)}) copy-start(f32[256,768]{1,0:T(8,128)} %copy-done.43) | copy-start | bytes 2359300
  455.3 8.4 %copy-start.96 = (bf16[256,3072]{1,0:T(8,128)(2,1)S(1)}, bf16[256,3072]{1,0:T(8,128)(2,1)}, u32[]{:S(2)}) copy-start(bf16[256,3072]{1,0:T(8,128)(2,1)} %copy-done.95) | copy-start | bytes 4718596
  483.5 22.8 %all-to-all-start.3 = ((bf16[4,2,128,192]{2,3,1,0:T(8,128)(2,1)}), bf16[4,2,128,192]{2,3,1,0:T(8,128)(2,1)S(1)}, u32[]{:S(2)}, u32[]{:S(2)}) async-start(bf16[4,2,128,192]{2,3,1,0:T(8,128)(2,1)} %copy.107), calls=%async_computation.3 | async-start | bytes 786432 | tf_op jit(solution)/shard_map/all_to_all | solution.py:1106
  503.1 9.6 %copy-start.15 = (bf16[1024,640]{1,0:T(8,128)(2,1)S(1)}, bf16[1024,640]{1,0:T(8,128)(2,1)}, u32[]{:S(2)}) copy-start(bf16[1024,640]{1,0:T(8,128)(2,1)} %copy-done.14) | copy-start | bytes 3932164
  507.0 37.3 %all-to-all-start.2 = ((bf16[4,2,256,192]{2,3,1,0:T(8,128)(2,1)}), bf16[4,2,256,192]{2,3,1,0:T(8,128)(2,1)}, u32[]{:S(2)}, u32[]{:S(2)}) async-start(bf16[4,2,256,192]{2,3,1,0:T(8,128)(2,1)} %copy.102), calls=%async_computation.2 | async-start | bytes 1572864 | tf_op jit(solution)/shard_map/all_to_all | solution.py:1106
  541.7 53.2 %copy-start.30 = (bf16[4,2,128,256]{3,2,1,0:T(8,128)(2,1)}, bf16[4,2,128,256]{3,2,1,0:T(8,128)(2,1)S(1)}, u32[]{:S(2)}) copy-start(bf16[4,2,128,256]{3,2,1,0:T(8,128)(2,1)S(1)} %slice.133) | copy-start | bytes 1572868
  541.7 48.3 %collective-permute-start = (bf16[4,2,128,384]{3,2,1,0:T(8,128)(2,1)}, bf16[4,2,128,384]{3,2,1,0:T(8,128)(2,1)}, u32[]{:S(2)}, u32[]{:S(2)}) collective-permute-start(bf16[4,2,128,384]{3,2,1,0:T(8,128)(2,1)} %get-tuple-element.148), channel_id=1, source_target_pairs={{8,0},{12,4},{16,8},{20,12},{24,16},{28,20},{9,1},{13,5},{17,9},{2... | collective-permute-start | bytes 2359304 | tf_op jit(solution)/shard_map/ppermute | solution.py:1116
  543.0 47.0 %collective-permute-start.1 = (bf16[4,2,128,384]{3,2,1,0:T(8,128)(2,1)S(1)}, bf16[4,2,128,384]{3,2,1,0:T(8,128)(2,1)}, u32[]{:S(2)}, u32[]{:S(2)}) collective-permute-start(bf16[4,2,128,384]{3,2,1,0:T(8,128)(2,1)S(1)} %get-tuple-element.149), channel_id=1, source_target_pairs={{4,0},{8,4},{12,8},{16,12},{20,16},{24,20},{28,24},{5,1},{9,5},{13... | collective-permute-start | bytes 2359304 | tf_op jit(solution)/shard_map/ppermute | solution.py:1116
  (87 other events, 383.0 us)
Sparse Core Ops, SparseCore 0:
  122.9 128.5 all-gather.2
  254.3 69.3 all-gather.4
  475.8 222.0 reduce-scatter.1

commit v4 on v3

--- a/solution.py
+++ b/solution.py
@@ -66,12 +66,13 @@
     pl.semaphore_wait(barrier, count)
 
 
-def gather_kernel(count, shared, reach, orders, *refs):
+def gather_kernel(count, shared, reach, orders, *refs, greeted=False):
     every = count + shared
     ins, outs, refs = refs[:every], refs[every : 2 * every + reach], refs[2 * every + reach :]
     own_sem, recv_sem, send_sem, group_recv, group_send, ahead_send = refs
     z, y, x, c = place()
-    greet(z, y, x, c, reach > 0)
+    if not greeted:
+        greet(z, y, x, c, reach > 0)
     here = [(x, y) if order in "xX" else (y, x) for order in orders]
 
     def shard_of(a, zo, f, l):
@@ -164,21 +165,7 @@
         group_copy(b, source, x, c, 1, beside).wait_send()
         group_copy(b, landed, 1 - x, c, 2, beside).wait_send()
 
-    for by in range(1, reach + 1):
-
-        @pl.when(seq + by <= 7)
-        def _():
-            ahead_copy(by).start()
-
     kept = []
-    for b in range(shared):
-        spread(b, ins[count + b])
-        kept.append(
-            pltpu.make_async_copy(
-                ins[count + b], outs[count + b].at[x * 2 + c], own_sem.at[count + b]
-            )
-        )
-        kept[-1].start()
     for a in range(count):
         me = shard_of(a, z, *here[a])
         forward(a, ins[a], me, True, True, True)
@@ -190,15 +177,30 @@
     from_last(z, False)
     from_last(z, True)
     for b in range(shared):
-        spread_on(b)
+        spread(b, ins[count + b])
+        kept.append(
+            pltpu.make_async_copy(
+                ins[count + b], outs[count + b].at[x * 2 + c], own_sem.at[count + b]
+            )
+        )
+        kept[-1].start()
     for by in range(1, reach + 1):
 
-        @pl.when(seq >= by)
+        @pl.when(seq + by <= 7)
         def _():
-            ahead_copy(by).wait_recv()
-            spread(shared + by - 1, outs[every + by - 1].at[x * 2 + c])
+            ahead_copy(by).start()
 
     for distance in (1, 2, 3):
+        if distance == 3:
+            for b in range(shared):
+                spread_on(b)
+            for by in range(1, reach + 1):
+
+                @pl.when(seq >= by)
+                def _():
+                    ahead_copy(by).wait_recv()
+                    spread(shared + by - 1, outs[every + by - 1].at[x * 2 + c])
+
         for below in (True, False):
 
             @pl.when((z >= distance) if below else (z + distance <= 3))
@@ -272,26 +274,23 @@
     return pl.CostEstimate(flops=0, transcendentals=0, bytes_accessed=size * share)
 
 
+def gather_scratch(count, shared, reach):
+    spreads = max(shared + reach, 1)
+    shapes = [(count + shared,), (count, 32), (count, 5, 16), (spreads, 4), (spreads, 3)]
+    return [pltpu.SemaphoreType.DMA(shape) for shape in shapes + [(max(reach, 1),)]]
+
+
 def gather_all(arrays, orders, collective_id, group_arrays=(), reach=0):
     count, shared = len(arrays), len(group_arrays)
     every = [*arrays, *group_arrays]
     results = [(32, v) for v in arrays] + [(4, v) for v in group_arrays]
     results += [(4, v) for v in every[-1:] * reach]
-    spreads = max(shared + reach, 1)
-    D = pltpu.SemaphoreType.DMA
     return pl.pallas_call(
         functools.partial(gather_kernel, count, shared, reach, orders),
         out_shape=[jax.ShapeDtypeStruct((n,) + v.shape, v.dtype) for n, v in results],
         in_specs=[pl.BlockSpec(memory_space=pl.ANY)] * len(every),
         out_specs=[pl.BlockSpec(memory_space=pl.ANY)] * len(results),
-        scratch_shapes=[
-            D((len(every),)),
-            D((count, 32)),
-            D((count, 5, 16)),
-            D((spreads, 4)),
-            D((spreads, 3)),
-            D((max(reach, 1),)),
-        ],
+        scratch_shapes=gather_scratch(count, shared, reach),
         compiler_params=pltpu.CompilerParams(collective_id=collective_id, has_side_effects=True),
         cost_estimate=traffic(arrays, 500),
         name="gather_all",
@@ -582,9 +581,8 @@
             mid_copy(a, block(a, z, f, 1 - l), 0).wait_send()
 
 
-def scatter_sum(arrays, orders, collective_id, out_dtype=F32, group_arrays=()):
-    count, shared = len(arrays), len(group_arrays)
-    shapes = [v.shape[1:] for v in (*arrays, *group_arrays)]
+def scatter_scratch(shapes, orders, shared):
+    count = len(shapes) - shared
     late = [order in "XY" for order in orders]
     sizes = [[16, 16, 8, 4, 3, 3] if up else [16, 16, 8, 1, 6, 6] for up in late]
     scratch = []
@@ -595,18 +593,51 @@
     scratch += [pltpu.SemaphoreType.DMA((max(shared, 1), 2, 5))]
     scratch += [pltpu.VMEM((2,) + shape, BF16) for shape in shapes[count:]] * 2
     scratch += [pltpu.VMEM(shape, BF16) for shape in shapes[count:]]
+    return scratch
+
+
+def scatter_sum(arrays, orders, collective_id, out_dtype=F32, group_arrays=()):
+    count, shared = len(arrays), len(group_arrays)
+    shapes = [v.shape[1:] for v in (*arrays, *group_arrays)]
     return pl.pallas_call(
         functools.partial(scatter_kernel, count, shared, orders),
         out_shape=[jax.ShapeDtypeStruct(shape, out_dtype) for shape in shapes],
         in_specs=[pl.BlockSpec(memory_space=pl.ANY)] * len(shapes),
         out_specs=[pl.BlockSpec(memory_space=pltpu.VMEM)] * len(shapes),
-        scratch_shapes=scratch,
+        scratch_shapes=scatter_scratch(shapes, orders, shared),
         compiler_params=pltpu.CompilerParams(
             collective_id=collective_id, has_side_effects=True, vmem_limit_bytes=60 << 20
         ),
         cost_estimate=traffic(arrays, 1),
         name="scatter_sum",
     )(*arrays, *group_arrays)
+
+
+def exchange_kernel(count, orders, *refs):
+    grads, outs, sums = [refs[k * count : (k + 1) * count] for k in range(3)]
+    refs = refs[3 * count :]
+    scatter_refs = 6 * count + 7
+    scatter_kernel(count, 0, orders, *grads, *sums, *refs[:scatter_refs])
+    gather_kernel(count, 0, 0, orders, *sums, *outs, *refs[scatter_refs:], greeted=True)
+
+
+def exchange_all(arrays, orders, collective_id):
+    count = len(arrays)
+    shapes = [v.shape[1:] for v in arrays]
+    scratch = [pltpu.VMEM(shape, BF16) for shape in shapes]
+    scratch += scatter_scratch(shapes, orders, 0) + gather_scratch(count, 0, 0)
+    return pl.pallas_call(
+        functools.partial(exchange_kernel, count, orders),
+        out_shape=[jax.ShapeDtypeStruct(v.shape, v.dtype) for v in arrays],
+        in_specs=[pl.BlockSpec(memory_space=pl.ANY)] * count,
+        out_specs=[pl.BlockSpec(memory_space=pl.ANY)] * count,
+        scratch_shapes=scratch,
+        compiler_params=pltpu.CompilerParams(
+            collective_id=collective_id, has_side_effects=True, vmem_limit_bytes=48 << 20
+        ),
+        cost_estimate=traffic(arrays, 2),
+        name="exchange_all",
+    )(*arrays)
 
 
 def known_mesh():
@@ -628,6 +659,13 @@
         lax.psum_scatter(v, axes, scatter_dimension=0, tiled=False).astype(out_dtype)
         for v, axes in [(v, EVERY) for v in arrays] + [(v, "head") for v in group_arrays]
     ]
+
+
+def exchange(arrays, orders, collective_id):
+    if known_mesh():
+        return exchange_all(arrays, orders, collective_id)
+    sums = [lax.psum_scatter(v, EVERY, scatter_dimension=0, tiled=False) for v in arrays]
+    return [lax.all_gather(v, EVERY, axis=0, tiled=False) for v in sums]
 
 
 def fill(target, refs, columns, scale=None):
@@ -1208,7 +1246,7 @@
         preferred_element_type=F32,
     ).astype(BF16)
     picked = [picked[m].reshape(devices, asked // devices, D) for m in range(micro)]
-    fetched = gather(scatter(picked, "xy", 2, BF16), "xy", 3)
+    fetched = exchange(picked, "xy", 2)
     fetched = jnp.concatenate([v.reshape(asked, D) for v in fetched], axis=0)
     decoder_full, fetched = lax.optimization_barrier((decoder_full, fetched))
     ends = [0]
@@ -1261,7 +1299,7 @@
     g_pairs = g_pairs.reshape(micro * asked, 2 * D)
     g_fetched = mm_back(g_pairs, c_pairs).astype(BF16).reshape(micro, asked, D)
     g_fetched = [g_fetched[m].reshape(devices, asked // devices, D) for m in range(micro)]
-    g_fetched = gather(scatter(g_fetched, "xy", 4, BF16), "xy", 5)
+    g_fetched = exchange(g_fetched, "xy", 3)
     w_c_pairs = mm_rows(fetched, g_pairs)
     w_c_query = mm_rows(d_first_low, g_queries)
     g_first = g_sum_two + mm_back(g_queries, c_query)
@@ -1301,10 +1339,10 @@
         e_joined, [], *src_info, e_logs, ge_attended, heads, False, BF16
     )
     ge_joined = ge_joined.reshape(parts * micro * src_rows, -1)
-    w_e_qkv = mm_rows(source_all.reshape(-1, D), ge_joined)
+    w_e_qkv = mm_rows(source_all.reshape(-1, D), ge_joined).astype(BF16)
     g_source_all = mm_back(ge_joined, e_qkv_here).astype(BF16)
 
-    *g_back, ge_joined = lax.optimization_barrier((*g_back, ge_joined))
+    *g_back, g_source_all, w_e_qkv = lax.optimization_barrier((*g_back, g_source_all, w_e_qkv))
     width = heads * 128
     g_pairs_own = g_own[..., :width] + sum(g.astype(F32) for g in g_back)
     g_joined = jnp.concatenate([g_pairs_own.astype(BF16), g_own[..., width:].astype(BF16)], axis=-1)
@@ -1344,7 +1382,7 @@
     )
     late_sums = scatter(
         [
-            pieces(all_columns(w_e_qkv.astype(BF16), parts)),
+            pieces(all_columns(w_e_qkv, parts)),
             pieces(w_e_out),
             pieces(w_e_down),
             small_grads,
@@ -1352,8 +1390,8 @@
             pieces(w_d_out),
             pieces(w_d_down),
         ],
-        "xyxyyxy",
-        7,
+        "xyxyyyy",
+        4,
         F32,
         [v.reshape(parts, -1, D) for v in (g_source_all, g_target_all)],
     )

time: 778 us -> 756 us (0.972)
  Pallas kernels: 515 us -> 497 us
    pallas_call x0 -> x2, Pallas kernels: none -> 121 us  [exchange_all(): pl.pallas_call(functools.partial(exchange_kernel, count, orders), out_sha...]
    pallas_call x3 -> x1, Pallas kernels: 166 us -> 94.7 us  [gather_all(): pl.pallas_call(functools.partial(gather_kernel, count, shared, reach, ord...]
    pallas_call x3 -> x1, Pallas kernels: 220 us -> 152 us  [scatter_sum(): pl.pallas_call(functools.partial(scatter_kernel, count, shared, orders),...]
    unnamed x229 -> x233, local copies, waits for them, and re-layouts: 16.8 us -> 14.9 us
  transfers between devices with their start and end apart: 9 -> 9, of which waited for: 3 -> 3; matrix products, arithmetic and copies ran while one was open for 14% -> 15% of each run, Pallas kernels for 43% -> 45%
where the time goes in v4:
time: 756 us; the launch traced here: 751 us
  Pallas kernels  497 us (66%)
  matrix products  126 us (17%)
  local copies, waits for them, and re-layouts  41.3 us (5%)
  other arithmetic  27.3 us (4%)
  waiting for transfers between devices  23.6 us (3%)
  starting transfers between devices  18.9 us (2%)
  between operations  16 us (2%)
    pallas_call x1, Pallas kernels, scatter_sum(): pl.pallas_call(functools.partial(scatter_kernel, count, shared, orders),...  152 us
    pallas_call x2, Pallas kernels, exchange_all(): pl.pallas_call(functools.partial(exchange_kernel, count, orders), out_sha...  121 us
    pallas_call x1, Pallas kernels, gather_all(): pl.pallas_call(functools.partial(gather_kernel, count, shared, reach, ord...  94.7 us
    pallas_call x2, Pallas kernels, attend_back(): pl.pallas_call(functools.partial(attend_back_kernel, heads, tile, causal,...  54.3 us
    pallas_call x2, Pallas kernels, attend(): pl.pallas_call(functools.partial(attend_kernel, heads, tile, causal), gri...  45.5 us
    dot_general x13, matrix products, mm(): return jnp.dot(left, right, preferred_element_type=F32)  44.9 us
    dot_general x11, matrix products, mm_back(): lax.dot_general(left, right, (((1,), (1,)), ((), ())), preferred_element_...  43.1 us
    dot_general x11, matrix products, mm_rows(): lax.dot_general(left, right, (((0,), (0,)), ((), ())), preferred_element_...  35.5 us
  transfers between devices with their start and end apart: 9, of which 3 were waited for; matrix products, arithmetic and copies ran while one was open for 15% of the time, Pallas kernels for 45%

profile of v4, /device:TPU:0, one launch (start us, length us, event | category | flops | bytes accessed | tf_op | source)
XLA Modules:
  0.0 750.6 jit_solution(16846476465641649430)
XLA Ops:
  13.2 94.7 %gather_all.1 = (bf16[32,24,2560]{2,1,0:T(8,128)(2,1)}, bf16[32,24,768]{2,1,0:T(8,128)(2,1)}, bf16[32,24,3072]{2,1,0:T(8,128)(2,1)}, bf16[32,96,768]{2,1,0:T(8,1...) custom-call(bf16[24,2560]{1,0:T(8,128)(2,1)} %bitcast.209, ...), custom_call_target="tpu_custom_call" | custom-call | bytes 231424000 | tf_op jit(solution)/shard_map/gather_all/pallas_call | solution.py:288
  111.4 4.8 add_convert_fusion.1
  116.2 25.5 %attend.2 = (bf16[4,2,256,192]{3,2,1,0:T(8,128)(2,1)S(1)}, f32[2,3,1024]{2,1,0:T(4,128)S(1)}) custom-call(s32[2,1024,2]{2,1,0:T(8,128)S(1)} %copy.93.refs_0_, s32[2,2,1024]{2,1,0:T(2,128)S(1)} %pad_add_fusion.2.refs_1_, bf16[4,2,256,640]{3,2,1,0:T(8,128)(2,1)S(1)} %bitcast.169), custom_call_target="tpu_custom_call" | custom-call | flops 12884901888 | bytes 5242880 | tf_op jit(solution)/shard_map/attend/pallas_call | solution.py:757
  143.2 4.2 all-to-all-start
  151.9 16.0 %all-to-all-done = bf16[4,2,256,192]{2,3,1,0:T(8,128)(2,1)} async-done(((bf16[4,2,256,192]{2,3,1,0:T(8,128)(2,1)}), bf16[4,2,256,192]{2,3,1,0:T(8,128)(2,1)}, u32[]{:S(2)}, u32[]{:S(2)}) %all-to-all-start) | async-done | bytes 786464 | tf_op jit(solution)/shard_map/all_to_all | solution.py:1137
  171.4 7.4 multiply_convert_fusion.1
  185.2 71.6 %exchange_all.2 = (bf16[32,32,768]{2,1,0:T(8,128)(2,1)S(1)}, bf16[32,32,768]{2,1,0:T(8,128)(2,1)S(1)}) custom-call(bf16[32,32,768]{2,1,0:T(8,128)(2,1)S(1)} %bitcast.157, bf16[32,32,768]{2,1,0:T(8,128)(2,1)} %bitcast.188), custom_call_target="tpu_custom_call" | custom-call | bytes 6291456 | tf_op jit(solution)/shard_map/exchange_all/pallas_call | solution.py:629
  266.7 20.0 %attend.3 = (bf16[4,2,128,192]{3,2,1,0:T(8,128)(2,1)S(1)}, f32[2,3,512]{2,1,0:T(4,128)S(1)}) custom-call(s32[2,1536,2]{2,1,0:T(8,128)S(1)} %pad_add_fusion.refs_0_, s32[2,2,512]{2,1,0:T(2,128)S(1)} %pad_add_fusion.3.refs_1_, bf16[4,2,128,640]{3,2,1,0:T(8,128)(2,1)S(1)} %bitcast.171, bf16[4,2,128,384]{3,2,1,0:T(8,128)(2,1)S(1)} %bitcast.173, ...), custom_call_target="tpu_custom_call" | custom-call | flops 9663676416 | bytes 2621440 | tf_op jit(solution)/shard_map/attend/pallas_call | solution.py:757
  287.6 3.5 all-to-all-start.1
  291.4 9.1 %add_convert_fusion = bf16[2048,1536]{1,0:T(8,128)(2,1)} fusion(bf16[2048,768]{1,0:T(8,128)(2,1)} %pad_maximum_fusion, f32[1536]{0:T(1024)S(1)} %reduce.23, bf16[768,9472]{1,0:T(8,128)(2,1)} %all-gather.3.cloned.1.call-done), kind=kOutput, calls=%fused_computation.1 | convolution fusion | flops 4838129664 | bytes 11802624 | tf_op jit(solution)/shard_map/dot_general | solution.py:1069
  307.8 8.2 %cross.1 = (bf16[2,128,768]{2,1,0:T(8,128)(2,1)S(1)}, f32[2,12,128]{2,1,0:T(8,128)S(1)}) custom-call(bf16[2,128,768]{2,1,0:T(8,128)(2,1)S(1)} %bitcast.177, bf16[2,1024,1536]{2,1,0:T(8,128)(2,1)} %bitcast.238), custom_call_target="tpu_custom_call" | custom-call | flops 6442450944 | bytes 6291456 | tf_op jit(solution)/shard_map/cross/pallas_call | solution.py:877
  318.2 6.4 multiply_convert_fusion.2
  324.6 4.5 fusion.112
  334.9 4.6 multiply_reduce_fusion.7
  342.2 16.2 %cross_back.1 = (bf16[2,128,768]{2,1,0:T(8,128)(2,1)S(1)}, bf16[2,1024,1536]{2,1,0:T(8,128)(2,1)}) custom-call(bf16[2,128,768]{2,1,0:T(8,128)(2,1)S(1)} %bitcast.178, bf16[2,1024,1536]{2,1,0:T(8,128)(2,1)} %bitcast.239, f32[2,12,128]{2,1,0:T(8,128)S(1)} %get-tuple-element.133.log_ref, bf16[2,128,768]{2,1,0:T(8,128)(2,1)S(1)} %bitcast.164), custom_call_target="tpu_custom_call" | custom-call | flops 9663676416 | bytes 12582912 | tf_op jit(solution)/shard_map/cross_back/pallas_call | solution.py:919
  358.4 7.9 %convolution_convert_fusion.6 = bf16[2048,768]{1,0:T(8,128)(2,1)S(1)} fusion(bf16[2048,1536]{1,0:T(8,128)(2,1)} %bitcast.182, bf16[768,9472]{1,0:T(8,128)(2,1)} %all-gather.3.cloned.1.call-done), kind=kOutput, calls=%fused_computation.24 | convolution fusion | flops 4833411072 | bytes 11796480 | tf_op jit(solution)/shard_map/dot_general | solution.py:1077
  367.6 49.8 %exchange_all.3 = (bf16[32,32,768]{2,1,0:T(8,128)(2,1)S(1)}, bf16[32,32,768]{2,1,0:T(8,128)(2,1)S(1)}) custom-call(bf16[32,32,768]{2,1,0:T(8,128)(2,1)S(1)} %bitcast.158, bf16[32,32,768]{2,1,0:T(8,128)(2,1)} %bitcast.189), custom_call_target="tpu_custom_call" | custom-call | bytes 6291456 | tf_op jit(solution)/shard_map/exchange_all/pallas_call | solution.py:629
  421.5 5.3 convert_reduce_fusion.1
  426.9 4.7 multiply_reduce_fusion
  433.9 6.5 fusion.10
  442.2 3.8 fusion.1
  446.0 5.0 fusion
  462.1 3.5 all-to-all-start.2
  468.7 3.6 convolution_convert_fusion
  475.0 4.4 convolution_convert_fusion.1
  485.4 4.4 all-to-all-start.3
  493.4 25.2 %attend_back.2 = (f32[4,2,128,640]{3,2,1,0:T(8,128)}, bf16[4,2,128,384]{3,2,1,0:T(8,128)(2,1)}, bf16[4,2,128,384]{3,2,1,0:T(8,128)(2,1)S(1)}) custom-call(s32[2,1536,2]{2,1,0:T(8,128)} %copy-done, s32[2,2,512]{2,1,0:T(2,128)S(1)} %pad_add_fusion.3.refs_1_, bf16[4,2,128,640]{3,2,1,0:T(8,128)(2,1)S(1)} %bitcast.172, ...), custom_call_target="tpu_custom_call" | custom-call | flops 14495514624 | bytes 3932160 | tf_op jit(solution)/shard_map/attend_back/pallas_call | solution.py:827
  524.3 29.0 %attend_back.3 = bf16[4,2,256,640]{3,2,1,0:T(8,128)(2,1)S(1)} custom-call(s32[2,1024,2]{2,1,0:T(8,128)S(1)} %copy-done.2, s32[2,2,1024]{2,1,0:T(2,128)S(1)} %copy-done.12, bf16[4,2,256,640]{3,2,1,0:T(8,128)(2,1)} %bitcast.170, f32[2,3,1024]{2,1,0:T(4,128)S(1)} %get-tuple-element.141.refs_3_, bf16[4,2,256,192]{3,2,1,0:T(8,128)(2,1)S(1)} %copy.107.refs_4_), custom_call_target="tpu_custom_call" | custom-call | flops 19327352832 | bytes 7864320 | tf_op jit(solution)/shard_map/attend_back/pallas_call | solution.py:827
  553.4 5.8 convolution_convert_fusion.4
  562.4 4.6 collective-permute-done
  572.0 4.6 convolution_convert_fusion.7
  581.8 151.8 %scatter_sum.1 = (f32[24,2560]{1,0:T(8,128)}, f32[24,768]{1,0:T(8,128)}, f32[96,768]{1,0:T(8,128)}, f32[32,128]{1,0:T(8,128)}, f32[24,2560]{1,0:T(8,128)}, /*ind...) custom-call(bf16[32,24,2560]{2,1,0:T(8,128)(2,1)} %bitcast.181, ...), custom_call_target="tpu_custom_call" | custom-call | bytes 19922944 | tf_op jit(solution)/shard_map/scatter_sum/pallas_call | solution.py:602
  (410 shorter events, 118.0 us)
Async XLA Ops:
  7.3 251.4 %all-gather.3.cloned.1.call-start = ((), (), s32[]{:S(2)}) async-start(), calls=%async_computation.5 | async-start | bytes 15003648 | tf_op jit(solution)/shard_map/all_gather | solution.py:1212
  10.7 99.1 %copy-start.84 = (s32[2,16]{1,0:T(2,128)S(1)}, s32[2,16]{1,0:T(2,128)}, u32[]{:S(2)}) copy-start(s32[2,16]{1,0:T(2,128)} %param.24) | copy-start | bytes 388
  12.5 95.5 %copy-start.53 = (bf16[24,9472]{1,0:T(8,128)(2,1)}, bf16[24,9472]{1,0:T(8,128)(2,1)S(1)}, u32[]{:S(2)}) copy-start(bf16[24,9472]{1,0:T(8,128)(2,1)S(1)} %constant_dynamic-update-slice_fusion) | copy-start | bytes 1363972
  116.2 25.5 %copy-start.13 = (bf16[2048,640]{1,0:T(8,128)(2,1)}, bf16[2048,640]{1,0:T(8,128)(2,1)S(1)}, u32[]{:S(2)}) copy-start(bf16[2048,640]{1,0:T(8,128)(2,1)S(1)} %add_convert_fusion.1) | copy-start | bytes 7864324
  141.8 8.3 %copy-start.71 = (f32[1,768]{1,0:T(1,128)S(1)}, f32[1,768]{1,0:T(1,128)}, u32[]{:S(2)}) copy-start(f32[1,768]{1,0:T(1,128)} %get-tuple-element.121) | copy-start | bytes 9220
  141.9 8.3 %copy-start.70 = (f32[1,768]{1,0:T(1,128)S(1)}, f32[1,768]{1,0:T(1,128)}, u32[]{:S(2)}) copy-start(f32[1,768]{1,0:T(1,128)} %get-tuple-element.120) | copy-start | bytes 9220
  141.9 8.3 %copy-start.63 = (f32[1,1536]{1,0:T(1,128)S(1)}, f32[1,1536]{1,0:T(1,128)}, u32[]{:S(2)}) copy-start(f32[1,1536]{1,0:T(1,128)} %get-tuple-element.124) | copy-start | bytes 18436
  141.9 8.3 %copy-start.69 = (f32[1,768]{1,0:T(1,128)S(1)}, f32[1,768]{1,0:T(1,128)}, u32[]{:S(2)}) copy-start(f32[1,768]{1,0:T(1,128)} %get-tuple-element.128) | copy-start | bytes 9220
  141.9 8.4 %copy-start.68 = (f32[1,768]{1,0:T(1,128)S(1)}, f32[1,768]{1,0:T(1,128)}, u32[]{:S(2)}) copy-start(f32[1,768]{1,0:T(1,128)} %get-tuple-element.127) | copy-start | bytes 9220
  141.9 8.4 %copy-start.67 = (f32[1,768]{1,0:T(1,128)S(1)}, f32[1,768]{1,0:T(1,128)}, u32[]{:S(2)}) copy-start(f32[1,768]{1,0:T(1,128)} %get-tuple-element.131) | copy-start | bytes 9220
  141.9 8.4 %copy-start.66 = (f32[1,768]{1,0:T(1,128)S(1)}, f32[1,768]{1,0:T(1,128)}, u32[]{:S(2)}) copy-start(f32[1,768]{1,0:T(1,128)} %get-tuple-element.132) | copy-start | bytes 9220
  141.9 8.5 %copy-start.34 = (bf16[2,128,768]{2,1,0:T(8,128)(2,1)S(1)}, bf16[2,128,768]{2,1,0:T(8,128)(2,1)}, u32[]{:S(2)}) copy-start(bf16[2,128,768]{2,1,0:T(8,128)(2,1)} %param.23) | copy-start | bytes 1179652
  143.2 24.7 %all-to-all-start = ((bf16[4,2,256,192]{2,3,1,0:T(8,128)(2,1)}), bf16[4,2,256,192]{2,3,1,0:T(8,128)(2,1)}, u32[]{:S(2)}, u32[]{:S(2)}) async-start(bf16[4,2,256,192]{2,3,1,0:T(8,128)(2,1)} %copy.94), calls=%async_computation | async-start | bytes 1572864 | tf_op jit(solution)/shard_map/all_to_all | solution.py:1137
  147.4 177.1 %all-gather.5.cloned.1.call-start = ((), (), s32[]{:S(2)}) async-start(), calls=%async_computation.6 | async-start | bytes 4866048 | tf_op jit(solution)/shard_map/all_gather | solution.py:1213
  151.9 114.8 %copy-start = (s32[2,1536,2]{2,1,0:T(8,128)}, s32[2,1536,2]{2,1,0:T(8,128)S(1)}, u32[]{:S(2)}) copy-start(s32[2,1536,2]{2,1,0:T(8,128)S(1)} %pad_add_fusion.refs_0_) | copy-start | bytes 73732
  151.9 18.2 %copy-start.51 = (bf16[2,256,768]{2,1,0:T(8,128)(2,1)S(1)}, bf16[2,256,768]{2,1,0:T(8,128)(2,1)}, u32[]{:S(2)}) copy-start(bf16[2,256,768]{2,1,0:T(8,128)(2,1)} %refs_5_.1) | copy-start | bytes 2359300
  171.1 7.7 %copy-start.27 = (f32[512,768]{1,0:T(8,128)}, f32[512,768]{1,0:T(8,128)S(1)}, u32[]{:S(2)}) copy-start(f32[512,768]{1,0:T(8,128)S(1)} %get-tuple-element.210) | copy-start | bytes 4718596
  171.1 7.7 %slice-start.6 = ((s8[4718592]{0:T(1024)(128)(4,1)}), s8[4194304]{0:T(1024)(128)(4,1)S(1)}, s32[]{:S(2)}) async-start(s8[4718592]{0:T(1024)(128)(4,1)} %bitcast.219), calls=%async_computation.14 | async-start | bytes 8388608
  266.7 20.0 %copy-start.14 = (bf16[1024,640]{1,0:T(8,128)(2,1)}, bf16[1024,640]{1,0:T(8,128)(2,1)S(1)}, u32[]{:S(2)}) copy-start(bf16[1024,640]{1,0:T(8,128)(2,1)S(1)} %add_convert_fusion.2) | copy-start | bytes 3932164
  287.6 15.5 %all-to-all-start.1 = ((bf16[4,2,128,192]{2,3,1,0:T(8,128)(2,1)}), bf16[4,2,128,192]{2,3,1,0:T(8,128)(2,1)S(1)}, u32[]{:S(2)}, u32[]{:S(2)}) async-start(bf16[4,2,128,192]{2,3,1,0:T(8,128)(2,1)} %copy.97), calls=%async_computation.1 | async-start | bytes 786432 | tf_op jit(solution)/shard_map/all_to_all | solution.py:1137
  291.1 12.4 %copy-start.54 = (bf16[2,128,768]{2,1,0:T(8,128)(2,1)S(1)}, bf16[2,128,768]{2,1,0:T(8,128)(2,1)}, u32[]{:S(2)}) copy-start(bf16[2,128,768]{2,1,0:T(8,128)(2,1)} %refs_6_.1) | copy-start | bytes 1179652
  291.2 447.9 %reduce-scatter.2.cloned.1.call-start = ((), (), s32[]{:S(2)}) async-start(), calls=%async_computation.7 | async-start | bytes 14598144 | tf_op jit(solution)/shard_map/reduce_scatter | solution.py:1335
  305.5 10.5 %copy-start.40 = (f32[256,768]{1,0:T(8,128)}, f32[256,768]{1,0:T(8,128)S(1)}, u32[]{:S(2)}) copy-start(f32[256,768]{1,0:T(8,128)S(1)} %get-tuple-element.216) | copy-start | bytes 2359300
  317.9 21.6 %copy-start.43 = (f32[256,768]{1,0:T(8,128)}, f32[256,768]{1,0:T(8,128)S(1)}, u32[]{:S(2)}) copy-start(f32[256,768]{1,0:T(8,128)S(1)} %get-tuple-element.218) | copy-start | bytes 2359300
  366.3 55.2 %slice-start.12 = ((s8[6291456]{0:T(1024)(128)(4,1)}), s8[4194304]{0:T(1024)(128)(4,1)S(1)}, s32[]{:S(2)}) async-start(s8[6291456]{0:T(1024)(128)(4,1)} %bitcast.240), calls=%async_computation.20 | async-start | bytes 8388608
  433.9 8.2 %copy-start.44 = (f32[256,768]{1,0:T(8,128)S(1)}, f32[256,768]{1,0:T(8,128)}, u32[]{:S(2)}) copy-start(f32[256,768]{1,0:T(8,128)} %copy-done.43) | copy-start | bytes 2359300
  462.1 22.5 %all-to-all-start.2 = ((bf16[4,2,128,192]{2,3,1,0:T(8,128)(2,1)}), bf16[4,2,128,192]{2,3,1,0:T(8,128)(2,1)S(1)}, u32[]{:S(2)}, u32[]{:S(2)}) async-start(bf16[4,2,128,192]{2,3,1,0:T(8,128)(2,1)} %copy.100), calls=%async_computation.2 | async-start | bytes 786432 | tf_op jit(solution)/shard_map/all_to_all | solution.py:1144
  481.5 9.5 %copy-start.15 = (bf16[1024,640]{1,0:T(8,128)(2,1)S(1)}, bf16[1024,640]{1,0:T(8,128)(2,1)}, u32[]{:S(2)}) copy-start(bf16[1024,640]{1,0:T(8,128)(2,1)} %copy-done.14) | copy-start | bytes 3932164
  485.4 37.3 %all-to-all-start.3 = ((bf16[4,2,256,192]{2,3,1,0:T(8,128)(2,1)}), bf16[4,2,256,192]{2,3,1,0:T(8,128)(2,1)}, u32[]{:S(2)}, u32[]{:S(2)}) async-start(bf16[4,2,256,192]{2,3,1,0:T(8,128)(2,1)} %copy.105), calls=%async_computation.3 | async-start | bytes 1572864 | tf_op jit(solution)/shard_map/all_to_all | solution.py:1144
  518.6 48.4 %collective-permute-start = (bf16[4,2,128,384]{3,2,1,0:T(8,128)(2,1)}, bf16[4,2,128,384]{3,2,1,0:T(8,128)(2,1)}, u32[]{:S(2)}, u32[]{:S(2)}) collective-permute-start(bf16[4,2,128,384]{3,2,1,0:T(8,128)(2,1)} %get-tuple-element.139), channel_id=1, source_target_pairs={{8,0},{12,4},{16,8},{20,12},{24,16},{28,20},{9,1},{13,5},{17,9},{2... | collective-permute-start | bytes 2359304 | tf_op jit(solution)/shard_map/ppermute | solution.py:1154
  520.1 47.0 %collective-permute-start.1 = (bf16[4,2,128,384]{3,2,1,0:T(8,128)(2,1)S(1)}, bf16[4,2,128,384]{3,2,1,0:T(8,128)(2,1)}, u32[]{:S(2)}, u32[]{:S(2)}) collective-permute-start(bf16[4,2,128,384]{3,2,1,0:T(8,128)(2,1)S(1)} %get-tuple-element.140), channel_id=1, source_target_pairs={{4,0},{8,4},{12,8},{16,12},{20,16},{24,20},{28,24},{5,1},{9,5},{13... | collective-permute-start | bytes 2359304 | tf_op jit(solution)/shard_map/ppermute | solution.py:1154
  522.7 49.2 %copy-start.30 = (bf16[4,2,128,256]{3,2,1,0:T(8,128)(2,1)}, bf16[4,2,128,256]{3,2,1,0:T(8,128)(2,1)S(1)}, u32[]{:S(2)}) copy-start(bf16[4,2,128,256]{3,2,1,0:T(8,128)(2,1)S(1)} %slice.133) | copy-start | bytes 1572868
  (89 other events, 371.8 us)
Sparse Core Ops, SparseCore 0:
  108.1 136.2 all-gather.2
  247.3 66.2 all-gather.4
  454.4 221.0 reduce-scatter.1

commit v5 on v4

--- a/solution.py
+++ b/solution.py
@@ -749,7 +749,7 @@
     return pl.BlockSpec((1,) + shape[1:], lambda m: (m, 0, 0))
 
 
-def attend(joined, prior, key_info, query_info, heads, causal, tile=256):
+def attend(joined, prior, key_info, query_info, heads, causal, tile=512):
     parts, micro, rows, _ = joined.shape
     group = parts * rows
     keys = key_info.shape[1]
@@ -819,7 +819,7 @@
 
 
 def attend_back(
-    joined, prior, key_info, query_info, logs, grad, heads, causal, out_dtype, tile=256
+    joined, prior, key_info, query_info, logs, grad, heads, causal, out_dtype, tile=512
 ):
     parts, micro, rows, _ = joined.shape
     group = parts * rows

time: 756 us -> 750 us (level)
    pallas_call x2, Pallas kernels: 121 us -> 137 us  [exchange_all(): pl.pallas_call(functools.partial(exchange_kernel, count, orders), out_sha...]
    pallas_call x2, Pallas kernels: 45.5 us -> 30.6 us  [attend(): pl.pallas_call(functools.partial(attend_kernel, heads, tile, causal), gri...]
    all_to_all x2, waiting for transfers between devices: 18.6 us -> 10.5 us  [to_tokens(): got = lax.all_to_all(value, 'head', split_axis=0, concat_axis=0, tiled=True)]
  transfers between devices with their start and end apart: 9 -> 9, of which waited for: 3 -> 2; matrix products, arithmetic and copies ran while one was open for 15% -> 15% of each run, Pallas kernels for 45% -> 44%
where the time goes in v5:
time: 750 us; the launch traced here: 744 us
  Pallas kernels  492 us (66%)
  matrix products  126 us (17%)
  local copies, waits for them, and re-layouts  41.8 us (6%)
  other arithmetic  27.3 us (4%)
  waiting for transfers between devices  21.7 us (3%)
  starting transfers between devices  18.7 us (2%)
  between operations  16 us (2%)
    pallas_call x1, Pallas kernels, scatter_sum(): pl.pallas_call(functools.partial(scatter_kernel, count, shared, orders),...  153 us
    pallas_call x2, Pallas kernels, exchange_all(): pl.pallas_call(functools.partial(exchange_kernel, count, orders), out_sha...  137 us
    pallas_call x1, Pallas kernels, gather_all(): pl.pallas_call(functools.partial(gather_kernel, count, shared, reach, ord...  94.7 us
    pallas_call x2, Pallas kernels, attend_back(): pl.pallas_call(functools.partial(attend_back_kernel, heads, tile, causal,...  47.1 us
    dot_general x13, matrix products, mm(): return jnp.dot(left, right, preferred_element_type=F32)  45.1 us
    dot_general x11, matrix products, mm_back(): lax.dot_general(left, right, (((1,), (1,)), ((), ())), preferred_element_...  43 us
    dot_general x11, matrix products, mm_rows(): lax.dot_general(left, right, (((0,), (0,)), ((), ())), preferred_element_...  35.6 us
    pallas_call x2, Pallas kernels, attend(): pl.pallas_call(functools.partial(attend_kernel, heads, tile, causal), gri...  30.6 us
  transfers between devices with their start and end apart: 9, of which 2 were waited for; matrix products, arithmetic and copies ran while one was open for 15% of the time, Pallas kernels for 44%

profile of v5, /device:TPU:0, one launch (start us, length us, event | category | flops | bytes accessed | tf_op | source)
XLA Modules:
  0.0 744.3 jit_solution(15386547235079498488)
XLA Ops:
  13.3 94.7 %gather_all.1 = (bf16[32,24,2560]{2,1,0:T(8,128)(2,1)}, bf16[32,24,768]{2,1,0:T(8,128)(2,1)}, bf16[32,24,3072]{2,1,0:T(8,128)(2,1)}, bf16[32,96,768]{2,1,0:T(8,1...) custom-call(bf16[24,2560]{1,0:T(8,128)(2,1)} %bitcast.209, ...), custom_call_target="tpu_custom_call" | custom-call | bytes 231424000 | tf_op jit(solution)/shard_map/gather_all/pallas_call | solution.py:288
  111.4 4.8 add_convert_fusion.1
  116.2 17.6 %attend.2 = (bf16[4,2,256,192]{3,2,1,0:T(8,128)(2,1)S(1)}, f32[2,3,1024]{2,1,0:T(4,128)S(1)}) custom-call(s32[2,1024,2]{2,1,0:T(8,128)S(1)} %copy.93.refs_0_, s32[2,2,1024]{2,1,0:T(2,128)S(1)} %pad_add_fusion.2.refs_1_, bf16[4,2,256,640]{3,2,1,0:T(8,128)(2,1)S(1)} %bitcast.169), custom_call_target="tpu_custom_call" | custom-call | flops 12884901888 | bytes 5242880 | tf_op jit(solution)/shard_map/attend/pallas_call | solution.py:757
  135.3 4.2 all-to-all-start
  144.0 10.5 %all-to-all-done = bf16[4,2,256,192]{2,3,1,0:T(8,128)(2,1)} async-done(((bf16[4,2,256,192]{2,3,1,0:T(8,128)(2,1)}), bf16[4,2,256,192]{2,3,1,0:T(8,128)(2,1)}, u32[]{:S(2)}, u32[]{:S(2)}) %all-to-all-start) | async-done | bytes 786464 | tf_op jit(solution)/shard_map/all_to_all | solution.py:1137
  158.0 7.4 multiply_convert_fusion.1
  171.8 86.5 %exchange_all.2 = (bf16[32,32,768]{2,1,0:T(8,128)(2,1)S(1)}, bf16[32,32,768]{2,1,0:T(8,128)(2,1)S(1)}) custom-call(bf16[32,32,768]{2,1,0:T(8,128)(2,1)S(1)} %bitcast.157, bf16[32,32,768]{2,1,0:T(8,128)(2,1)} %bitcast.188), custom_call_target="tpu_custom_call" | custom-call | bytes 6291456 | tf_op jit(solution)/shard_map/exchange_all/pallas_call | solution.py:629
  268.2 13.1 %attend.3 = (bf16[4,2,128,192]{3,2,1,0:T(8,128)(2,1)S(1)}, f32[2,3,512]{2,1,0:T(4,128)S(1)}) custom-call(s32[2,1536,2]{2,1,0:T(8,128)S(1)} %pad_add_fusion.refs_0_, s32[2,2,512]{2,1,0:T(2,128)S(1)} %pad_add_fusion.3.refs_1_, bf16[4,2,128,640]{3,2,1,0:T(8,128)(2,1)S(1)} %bitcast.171, bf16[4,2,128,384]{3,2,1,0:T(8,128)(2,1)S(1)} %bitcast.173, ...), custom_call_target="tpu_custom_call" | custom-call | flops 9663676416 | bytes 2621440 | tf_op jit(solution)/shard_map/attend/pallas_call | solution.py:757
  282.2 3.5 all-to-all-start.1
  285.9 9.1 %add_convert_fusion = bf16[2048,1536]{1,0:T(8,128)(2,1)} fusion(bf16[2048,768]{1,0:T(8,128)(2,1)} %pad_maximum_fusion, f32[1536]{0:T(1024)S(1)} %reduce.23, bf16[768,9472]{1,0:T(8,128)(2,1)} %all-gather.3.cloned.1.call-done), kind=kOutput, calls=%fused_computation.1 | convolution fusion | flops 4838129664 | bytes 11802624 | tf_op jit(solution)/shard_map/dot_general | solution.py:1069
  299.6 8.3 %cross.1 = (bf16[2,128,768]{2,1,0:T(8,128)(2,1)S(1)}, f32[2,12,128]{2,1,0:T(8,128)S(1)}) custom-call(bf16[2,128,768]{2,1,0:T(8,128)(2,1)S(1)} %bitcast.177, bf16[2,1024,1536]{2,1,0:T(8,128)(2,1)} %bitcast.238), custom_call_target="tpu_custom_call" | custom-call | flops 6442450944 | bytes 6291456 | tf_op jit(solution)/shard_map/cross/pallas_call | solution.py:877
  310.1 6.6 multiply_convert_fusion.2
  316.7 4.5 fusion.112
  327.0 4.6 multiply_reduce_fusion.7
  334.3 16.2 %cross_back.1 = (bf16[2,128,768]{2,1,0:T(8,128)(2,1)S(1)}, bf16[2,1024,1536]{2,1,0:T(8,128)(2,1)}) custom-call(bf16[2,128,768]{2,1,0:T(8,128)(2,1)S(1)} %bitcast.178, bf16[2,1024,1536]{2,1,0:T(8,128)(2,1)} %bitcast.239, f32[2,12,128]{2,1,0:T(8,128)S(1)} %get-tuple-element.133.log_ref, bf16[2,128,768]{2,1,0:T(8,128)(2,1)S(1)} %bitcast.164), custom_call_target="tpu_custom_call" | custom-call | flops 9663676416 | bytes 12582912 | tf_op jit(solution)/shard_map/cross_back/pallas_call | solution.py:919
  350.5 7.9 %convolution_convert_fusion.6 = bf16[2048,768]{1,0:T(8,128)(2,1)S(1)} fusion(bf16[2048,1536]{1,0:T(8,128)(2,1)} %bitcast.182, bf16[768,9472]{1,0:T(8,128)(2,1)} %all-gather.3.cloned.1.call-done), kind=kOutput, calls=%fused_computation.24 | convolution fusion | flops 4833411072 | bytes 11796480 | tf_op jit(solution)/shard_map/dot_general | solution.py:1077
  359.8 51.0 %exchange_all.3 = (bf16[32,32,768]{2,1,0:T(8,128)(2,1)S(1)}, bf16[32,32,768]{2,1,0:T(8,128)(2,1)S(1)}) custom-call(bf16[32,32,768]{2,1,0:T(8,128)(2,1)S(1)} %bitcast.158, bf16[32,32,768]{2,1,0:T(8,128)(2,1)} %bitcast.189), custom_call_target="tpu_custom_call" | custom-call | bytes 6291456 | tf_op jit(solution)/shard_map/exchange_all/pallas_call | solution.py:629
  414.8 5.3 convert_reduce_fusion.1
  420.2 4.7 multiply_reduce_fusion
  427.2 6.5 fusion.10
  435.4 3.8 fusion.1
  439.2 5.0 fusion
  455.5 3.5 all-to-all-start.2
  462.1 3.6 convolution_convert_fusion
  468.4 4.4 convolution_convert_fusion.1
  478.8 4.4 all-to-all-start.3
  486.8 20.4 %attend_back.2 = (f32[4,2,128,640]{3,2,1,0:T(8,128)}, bf16[4,2,128,384]{3,2,1,0:T(8,128)(2,1)}, bf16[4,2,128,384]{3,2,1,0:T(8,128)(2,1)S(1)}) custom-call(s32[2,1536,2]{2,1,0:T(8,128)} %copy-done, s32[2,2,512]{2,1,0:T(2,128)S(1)} %pad_add_fusion.3.refs_1_, bf16[4,2,128,640]{3,2,1,0:T(8,128)(2,1)S(1)} %bitcast.172, ...), custom_call_target="tpu_custom_call" | custom-call | flops 14495514624 | bytes 3932160 | tf_op jit(solution)/shard_map/attend_back/pallas_call | solution.py:827
  513.2 26.6 %attend_back.3 = bf16[4,2,256,640]{3,2,1,0:T(8,128)(2,1)S(1)} custom-call(s32[2,1024,2]{2,1,0:T(8,128)S(1)} %copy-done.2, s32[2,2,1024]{2,1,0:T(2,128)S(1)} %copy-done.12, bf16[4,2,256,640]{3,2,1,0:T(8,128)(2,1)} %bitcast.170, f32[2,3,1024]{2,1,0:T(4,128)S(1)} %get-tuple-element.141.refs_3_, bf16[4,2,256,192]{3,2,1,0:T(8,128)(2,1)S(1)} %copy.107.refs_4_), custom_call_target="tpu_custom_call" | custom-call | flops 19327352832 | bytes 7864320 | tf_op jit(solution)/shard_map/attend_back/pallas_call | solution.py:827
  539.8 5.6 convolution_convert_fusion.4
  548.6 10.8 %collective-permute-done = bf16[4,2,128,384]{3,2,1,0:T(8,128)(2,1)} collective-permute-done((bf16[4,2,128,384]{3,2,1,0:T(8,128)(2,1)}, bf16[4,2,128,384]{3,2,1,0:T(8,128)(2,1)}, u32[]{:S(2)}, u32[]{:S(2)}) %collective-permute-start) | collective-permute-done | bytes 786464 | tf_op jit(solution)/shard_map/ppermute | solution.py:1154
  564.4 4.5 convolution_convert_fusion.7
  574.4 153.0 %scatter_sum.1 = (f32[24,2560]{1,0:T(8,128)}, f32[24,768]{1,0:T(8,128)}, f32[96,768]{1,0:T(8,128)}, f32[32,128]{1,0:T(8,128)}, f32[24,2560]{1,0:T(8,128)}, /*ind...) custom-call(bf16[32,24,2560]{2,1,0:T(8,128)(2,1)} %bitcast.181, ...), custom_call_target="tpu_custom_call" | custom-call | bytes 19922944 | tf_op jit(solution)/shard_map/scatter_sum/pallas_call | solution.py:602
  (410 shorter events, 116.0 us)
Async XLA Ops:
  7.3 252.8 %all-gather.3.cloned.1.call-start = ((), (), s32[]{:S(2)}) async-start(), calls=%async_computation.5 | async-start | bytes 15003648 | tf_op jit(solution)/shard_map/all_gather | solution.py:1212
  10.7 99.2 %copy-start.84 = (s32[2,16]{1,0:T(2,128)S(1)}, s32[2,16]{1,0:T(2,128)}, u32[]{:S(2)}) copy-start(s32[2,16]{1,0:T(2,128)} %param.24) | copy-start | bytes 388
  12.5 95.5 %copy-start.53 = (bf16[24,9472]{1,0:T(8,128)(2,1)}, bf16[24,9472]{1,0:T(8,128)(2,1)S(1)}, u32[]{:S(2)}) copy-start(bf16[24,9472]{1,0:T(8,128)(2,1)S(1)} %constant_dynamic-update-slice_fusion) | copy-start | bytes 1363972
  116.2 17.6 %copy-start.13 = (bf16[2048,640]{1,0:T(8,128)(2,1)}, bf16[2048,640]{1,0:T(8,128)(2,1)S(1)}, u32[]{:S(2)}) copy-start(bf16[2048,640]{1,0:T(8,128)(2,1)S(1)} %add_convert_fusion.1) | copy-start | bytes 7864324
  133.9 8.3 %copy-start.71 = (f32[1,768]{1,0:T(1,128)S(1)}, f32[1,768]{1,0:T(1,128)}, u32[]{:S(2)}) copy-start(f32[1,768]{1,0:T(1,128)} %get-tuple-element.121) | copy-start | bytes 9220
  134.0 8.3 %copy-start.70 = (f32[1,768]{1,0:T(1,128)S(1)}, f32[1,768]{1,0:T(1,128)}, u32[]{:S(2)}) copy-start(f32[1,768]{1,0:T(1,128)} %get-tuple-element.120) | copy-start | bytes 9220
  134.0 8.3 %copy-start.63 = (f32[1,1536]{1,0:T(1,128)S(1)}, f32[1,1536]{1,0:T(1,128)}, u32[]{:S(2)}) copy-start(f32[1,1536]{1,0:T(1,128)} %get-tuple-element.124) | copy-start | bytes 18436
  134.0 8.3 %copy-start.69 = (f32[1,768]{1,0:T(1,128)S(1)}, f32[1,768]{1,0:T(1,128)}, u32[]{:S(2)}) copy-start(f32[1,768]{1,0:T(1,128)} %get-tuple-element.128) | copy-start | bytes 9220
  134.0 8.4 %copy-start.68 = (f32[1,768]{1,0:T(1,128)S(1)}, f32[1,768]{1,0:T(1,128)}, u32[]{:S(2)}) copy-start(f32[1,768]{1,0:T(1,128)} %get-tuple-element.127) | copy-start | bytes 9220
  134.0 8.4 %copy-start.67 = (f32[1,768]{1,0:T(1,128)S(1)}, f32[1,768]{1,0:T(1,128)}, u32[]{:S(2)}) copy-start(f32[1,768]{1,0:T(1,128)} %get-tuple-element.131) | copy-start | bytes 9220
  134.0 8.4 %copy-start.66 = (f32[1,768]{1,0:T(1,128)S(1)}, f32[1,768]{1,0:T(1,128)}, u32[]{:S(2)}) copy-start(f32[1,768]{1,0:T(1,128)} %get-tuple-element.132) | copy-start | bytes 9220
  134.0 8.5 %copy-start.34 = (bf16[2,128,768]{2,1,0:T(8,128)(2,1)S(1)}, bf16[2,128,768]{2,1,0:T(8,128)(2,1)}, u32[]{:S(2)}) copy-start(bf16[2,128,768]{2,1,0:T(8,128)(2,1)} %param.23) | copy-start | bytes 1179652
  135.3 19.1 %all-to-all-start = ((bf16[4,2,256,192]{2,3,1,0:T(8,128)(2,1)}), bf16[4,2,256,192]{2,3,1,0:T(8,128)(2,1)}, u32[]{:S(2)}, u32[]{:S(2)}) async-start(bf16[4,2,256,192]{2,3,1,0:T(8,128)(2,1)} %copy.94), calls=%async_computation | async-start | bytes 1572864 | tf_op jit(solution)/shard_map/all_to_all | solution.py:1137
  139.5 177.2 %all-gather.5.cloned.1.call-start = ((), (), s32[]{:S(2)}) async-start(), calls=%async_computation.6 | async-start | bytes 4866048 | tf_op jit(solution)/shard_map/all_gather | solution.py:1213
  143.9 124.2 %copy-start = (s32[2,1536,2]{2,1,0:T(8,128)}, s32[2,1536,2]{2,1,0:T(8,128)S(1)}, u32[]{:S(2)}) copy-start(s32[2,1536,2]{2,1,0:T(8,128)S(1)} %pad_add_fusion.refs_0_) | copy-start | bytes 73732
  144.0 12.7 %copy-start.51 = (bf16[2,256,768]{2,1,0:T(8,128)(2,1)S(1)}, bf16[2,256,768]{2,1,0:T(8,128)(2,1)}, u32[]{:S(2)}) copy-start(bf16[2,256,768]{2,1,0:T(8,128)(2,1)} %refs_5_.1) | copy-start | bytes 2359300
  157.6 7.7 %copy-start.27 = (f32[512,768]{1,0:T(8,128)}, f32[512,768]{1,0:T(8,128)S(1)}, u32[]{:S(2)}) copy-start(f32[512,768]{1,0:T(8,128)S(1)} %get-tuple-element.210) | copy-start | bytes 4718596
  268.1 13.1 %copy-start.14 = (bf16[1024,640]{1,0:T(8,128)(2,1)}, bf16[1024,640]{1,0:T(8,128)(2,1)S(1)}, u32[]{:S(2)}) copy-start(bf16[1024,640]{1,0:T(8,128)(2,1)S(1)} %add_convert_fusion.2) | copy-start | bytes 3932164
  282.2 12.8 %all-to-all-start.1 = ((bf16[4,2,128,192]{2,3,1,0:T(8,128)(2,1)}), bf16[4,2,128,192]{2,3,1,0:T(8,128)(2,1)S(1)}, u32[]{:S(2)}, u32[]{:S(2)}) async-start(bf16[4,2,128,192]{2,3,1,0:T(8,128)(2,1)} %copy.97), calls=%async_computation.1 | async-start | bytes 786432 | tf_op jit(solution)/shard_map/all_to_all | solution.py:1137
  285.7 9.7 %copy-start.54 = (bf16[2,128,768]{2,1,0:T(8,128)(2,1)S(1)}, bf16[2,128,768]{2,1,0:T(8,128)(2,1)}, u32[]{:S(2)}) copy-start(bf16[2,128,768]{2,1,0:T(8,128)(2,1)} %refs_6_.1) | copy-start | bytes 1179652
  285.7 447.1 %reduce-scatter.2.cloned.1.call-start = ((), (), s32[]{:S(2)}) async-start(), calls=%async_computation.7 | async-start | bytes 14598144 | tf_op jit(solution)/shard_map/reduce_scatter | solution.py:1335
  297.4 10.5 %copy-start.40 = (f32[256,768]{1,0:T(8,128)}, f32[256,768]{1,0:T(8,128)S(1)}, u32[]{:S(2)}) copy-start(f32[256,768]{1,0:T(8,128)S(1)} %get-tuple-element.216) | copy-start | bytes 2359300
  309.8 21.8 %copy-start.43 = (f32[256,768]{1,0:T(8,128)}, f32[256,768]{1,0:T(8,128)S(1)}, u32[]{:S(2)}) copy-start(f32[256,768]{1,0:T(8,128)S(1)} %get-tuple-element.218) | copy-start | bytes 2359300
  358.4 56.3 %slice-start.12 = ((s8[6291456]{0:T(1024)(128)(4,1)}), s8[4194304]{0:T(1024)(128)(4,1)S(1)}, s32[]{:S(2)}) async-start(s8[6291456]{0:T(1024)(128)(4,1)} %bitcast.240), calls=%async_computation.20 | async-start | bytes 8388608
  427.2 8.2 %copy-start.44 = (f32[256,768]{1,0:T(8,128)S(1)}, f32[256,768]{1,0:T(8,128)}, u32[]{:S(2)}) copy-start(f32[256,768]{1,0:T(8,128)} %copy-done.43) | copy-start | bytes 2359300
  455.5 22.5 %all-to-all-start.2 = ((bf16[4,2,128,192]{2,3,1,0:T(8,128)(2,1)}), bf16[4,2,128,192]{2,3,1,0:T(8,128)(2,1)S(1)}, u32[]{:S(2)}, u32[]{:S(2)}) async-start(bf16[4,2,128,192]{2,3,1,0:T(8,128)(2,1)} %copy.100), calls=%async_computation.2 | async-start | bytes 786432 | tf_op jit(solution)/shard_map/all_to_all | solution.py:1144
  474.9 9.5 %copy-start.15 = (bf16[1024,640]{1,0:T(8,128)(2,1)S(1)}, bf16[1024,640]{1,0:T(8,128)(2,1)}, u32[]{:S(2)}) copy-start(bf16[1024,640]{1,0:T(8,128)(2,1)} %copy-done.14) | copy-start | bytes 3932164
  478.8 32.5 %all-to-all-start.3 = ((bf16[4,2,256,192]{2,3,1,0:T(8,128)(2,1)}), bf16[4,2,256,192]{2,3,1,0:T(8,128)(2,1)}, u32[]{:S(2)}, u32[]{:S(2)}) async-start(bf16[4,2,256,192]{2,3,1,0:T(8,128)(2,1)} %copy.105), calls=%async_computation.3 | async-start | bytes 1572864 | tf_op jit(solution)/shard_map/all_to_all | solution.py:1144
  507.3 52.1 %collective-permute-start = (bf16[4,2,128,384]{3,2,1,0:T(8,128)(2,1)}, bf16[4,2,128,384]{3,2,1,0:T(8,128)(2,1)}, u32[]{:S(2)}, u32[]{:S(2)}) collective-permute-start(bf16[4,2,128,384]{3,2,1,0:T(8,128)(2,1)} %get-tuple-element.139), channel_id=1, source_target_pairs={{8,0},{12,4},{16,8},{20,12},{24,16},{28,20},{9,1},{13,5},{17,9},{2... | collective-permute-start | bytes 2359304 | tf_op jit(solution)/shard_map/ppermute | solution.py:1154
  508.7 50.7 %collective-permute-start.1 = (bf16[4,2,128,384]{3,2,1,0:T(8,128)(2,1)S(1)}, bf16[4,2,128,384]{3,2,1,0:T(8,128)(2,1)}, u32[]{:S(2)}, u32[]{:S(2)}) collective-permute-start(bf16[4,2,128,384]{3,2,1,0:T(8,128)(2,1)S(1)} %get-tuple-element.140), channel_id=1, source_target_pairs={{4,0},{8,4},{12,8},{16,12},{20,16},{24,20},{28,24},{5,1},{9,5},{13... | collective-permute-start | bytes 2359304 | tf_op jit(solution)/shard_map/ppermute | solution.py:1154
  511.3 53.0 %copy-start.30 = (bf16[4,2,128,256]{3,2,1,0:T(8,128)(2,1)}, bf16[4,2,128,256]{3,2,1,0:T(8,128)(2,1)S(1)}, u32[]{:S(2)}) copy-start(bf16[4,2,128,256]{3,2,1,0:T(8,128)(2,1)S(1)} %slice.133) | copy-start | bytes 1572868
  545.9 13.4 %copy-start.45 = (f32[4,2,128,640]{3,2,1,0:T(8,128)S(1)}, f32[4,2,128,640]{3,2,1,0:T(8,128)}, u32[]{:S(2)}) copy-start(f32[4,2,128,640]{3,2,1,0:T(8,128)} %get-tuple-element.144) | copy-start | bytes 7864324
  (89 other events, 373.1 us)
Sparse Core Ops, SparseCore 0:
  108.1 139.0 all-gather.2
  250.2 62.1 all-gather.4
  447.7 221.2 reduce-scatter.1
